TPU v7x, 256 devices: a whole 4x4x8 slice. The times are simulated.
256 devices in a mesh: table: 16 (over z_lo, x, core), batch: 16 (over y, z_hi).
Axes of the slice: x: 4, y: 4, z: 8 (z_hi: 4, z_lo: 2; z = z_hi * 2 + z_lo), core: 2. Of those that a mesh axis runs over, the one named last changes fastest.
Arguments:
- emb_table: bfloat16 [65536, 256], P('table'), may hold values from -2 to 2
- feature_ids: int32 [512, 1024, 8], P('batch', 'table'), may hold values from 0 to 4095
- projection: bfloat16 [1024, 256], P('table'), may hold values from -0.1875 to 0.1875
- norm_gain: float32 [256], replicated, may hold values from 0.1 to 1.9
- gate_weight: bfloat16 [256, 512], replicated, may hold values from -0.375 to 0.375
- up_weight: bfloat16 [256, 512], replicated, may hold values from -0.375 to 0.375
- down_weight: bfloat16 [512, 256], replicated, may hold values from -0.25 to 0.25
- out_grad: bfloat16 [512, 1024, 256], P(('batch', 'table')), may hold values from -24 to 24
Outputs:
- block_out: bfloat16 [512, 1024, 256], P(('batch', 'table'))
- table_grad: float32 [65536, 256], P(('table', 'batch'))
- projection_grad: float32 [1024, 256], P('table')
- gain_grad: float32 [256], replicated
- gate_grad: float32 [256, 512], replicated
- up_grad: float32 [256, 512], replicated
- down_grad: float32 [512, 256], replicated
Inputs may be any that keep to these rules, and one draw needn't show every extreme that they name: `feature_ids`: an id names a row of the table shard of the device that holds the feature's table.
All inputs are finite; a program needn't handle non-finite values.
Results may differ from a plain program's by a relative error of at most 0.035.
Values may be sent and summed in bfloat16 or wider, within the bound.
No kernel may reach another device: no remote copies, remote signals or barrier semaphores. Data moves between devices by JAX's collectives and lax.ppermute only.
A program may use at most 128 MiB of HBM per device.

v0:
```python
import jax
import jax.numpy as jnp
from jax import lax
from jax.experimental import pallas as pl
from jax.sharding import PartitionSpec as P

epsilon = 1e-06
BF = jnp.bfloat16
F32 = jnp.float32
STEPS = {"y": 4, "z": 1}


def contract(left, right, left_dim, right_dim):
    return lax.dot_general(
        left, right, (((left_dim,), (right_dim,)), ((), ())), preferred_element_type=F32
    )


def lookup_kernel(high_ref, low_ref, table_ref, counts_ref, embeds_ref):
    groups = high_ref.shape[0]
    slot = lax.broadcasted_iota(jnp.int32, (256, 128), 0)

    def step(g, carry):
        left = jnp.where(slot == high_ref[pl.ds(g, 1), :], 1.0, 0.0).astype(BF)
        right = jnp.where(slot == low_ref[pl.ds(g, 1), :], 1.0, 0.0).astype(BF)
        both = contract(left, right, 1, 1).astype(BF)
        for h in range(16):
            counts_ref[pl.ds(pl.multiple_of(g * 16, 16), 16), h * 256 : (h + 1) * 256] = both[
                h * 16 : (h + 1) * 16
            ]
        return carry

    lax.fori_loop(0, groups, step, 0, unroll=2)
    embeds_ref[...] = jnp.dot(
        counts_ref[...], table_ref[...], preferred_element_type=F32
    ).astype(BF)


def lookup(emb_table, feature_ids):
    samples, feats, pool = feature_ids.shape
    rows = samples * feats
    lanes = (
        feature_ids.reshape(samples, feats // 16, 16, pool)
        .transpose(0, 1, 3, 2)
        .reshape(rows // 16, 128)
    )
    high = (lanes // 256) * 16 + lax.broadcasted_iota(jnp.int32, lanes.shape, 1) % 16
    low = lanes % 256
    steps = 4
    return pl.pallas_call(
        lookup_kernel,
        grid=(steps,),
        in_specs=[
            pl.BlockSpec((rows // 16 // steps, 128), lambda i: (i, 0)),
            pl.BlockSpec((rows // 16 // steps, 128), lambda i: (i, 0)),
            pl.BlockSpec(emb_table.shape, lambda i: (0, 0)),
        ],
        out_specs=[
            pl.BlockSpec((rows // steps, emb_table.shape[0]), lambda i: (i, 0)),
            pl.BlockSpec((rows // steps, emb_table.shape[1]), lambda i: (i, 0)),
        ],
        out_shape=[
            jax.ShapeDtypeStruct((rows, emb_table.shape[0]), BF),
            jax.ShapeDtypeStruct((rows, emb_table.shape[1]), BF),
        ],
        cost_estimate=pl.CostEstimate(
            flops=4 * rows * emb_table.shape[0] * emb_table.shape[1],
            bytes_accessed=2 * rows * emb_table.shape[0] + 4 * emb_table.size,
            transcendentals=0,
        ),
        name="lookup",
    )(high, low, emb_table)


def exchange(values, axis):
    return lax.all_to_all(values, axis, 0, 0)


def place(part):
    batch = lax.axis_index("batch")
    return batch // 4 if part == "y" else batch % 4


def swap(values, part, offset):
    pairs = [(b, b ^ (STEPS[part] * offset)) for b in range(16)]
    return lax.ppermute(values, "batch", pairs)


def sum_scattered(values, part):
    mine = place(part)
    take = lambda i: lax.dynamic_index_in_dim(values, i, 0, keepdims=False)
    came = [swap(take(mine ^ k), part, k) for k in (1, 2, 3)]
    return sum((c.astype(F32) for c in came), take(mine).astype(F32))


def sum_all(values, part):
    came = [swap(values, part, k) for k in (1, 2, 3)]
    return sum((c.astype(F32) for c in came), values.astype(F32)).astype(BF)


def gathered(values, axis, size):
    return exchange(jnp.broadcast_to(values[None], (size,) + values.shape), axis)


def mlp_forward(interact, norm_gain, gate_weight, up_weight, down_weight):
    mean_sq = jnp.mean(interact * interact, axis=-1, keepdims=True)
    inv_rms = lax.rsqrt(mean_sq + epsilon)
    normed = interact * inv_rms
    scaled = (normed * norm_gain).astype(BF)
    gate_pre = jnp.dot(scaled, gate_weight, preferred_element_type=F32)
    up_pre = jnp.dot(scaled, up_weight, preferred_element_type=F32)
    hidden = (jax.nn.silu(gate_pre) * up_pre).astype(BF)
    result = jnp.dot(hidden, down_weight, preferred_element_type=F32).astype(BF)
    return (result, (inv_rms, normed, scaled, gate_pre, up_pre, hidden))


def mlp_backward(stored, grad_rows, norm_gain, gate_weight, up_weight, down_weight):
    inv_rms, normed, scaled, gate_pre, up_pre, hidden = stored
    hidden_grad = contract(grad_rows, down_weight, 1, 1)
    down_part = contract(hidden, grad_rows, 0, 0)
    sigmoid_gate = jax.nn.sigmoid(gate_pre)
    up_pre_grad = (hidden_grad * jax.nn.silu(gate_pre)).astype(BF)
    gate_pre_grad = (
        hidden_grad * up_pre * sigmoid_gate * (1.0 + gate_pre * (1.0 - sigmoid_gate))
    ).astype(BF)
    gate_part = contract(scaled, gate_pre_grad, 0, 0)
    up_part = contract(scaled, up_pre_grad, 0, 0)
    scaled_grad = contract(gate_pre_grad, gate_weight, 1, 1) + contract(
        up_pre_grad, up_weight, 1, 1
    )
    gain_part = jnp.sum(scaled_grad * normed, axis=0)
    inner_term = scaled_grad * norm_gain
    interact_grad = inv_rms * (
        inner_term - normed * jnp.mean(inner_term * normed, axis=-1, keepdims=True)
    )
    return (interact_grad.astype(BF), gate_part, up_part, down_part, gain_part)


def per_device(
    emb_table, feature_ids, projection, norm_gain, gate_weight, up_weight, down_weight, out_grad
):
    samples, feats, _ = feature_ids.shape
    shards = 16
    own = samples // shards
    width = emb_table.shape[1]
    rank = projection.shape[1]
    all_feats = shards * feats
    proj = gathered(projection, "table", shards).reshape(all_feats, rank)
    counts, embeds = lookup(emb_table, feature_ids)
    embeds, proj = lax.optimization_barrier((embeds, proj))
    x = (
        exchange(embeds.reshape(shards, own, feats, width), "table")
        .transpose(1, 0, 2, 3)
        .reshape(own, all_feats, width)
    )
    inter_map = jnp.einsum("sfd,fk->sdk", x, proj, preferred_element_type=F32).astype(BF)
    interact = jnp.einsum("sfd,sdk->sfk", x, inter_map, preferred_element_type=F32)
    result, stored = mlp_forward(
        interact.reshape(-1, rank), norm_gain, gate_weight, up_weight, down_weight
    )
    block_out = result.reshape(own, all_feats, width)
    interact_grad, gate_part, up_part, down_part, gain_part = mlp_backward(
        stored, out_grad.reshape(-1, width), norm_gain, gate_weight, up_weight, down_weight
    )
    interact_grad = interact_grad.reshape(own, all_feats, rank)
    inter_grad = jnp.einsum("sfd,sfk->sdk", x, interact_grad, preferred_element_type=F32).astype(
        BF
    )
    embed_grad = (
        jnp.einsum("sfk,sdk->sfd", interact_grad, inter_map, preferred_element_type=F32)
        + jnp.einsum("fk,sdk->sfd", proj, inter_grad, preferred_element_type=F32)
    ).astype(BF)
    back = exchange(
        embed_grad.reshape(own, shards, feats, width).transpose(1, 0, 2, 3), "table"
    ).reshape(-1, width)

    proj_part = jnp.einsum("sfd,sdk->fk", x, inter_grad, preferred_element_type=F32)
    hidden_width = gate_part.shape[1]

    def halves(part):
        return (
            part.astype(BF)
            .reshape(shards, rank // shards, 2, hidden_width // 2)
            .transpose(0, 2, 1, 3)
            .reshape(shards, -1, width)
        )

    gain_rows = jnp.pad(gain_part.astype(BF)[None], ((0, 15), (0, 0)))
    parts = jnp.concatenate(
        [
            halves(gate_part),
            halves(up_part),
            down_part.astype(BF).reshape(shards, -1, width),
            proj_part.astype(BF).reshape(shards, -1, width),
            jnp.broadcast_to(gain_rows[None], (shards, 16, width)),
        ],
        axis=1,
    )
    parts, back = lax.optimization_barrier((parts, back))
    parts = exchange(parts, "table")
    parts = jnp.sum(parts.astype(F32), axis=0).astype(BF)
    parts = sum_all(sum_all(parts, "y"), "z")
    projection_grad = parts[96:160].astype(F32)
    gain_grad = parts[160].astype(F32)
    weights = gathered(parts[:96], "table", shards).astype(F32)

    def joined(piece):
        return (
            piece.reshape(shards, 2, rank // shards, hidden_width // 2)
            .transpose(0, 2, 1, 3)
            .reshape(rank, hidden_width)
        )

    gate_grad = joined(weights[:, :32])
    up_grad = joined(weights[:, 32:64])
    down_grad = weights[:, 64:96].reshape(hidden_width, width)

    table_term = contract(counts, back, 0, 0).astype(BF)
    here = table_term.shape[0] // 16
    table_term = sum_scattered(table_term.reshape(4, 4 * here, width), "y").astype(BF)
    table_grad = sum_scattered(table_term.reshape(4, here, width), "z")
    return (block_out, table_grad, projection_grad, gain_grad, gate_grad, up_grad, down_grad)


def solution(mesh):
    return jax.shard_map(
        per_device,
        mesh=mesh,
        in_specs=(
            P("table", None),
            P("batch", "table", None),
            P("table", None),
            P(),
            P(),
            P(),
            P(),
            P(("batch", "table"), None, None),
        ),
        out_specs=(
            P(("batch", "table"), None, None),
            P(("table", "batch"), None),
            P("table", None),
            P(),
            P(),
            P(),
            P(),
        ),
        check_vma=False,
    )
```

profile of v0, /device:TPU:1, one launch (start us, length us, event | category | flops | bytes accessed | tf_op | source)
XLA Modules:
  0.0 184.8 jit_solution(10440628463072770985)
XLA Ops:
  0.6 1.7 broadcast_in_dim.6
  2.3 7.2 %all-to-all-start = ((bf16[16,64,256]{2,1,0:T(8,128)(2,1)}), bf16[16,64,256]{2,1,0:T(8,128)(2,1)S(1)}, u32[]{:S(2)}, u32[]{:S(2)}) async-start(bf16[16,64,256]{2,1,0:T(8,128)(2,1)} %broadcast_in_dim.6), calls=%async_computation | async-start | bytes 1048576 | tf_op jit(solution)/shard_map/all_to_all | solution.py:76
  12.0 23.2 %lookup.1 = (bf16[2048,4096]{1,0:T(8,128)(2,1)}, bf16[2048,256]{1,0:T(8,128)(2,1)}) custom-call(s32[128,128]{1,0:T(8,128)} %get-tuple-element.34.high_ref, s32[128,128]{1,0:T(8,128)} %get-tuple-element.33.low_ref, bf16[4096,256]{1,0:T(8,128)(2,1)} %table_ref.1), custom_call_target="tpu_custom_call" | custom-call | flops 8589934592 | bytes 20971520 | tf_op jit(solution)/shard_map/lookup/pallas_call | solution.py:50
  35.2 21.0 %all_to_all.25 = bf16[16,2,64,256]{3,2,1,0:T(8,128)(2,1)S(1)} all-to-all(bf16[16,2,64,256]{3,2,1,0:T(8,128)(2,1)} %bitcast.138), channel_id=1, replica_groups=mesh['table'=16,'batch'=16] {'table'}, dimensions={0} | all-to-all | bytes 2097152 | tf_op jit(solution)/shard_map/all_to_all | solution.py:76
  60.2 3.7 %multiply_convert_fusion = (bf16[2048,512]{1,0:T(8,128)(2,1)S(1)}, bf16[2048,512]{1,0:T(8,128)(2,1)S(1)}, bf16[2048,512]{1,0:T(8,128)(2,1)}) fusion(f32[2048,512]{1,0:T(8,128)S(1)} %fusion.15, f32[2048,512]{1,0:T(8,128)S(1)} %fusion.16, bf16[2048,256]{1,0:T(8,128)(2,1)S(1)} %bitcast.116, bf16[512,256]{1,0:T(8,128)(2,1)S(1)} %copy-done.9), kind=kOutput, calls=%fused_computation.1 | convolution fusion | flops 552599552 | bytes 15990784 | tf_op jit(solution)/shard_map/dot_general | solution.py:14
  70.6 5.3 %all-to-all-start.2 = ((bf16[16,2,64,256]{3,2,1,0:T(8,128)(2,1)}), bf16[16,2,64,256]{3,2,1,0:T(8,128)(2,1)}, u32[]{:S(2)}, u32[]{:S(2)}) async-start(bf16[16,2,64,256]{3,2,1,0:T(8,128)(2,1)} %bitcast.124), calls=%async_computation.2 | async-start | bytes 2097152 | tf_op jit(solution)/shard_map/all_to_all | solution.py:76
  75.9 3.0 %convolution_convert_fusion.4 = bf16[256,512]{1,0:T(8,128)(2,1)} fusion(bf16[2048,256]{1,0:T(8,128)(2,1)S(1)} %multiply_convert_fusion.4, bf16[2048,512]{1,0:T(8,128)(2,1)} %copy-done.2), kind=kOutput, calls=%fused_computation.20 | convolution fusion | flops 537001984 | bytes 3407872 | tf_op jit(solution)/shard_map/dot_general | solution.py:14
  79.0 1.7 reshape.135
  82.4 3.0 %convolution_convert_fusion.5 = bf16[256,512]{1,0:T(8,128)(2,1)} fusion(bf16[2048,256]{1,0:T(8,128)(2,1)S(1)} %multiply_convert_fusion.4, bf16[2048,512]{1,0:T(8,128)(2,1)} %copy-done.1), kind=kOutput, calls=%fused_computation.21 | convolution fusion | flops 537001984 | bytes 3407872 | tf_op jit(solution)/shard_map/dot_general | solution.py:14
  88.9 2.3 %convolution_convert_fusion.3 = bf16[512,256]{1,0:T(8,128)(2,1)S(1)} fusion(bf16[2048,512]{1,0:T(8,128)(2,1)} %get-tuple-element.23, bf16[2048,256]{1,0:T(8,128)(2,1)S(1)} %bitcast.117), kind=kOutput, calls=%fused_computation.19 | convolution fusion | flops 537001984 | bytes 3407872 | tf_op jit(solution)/shard_map/dot_general | solution.py:14
  93.9 5.8 %all-to-all-start.3 = ((bf16[16,176,256]{2,1,0:T(8,128)(2,1)}), bf16[16,176,256]{2,1,0:T(8,128)(2,1)S(1)}, u32[]{:S(2)}, u32[]{:S(2)}) async-start(bf16[16,176,256]{2,1,0:T(8,128)(2,1)} %broadcast_dynamic-update-slice_fusion), calls=%async_computation.3 | async-start | bytes 2883584 | tf_op jit(solution)/shard_map/all_to_all | solution.py:76
  99.7 12.3 %convolution_convert_fusion = bf16[4096,256]{1,0:T(8,128)(2,1)} fusion(bf16[2048,4096]{1,0:T(8,128)(2,1)} %get-tuple-element.16, bf16[2048,256]{1,0:T(8,128)(2,1)} %bitcast.22), kind=kOutput, calls=%fused_computation | convolution fusion | flops 4296015872 | bytes 19922944 | tf_op jit(solution)/shard_map/dot_general | solution.py:14
  112.0 7.6 %all-to-all-done.3 = bf16[16,176,256]{2,1,0:T(8,128)(2,1)S(1)} async-done(((bf16[16,176,256]{2,1,0:T(8,128)(2,1)}), bf16[16,176,256]{2,1,0:T(8,128)(2,1)S(1)}, u32[]{:S(2)}, u32[]{:S(2)}) %all-to-all-start.3) | async-done | bytes 1441824 | tf_op jit(solution)/shard_map/all_to_all | solution.py:76
  121.2 2.6 %collective-permute-start.7 = (bf16[176,256]{1,0:T(8,128)(2,1)S(1)}, bf16[176,256]{1,0:T(8,128)(2,1)S(1)}, u32[]{:S(2)}, u32[]{:S(2)}) collective-permute-start(bf16[176,256]{1,0:T(8,128)(2,1)S(1)} %reduce_sum.42), channel_id=1, source_target_pairs={{0,8},{1,9},{2,10},{3,11},{4,12},{5,13},{6,14},{7,15},{8,0},{9,1},... | collective-permute-start | bytes 270344 | tf_op jit(solution)/shard_map/ppermute | solution.py:86
  125.4 3.8 %collective-permute-start.1 = (bf16[1024,256]{1,0:T(8,128)(2,1)S(1)}, bf16[1024,256]{1,0:T(8,128)(2,1)}, u32[]{:S(2)}, u32[]{:S(2)}) collective-permute-start(bf16[1024,256]{1,0:T(8,128)(2,1)S(1)} %get-tuple-element.26), channel_id=1, source_target_pairs={{0,8},{1,9},{2,10},{3,11},{4,12},{5,13},{6,14},{7,15},{8,0},{9,1},... | collective-permute-start | bytes 1572872 | tf_op jit(solution)/shard_map/ppermute | solution.py:86
  129.5 6.1 %collective-permute-start.10 = (bf16[176,256]{1,0:T(8,128)(2,1)S(1)}, bf16[176,256]{1,0:T(8,128)(2,1)S(1)}, u32[]{:S(2)}, u32[]{:S(2)}) collective-permute-start(bf16[176,256]{1,0:T(8,128)(2,1)S(1)} %add_convert_fusion.1), channel_id=1, source_target_pairs={{0,2},{1,3},{2,0},{3,1},{4,6},{5,7},{6,4},{7,5},{8,10},{9,11},{10,... | collective-permute-start | bytes 270344 | tf_op jit(solution)/shard_map/ppermute | solution.py:86
  135.8 1.7 collective-permute-done.10
  137.6 3.1 %collective-permute-start.9 = (bf16[176,256]{1,0:T(8,128)(2,1)S(1)}, bf16[176,256]{1,0:T(8,128)(2,1)S(1)}, u32[]{:S(2)}, u32[]{:S(2)}) collective-permute-start(bf16[176,256]{1,0:T(8,128)(2,1)S(1)} %add_convert_fusion.1), channel_id=1, source_target_pairs={{0,1},{1,0},{2,3},{3,2},{4,5},{5,4},{6,7},{7,6},{8,9},{9,8},{10,11... | collective-permute-start | bytes 270344 | tf_op jit(solution)/shard_map/ppermute | solution.py:86
  140.6 2.9 %collective-permute-done.11 = bf16[176,256]{1,0:T(8,128)(2,1)S(1)} collective-permute-done((bf16[176,256]{1,0:T(8,128)(2,1)S(1)}, bf16[176,256]{1,0:T(8,128)(2,1)S(1)}, u32[]{:S(2)}, u32[]{:S(2)}) %collective-permute-start.11) | collective-permute-done | bytes 90144 | tf_op jit(solution)/shard_map/ppermute | solution.py:86
  145.0 8.6 %all-to-all-start.4 = ((bf16[16,96,256]{2,1,0:T(8,128)(2,1)}), bf16[16,96,256]{2,1,0:T(8,128)(2,1)S(1)}, u32[]{:S(2)}, u32[]{:S(2)}) async-start(bf16[16,96,256]{2,1,0:T(8,128)(2,1)} %broadcast_in_dim.8), calls=%async_computation.4 | async-start | bytes 1572864 | tf_op jit(solution)/shard_map/all_to_all | solution.py:76
  153.7 1.9 %fusion.5 = bf16[1024,256]{1,0:T(8,128)(2,1)S(1)} fusion(bf16[1024,256]{1,0:T(8,128)(2,1)} %collective-permute-done.2, bf16[1024,256]{1,0:T(8,128)(2,1)} %collective-permute-done.1, bf16[1024,256]{1,0:T(8,128)(2,1)} %collective-permute-done, bf16[4,1024,256]{2,1,0:T(8,128)(2,1)} %bitcast.130, s32[]{:T(128)S(6)} %select_n.56), kind=kLoop, calls=%fused_computation.26 | loop fusion | flops 2097152 | bytes 2621444 | tf_op jit(solution)/shard_map/convert_element_type | solution.py:220
  155.7 1.8 collective-permute-start.3
  157.5 5.0 %collective-permute-start.4 = (bf16[256,256]{1,0:T(8,128)(2,1)S(1)}, bf16[256,256]{1,0:T(8,128)(2,1)S(1)}, u32[]{:S(2)}, u32[]{:S(2)}) collective-permute-start(bf16[256,256]{1,0:T(8,128)(2,1)S(1)} %get-tuple-element.32), channel_id=1, source_target_pairs={{0,2},{1,3},{2,0},{3,1},{4,6},{5,7},{6,4},{7,5},{8,10},{9,11},{10,... | collective-permute-start | bytes 393224 | tf_op jit(solution)/shard_map/ppermute | solution.py:86
  165.5 13.9 %collective-permute-done.4 = bf16[256,256]{1,0:T(8,128)(2,1)S(1)} collective-permute-done((bf16[256,256]{1,0:T(8,128)(2,1)S(1)}, bf16[256,256]{1,0:T(8,128)(2,1)S(1)}, u32[]{:S(2)}, u32[]{:S(2)}) %collective-permute-start.4) | collective-permute-done | bytes 131104 | tf_op jit(solution)/shard_map/ppermute | solution.py:86
  (89 shorter events, 34.4 us)
Async XLA Ops:
  0.6 59.3 %copy-start = (bf16[2,1024,256]{2,1,0:T(8,128)(2,1)S(1)}, bf16[2,1024,256]{2,1,0:T(8,128)(2,1)}, u32[]{:S(2)}) copy-start(bf16[2,1024,256]{2,1,0:T(8,128)(2,1)} %param.15) | copy-start | bytes 3145732
  2.3 32.8 %all-to-all-start = ((bf16[16,64,256]{2,1,0:T(8,128)(2,1)}), bf16[16,64,256]{2,1,0:T(8,128)(2,1)S(1)}, u32[]{:S(2)}, u32[]{:S(2)}) async-start(bf16[16,64,256]{2,1,0:T(8,128)(2,1)} %broadcast_in_dim.6), calls=%async_computation | async-start | bytes 1048576 | tf_op jit(solution)/shard_map/all_to_all | solution.py:76
  35.2 21.1 %copy-start.3 = (bf16[16,64,256]{2,1,0:T(8,128)(2,1)}, bf16[16,64,256]{2,1,0:T(8,128)(2,1)S(1)}, u32[]{:S(2)}) copy-start(bf16[16,64,256]{2,1,0:T(8,128)(2,1)S(1)} %all-to-all-done) | copy-start | bytes 1572868
  57.3 1.0 copy-start.7
  63.9 1.3 copy-start.1
  63.9 2.0 %copy-start.2 = (bf16[2048,512]{1,0:T(8,128)(2,1)}, bf16[2048,512]{1,0:T(8,128)(2,1)S(1)}, u32[]{:S(2)}) copy-start(bf16[2048,512]{1,0:T(8,128)(2,1)S(1)} %get-tuple-element.21) | copy-start | bytes 6291460
  68.0 1.0 copy-start.4
  70.6 23.3 %all-to-all-start.2 = ((bf16[16,2,64,256]{3,2,1,0:T(8,128)(2,1)}), bf16[16,2,64,256]{3,2,1,0:T(8,128)(2,1)}, u32[]{:S(2)}, u32[]{:S(2)}) async-start(bf16[16,2,64,256]{3,2,1,0:T(8,128)(2,1)} %bitcast.124), calls=%async_computation.2 | async-start | bytes 2097152 | tf_op jit(solution)/shard_map/all_to_all | solution.py:76
  93.9 25.7 %all-to-all-start.3 = ((bf16[16,176,256]{2,1,0:T(8,128)(2,1)}), bf16[16,176,256]{2,1,0:T(8,128)(2,1)S(1)}, u32[]{:S(2)}, u32[]{:S(2)}) async-start(bf16[16,176,256]{2,1,0:T(8,128)(2,1)} %broadcast_dynamic-update-slice_fusion), calls=%async_computation.3 | async-start | bytes 2883584 | tf_op jit(solution)/shard_map/all_to_all | solution.py:76
  119.8 9.4 %collective-permute-start.6 = (bf16[176,256]{1,0:T(8,128)(2,1)S(1)}, bf16[176,256]{1,0:T(8,128)(2,1)S(1)}, u32[]{:S(2)}, u32[]{:S(2)}) collective-permute-start(bf16[176,256]{1,0:T(8,128)(2,1)S(1)} %reduce_sum.42), channel_id=1, source_target_pairs={{0,4},{1,5},{2,6},{3,7},{4,0},{5,1},{6,2},{7,3},{8,12},{9,13},{10,... | collective-permute-start | bytes 270344 | tf_op jit(solution)/shard_map/ppermute | solution.py:86
  121.2 8.0 %collective-permute-start.7 = (bf16[176,256]{1,0:T(8,128)(2,1)S(1)}, bf16[176,256]{1,0:T(8,128)(2,1)S(1)}, u32[]{:S(2)}, u32[]{:S(2)}) collective-permute-start(bf16[176,256]{1,0:T(8,128)(2,1)S(1)} %reduce_sum.42), channel_id=1, source_target_pairs={{0,8},{1,9},{2,10},{3,11},{4,12},{5,13},{6,14},{7,15},{8,0},{9,1},... | collective-permute-start | bytes 270344 | tf_op jit(solution)/shard_map/ppermute | solution.py:86
  123.8 5.6 %collective-permute-start.8 = (bf16[176,256]{1,0:T(8,128)(2,1)S(1)}, bf16[176,256]{1,0:T(8,128)(2,1)S(1)}, u32[]{:S(2)}, u32[]{:S(2)}) collective-permute-start(bf16[176,256]{1,0:T(8,128)(2,1)S(1)} %reduce_sum.42), channel_id=1, source_target_pairs={{0,12},{1,13},{2,14},{3,15},{4,8},{5,9},{6,10},{7,11},{8,4},{9,5},... | collective-permute-start | bytes 270344 | tf_op jit(solution)/shard_map/ppermute | solution.py:86
  125.3 28.3 %collective-permute-start = (bf16[1024,256]{1,0:T(8,128)(2,1)S(1)}, bf16[1024,256]{1,0:T(8,128)(2,1)}, u32[]{:S(2)}, u32[]{:S(2)}) collective-permute-start(bf16[1024,256]{1,0:T(8,128)(2,1)S(1)} %get-tuple-element.24), channel_id=1, source_target_pairs={{0,4},{1,5},{2,6},{3,7},{4,0},{5,1},{6,2},{7,3},{8,12},{9,13},{10,... | collective-permute-start | bytes 1572872 | tf_op jit(solution)/shard_map/ppermute | solution.py:86
  125.4 28.2 %collective-permute-start.1 = (bf16[1024,256]{1,0:T(8,128)(2,1)S(1)}, bf16[1024,256]{1,0:T(8,128)(2,1)}, u32[]{:S(2)}, u32[]{:S(2)}) collective-permute-start(bf16[1024,256]{1,0:T(8,128)(2,1)S(1)} %get-tuple-element.26), channel_id=1, source_target_pairs={{0,8},{1,9},{2,10},{3,11},{4,12},{5,13},{6,14},{7,15},{8,0},{9,1},... | collective-permute-start | bytes 1572872 | tf_op jit(solution)/shard_map/ppermute | solution.py:86
  129.3 24.4 %collective-permute-start.2 = (bf16[1024,256]{1,0:T(8,128)(2,1)S(1)}, bf16[1024,256]{1,0:T(8,128)(2,1)}, u32[]{:S(2)}, u32[]{:S(2)}) collective-permute-start(bf16[1024,256]{1,0:T(8,128)(2,1)S(1)} %get-tuple-element.25), channel_id=1, source_target_pairs={{0,12},{1,13},{2,14},{3,15},{4,8},{5,9},{6,10},{7,11},{8,4},{9,5},... | collective-permute-start | bytes 1572872 | tf_op jit(solution)/shard_map/ppermute | solution.py:86
  129.5 8.1 %collective-permute-start.10 = (bf16[176,256]{1,0:T(8,128)(2,1)S(1)}, bf16[176,256]{1,0:T(8,128)(2,1)S(1)}, u32[]{:S(2)}, u32[]{:S(2)}) collective-permute-start(bf16[176,256]{1,0:T(8,128)(2,1)S(1)} %add_convert_fusion.1), channel_id=1, source_target_pairs={{0,2},{1,3},{2,0},{3,1},{4,6},{5,7},{6,4},{7,5},{8,10},{9,11},{10,... | collective-permute-start | bytes 270344 | tf_op jit(solution)/shard_map/ppermute | solution.py:86
  135.6 8.0 %collective-permute-start.11 = (bf16[176,256]{1,0:T(8,128)(2,1)S(1)}, bf16[176,256]{1,0:T(8,128)(2,1)S(1)}, u32[]{:S(2)}, u32[]{:S(2)}) collective-permute-start(bf16[176,256]{1,0:T(8,128)(2,1)S(1)} %add_convert_fusion.1), channel_id=1, source_target_pairs={{0,3},{1,2},{2,1},{3,0},{4,7},{5,6},{6,5},{7,4},{8,11},{9,10},{10,... | collective-permute-start | bytes 270344 | tf_op jit(solution)/shard_map/ppermute | solution.py:86
  137.6 6.4 %collective-permute-start.9 = (bf16[176,256]{1,0:T(8,128)(2,1)S(1)}, bf16[176,256]{1,0:T(8,128)(2,1)S(1)}, u32[]{:S(2)}, u32[]{:S(2)}) collective-permute-start(bf16[176,256]{1,0:T(8,128)(2,1)S(1)} %add_convert_fusion.1), channel_id=1, source_target_pairs={{0,1},{1,0},{2,3},{3,2},{4,5},{5,4},{6,7},{7,6},{8,9},{9,8},{10,11... | collective-permute-start | bytes 270344 | tf_op jit(solution)/shard_map/ppermute | solution.py:86
  145.0 36.3 %all-to-all-start.4 = ((bf16[16,96,256]{2,1,0:T(8,128)(2,1)}), bf16[16,96,256]{2,1,0:T(8,128)(2,1)S(1)}, u32[]{:S(2)}, u32[]{:S(2)}) async-start(bf16[16,96,256]{2,1,0:T(8,128)(2,1)} %broadcast_in_dim.8), calls=%async_computation.4 | async-start | bytes 1572864 | tf_op jit(solution)/shard_map/all_to_all | solution.py:76
  153.6 8.8 %copy-start.5 = (bf16[2048,512]{1,0:T(8,128)(2,1)S(1)}, bf16[2048,512]{1,0:T(8,128)(2,1)}, u32[]{:S(2)}) copy-start(bf16[2048,512]{1,0:T(8,128)(2,1)} %get-tuple-element.23) | copy-start | bytes 6291460
  153.6 8.8 %copy-start.10 = (bf16[512,256]{1,0:T(8,128)(2,1)S(1)}, bf16[512,256]{1,0:T(8,128)(2,1)}, u32[]{:S(2)}) copy-start(bf16[512,256]{1,0:T(8,128)(2,1)} %param.14) | copy-start | bytes 786436
  155.7 9.8 %collective-permute-start.3 = (bf16[256,256]{1,0:T(8,128)(2,1)S(1)}, bf16[256,256]{1,0:T(8,128)(2,1)S(1)}, u32[]{:S(2)}, u32[]{:S(2)}) collective-permute-start(bf16[256,256]{1,0:T(8,128)(2,1)S(1)} %get-tuple-element.30), channel_id=1, source_target_pairs={{0,1},{1,0},{2,3},{3,2},{4,5},{5,4},{6,7},{7,6},{8,9},{9,8},{10,11... | collective-permute-start | bytes 393224 | tf_op jit(solution)/shard_map/ppermute | solution.py:86
  157.5 21.8 %collective-permute-start.4 = (bf16[256,256]{1,0:T(8,128)(2,1)S(1)}, bf16[256,256]{1,0:T(8,128)(2,1)S(1)}, u32[]{:S(2)}, u32[]{:S(2)}) collective-permute-start(bf16[256,256]{1,0:T(8,128)(2,1)S(1)} %get-tuple-element.32), channel_id=1, source_target_pairs={{0,2},{1,3},{2,0},{3,1},{4,6},{5,7},{6,4},{7,5},{8,10},{9,11},{10,... | collective-permute-start | bytes 393224 | tf_op jit(solution)/shard_map/ppermute | solution.py:86
  162.5 16.9 %collective-permute-start.5 = (bf16[256,256]{1,0:T(8,128)(2,1)S(1)}, bf16[256,256]{1,0:T(8,128)(2,1)S(1)}, u32[]{:S(2)}, u32[]{:S(2)}) collective-permute-start(bf16[256,256]{1,0:T(8,128)(2,1)S(1)} %get-tuple-element.31), channel_id=1, source_target_pairs={{0,3},{1,2},{2,1},{3,0},{4,7},{5,6},{6,5},{7,4},{8,11},{9,10},{10,... | collective-permute-start | bytes 393224 | tf_op jit(solution)/shard_map/ppermute | solution.py:86
  (3 other events, 2.6 us)
where the time goes:
time: 186 us; the launch traced here: 185 us
  starting transfers between devices  51.1 us (27%)
  matrix products  32.3 us (17%)
  waiting for transfers between devices  28 us (15%)
  Pallas kernels  23.2 us (12%)
  local copies, waits for them, and re-layouts  22 us (12%)
  blocking collectives  21 us (11%)
  other arithmetic  6.19 us (3%)
    all_to_all x4, starting transfers between devices, exchange(): return lax.all_to_all(values, axis, 0, 0)  26.9 us
    dot_general x7, matrix products, contract(): lax.dot_general(left, right, (((left_dim,), (right_dim,)), ((), ())), pre...  26.3 us
    ppermute x12, starting transfers between devices, swap(): return lax.ppermute(values, 'batch', pairs)  24.2 us
    pallas_call x1, Pallas kernels, lookup(): pl.pallas_call(lookup_kernel, grid=(steps,), in_specs=[pl.BlockSpec((rows...  23.2 us
    all_to_all x1, blocking collectives, exchange(): return lax.all_to_all(values, axis, 0, 0)  21 us
    ppermute x12, waiting for transfers between devices, swap(): return lax.ppermute(values, 'batch', pairs)  20.4 us
    unnamed x30, local copies, waits for them, and re-layouts  9.08 us
    all_to_all x4, waiting for transfers between devices, exchange(): return lax.all_to_all(values, axis, 0, 0)  7.62 us
  transfers between devices with their start and end apart: 16, of which 7 were waited for; matrix products, arithmetic and copies ran while one was open for 22% of the time, Pallas kernels for 13%

commit v1 on v0

--- a/solution.py
+++ b/solution.py
@@ -30,7 +30,7 @@
             ]
         return carry
 
-    lax.fori_loop(0, groups, step, 0, unroll=2)
+    lax.fori_loop(0, groups, step, 0, unroll=8)
     embeds_ref[...] = jnp.dot(
         counts_ref[...], table_ref[...], preferred_element_type=F32
     ).astype(BF)
@@ -199,10 +199,12 @@
     parts, back = lax.optimization_barrier((parts, back))
     parts = exchange(parts, "table")
     parts = jnp.sum(parts.astype(F32), axis=0).astype(BF)
-    parts = sum_all(sum_all(parts, "y"), "z")
+    parts = sum_all(parts, "z")
+    parts = sum_all(parts, "y")
     projection_grad = parts[96:160].astype(F32)
     gain_grad = parts[160].astype(F32)
-    weights = gathered(parts[:96], "table", shards).astype(F32)
+    weights = gathered(parts[:96], "table", shards)
+    weights = weights.astype(F32)
 
     def joined(piece):
         return (

time: 186 us -> 193 us (1.038)
  waiting for transfers between devices: 28 us -> 47.7 us
  Pallas kernels: 23.2 us -> 16.1 us
  starting transfers between devices: 51.1 us -> 46 us
    ppermute x12, waiting for transfers between devices: 20.4 us -> 40.1 us  [swap(): return lax.ppermute(values, 'batch', pairs)]
    pallas_call x1, Pallas kernels: 23.2 us -> 16.1 us  [lookup(): pl.pallas_call(lookup_kernel, grid=(steps,), in_specs=[pl.BlockSpec((rows...]
    ppermute x12, starting transfers between devices: 24.2 us -> 20.8 us  [swap(): return lax.ppermute(values, 'batch', pairs)]
  transfers between devices with their start and end apart: 16 -> 16, of which waited for: 7 -> 6; matrix products, arithmetic and copies ran while one was open for 22% -> 21% of each run, Pallas kernels for 13% -> 8%
where the time goes in v1:
time: 193 us; the launch traced here: 192 us
  waiting for transfers between devices  47.7 us (25%)
  starting transfers between devices  46 us (24%)
  matrix products  32.3 us (17%)
  local copies, waits for them, and re-layouts  22 us (11%)
  blocking collectives  21 us (11%)
  Pallas kernels  16.1 us (8%)
  other arithmetic  6.19 us (3%)
    ppermute x12, waiting for transfers between devices, swap(): return lax.ppermute(values, 'batch', pairs)  40.1 us
    dot_general x7, matrix products, contract(): lax.dot_general(left, right, (((left_dim,), (right_dim,)), ((), ())), pre...  26.3 us
    all_to_all x4, starting transfers between devices, exchange(): return lax.all_to_all(values, axis, 0, 0)  25.2 us
    all_to_all x1, blocking collectives, exchange(): return lax.all_to_all(values, axis, 0, 0)  21 us
    ppermute x12, starting transfers between devices, swap(): return lax.ppermute(values, 'batch', pairs)  20.8 us
    pallas_call x1, Pallas kernels, lookup(): pl.pallas_call(lookup_kernel, grid=(steps,), in_specs=[pl.BlockSpec((rows...  16.1 us
    unnamed x30, local copies, waits for them, and re-layouts  9.09 us
    all_to_all x4, waiting for transfers between devices, exchange(): return lax.all_to_all(values, axis, 0, 0)  7.62 us
  transfers between devices with their start and end apart: 16, of which 6 were waited for; matrix products, arithmetic and copies ran while one was open for 21% of the time, Pallas kernels for 8%

profile of v1, /device:TPU:1, one launch (start us, length us, event | category | flops | bytes accessed | tf_op | source)
XLA Modules:
  0.0 192.2 jit_solution(3924906765483424119)
XLA Ops:
  2.3 7.2 %all-to-all-start = ((bf16[16,64,256]{2,1,0:T(8,128)(2,1)}), bf16[16,64,256]{2,1,0:T(8,128)(2,1)S(1)}, u32[]{:S(2)}, u32[]{:S(2)}) async-start(bf16[16,64,256]{2,1,0:T(8,128)(2,1)} %broadcast_in_dim.6), calls=%async_computation | async-start | bytes 1048576 | tf_op jit(solution)/shard_map/all_to_all | solution.py:76
  12.0 16.1 %lookup.1 = (bf16[2048,4096]{1,0:T(8,128)(2,1)}, bf16[2048,256]{1,0:T(8,128)(2,1)}) custom-call(s32[128,128]{1,0:T(8,128)} %get-tuple-element.34.high_ref, s32[128,128]{1,0:T(8,128)} %get-tuple-element.33.low_ref, bf16[4096,256]{1,0:T(8,128)(2,1)} %table_ref.1), custom_call_target="tpu_custom_call" | custom-call | flops 8589934592 | bytes 20971520 | tf_op jit(solution)/shard_map/lookup/pallas_call | solution.py:50
  28.1 21.0 %all_to_all.25 = bf16[16,2,64,256]{3,2,1,0:T(8,128)(2,1)S(1)} all-to-all(bf16[16,2,64,256]{3,2,1,0:T(8,128)(2,1)} %bitcast.138), channel_id=1, replica_groups=mesh['table'=16,'batch'=16] {'table'}, dimensions={0} | all-to-all | bytes 2097152 | tf_op jit(solution)/shard_map/all_to_all | solution.py:76
  53.1 3.7 %multiply_convert_fusion = (bf16[2048,512]{1,0:T(8,128)(2,1)S(1)}, bf16[2048,512]{1,0:T(8,128)(2,1)S(1)}, bf16[2048,512]{1,0:T(8,128)(2,1)}) fusion(f32[2048,512]{1,0:T(8,128)S(1)} %fusion.15, f32[2048,512]{1,0:T(8,128)S(1)} %fusion.16, bf16[2048,256]{1,0:T(8,128)(2,1)S(1)} %bitcast.116, bf16[512,256]{1,0:T(8,128)(2,1)S(1)} %copy-done.9), kind=kOutput, calls=%fused_computation.1 | convolution fusion | flops 552599552 | bytes 15990784 | tf_op jit(solution)/shard_map/dot_general | solution.py:14
  63.5 5.3 %all-to-all-start.2 = ((bf16[16,2,64,256]{3,2,1,0:T(8,128)(2,1)}), bf16[16,2,64,256]{3,2,1,0:T(8,128)(2,1)}, u32[]{:S(2)}, u32[]{:S(2)}) async-start(bf16[16,2,64,256]{3,2,1,0:T(8,128)(2,1)} %bitcast.124), calls=%async_computation.2 | async-start | bytes 2097152 | tf_op jit(solution)/shard_map/all_to_all | solution.py:76
  68.9 3.0 %convolution_convert_fusion.4 = bf16[256,512]{1,0:T(8,128)(2,1)} fusion(bf16[2048,256]{1,0:T(8,128)(2,1)S(1)} %multiply_convert_fusion.4, bf16[2048,512]{1,0:T(8,128)(2,1)} %copy-done.2), kind=kOutput, calls=%fused_computation.20 | convolution fusion | flops 537001984 | bytes 3407872 | tf_op jit(solution)/shard_map/dot_general | solution.py:14
  71.9 1.7 reshape.135
  75.3 3.0 %convolution_convert_fusion.5 = bf16[256,512]{1,0:T(8,128)(2,1)} fusion(bf16[2048,256]{1,0:T(8,128)(2,1)S(1)} %multiply_convert_fusion.4, bf16[2048,512]{1,0:T(8,128)(2,1)} %copy-done.1), kind=kOutput, calls=%fused_computation.21 | convolution fusion | flops 537001984 | bytes 3407872 | tf_op jit(solution)/shard_map/dot_general | solution.py:14
  81.8 2.3 %convolution_convert_fusion.3 = bf16[512,256]{1,0:T(8,128)(2,1)S(1)} fusion(bf16[2048,512]{1,0:T(8,128)(2,1)} %get-tuple-element.23, bf16[2048,256]{1,0:T(8,128)(2,1)S(1)} %bitcast.117), kind=kOutput, calls=%fused_computation.19 | convolution fusion | flops 537001984 | bytes 3407872 | tf_op jit(solution)/shard_map/dot_general | solution.py:14
  86.8 5.8 %all-to-all-start.3 = ((bf16[16,176,256]{2,1,0:T(8,128)(2,1)}), bf16[16,176,256]{2,1,0:T(8,128)(2,1)S(1)}, u32[]{:S(2)}, u32[]{:S(2)}) async-start(bf16[16,176,256]{2,1,0:T(8,128)(2,1)} %broadcast_dynamic-update-slice_fusion), calls=%async_computation.3 | async-start | bytes 2883584 | tf_op jit(solution)/shard_map/all_to_all | solution.py:76
  92.6 12.3 %convolution_convert_fusion = bf16[4096,256]{1,0:T(8,128)(2,1)} fusion(bf16[2048,4096]{1,0:T(8,128)(2,1)} %get-tuple-element.16, bf16[2048,256]{1,0:T(8,128)(2,1)} %bitcast.22), kind=kOutput, calls=%fused_computation | convolution fusion | flops 4296015872 | bytes 19922944 | tf_op jit(solution)/shard_map/dot_general | solution.py:14
  105.0 7.6 %all-to-all-done.3 = bf16[16,176,256]{2,1,0:T(8,128)(2,1)S(1)} async-done(((bf16[16,176,256]{2,1,0:T(8,128)(2,1)}), bf16[16,176,256]{2,1,0:T(8,128)(2,1)S(1)}, u32[]{:S(2)}, u32[]{:S(2)}) %all-to-all-start.3) | async-done | bytes 1441824 | tf_op jit(solution)/shard_map/all_to_all | solution.py:76
  112.8 3.1 %collective-permute-start.6 = (bf16[176,256]{1,0:T(8,128)(2,1)S(1)}, bf16[176,256]{1,0:T(8,128)(2,1)S(1)}, u32[]{:S(2)}, u32[]{:S(2)}) collective-permute-start(bf16[176,256]{1,0:T(8,128)(2,1)S(1)} %reduce_sum.42), channel_id=1, source_target_pairs={{0,1},{1,0},{2,3},{3,2},{4,5},{5,4},{6,7},{7,6},{8,9},{9,8},{10,11... | collective-permute-start | bytes 270344 | tf_op jit(solution)/shard_map/ppermute | solution.py:86
  115.8 4.2 %collective-permute-start.7 = (bf16[176,256]{1,0:T(8,128)(2,1)S(1)}, bf16[176,256]{1,0:T(8,128)(2,1)S(1)}, u32[]{:S(2)}, u32[]{:S(2)}) collective-permute-start(bf16[176,256]{1,0:T(8,128)(2,1)S(1)} %reduce_sum.42), channel_id=1, source_target_pairs={{0,2},{1,3},{2,0},{3,1},{4,6},{5,7},{6,4},{7,5},{8,10},{9,11},{10,... | collective-permute-start | bytes 270344 | tf_op jit(solution)/shard_map/ppermute | solution.py:86
  122.9 2.6 %collective-permute-start.1 = (bf16[1024,256]{1,0:T(8,128)(2,1)S(1)}, bf16[1024,256]{1,0:T(8,128)(2,1)}, u32[]{:S(2)}, u32[]{:S(2)}) collective-permute-start(bf16[1024,256]{1,0:T(8,128)(2,1)S(1)} %get-tuple-element.26), channel_id=1, source_target_pairs={{0,8},{1,9},{2,10},{3,11},{4,12},{5,13},{6,14},{7,15},{8,0},{9,1},... | collective-permute-start | bytes 1572872 | tf_op jit(solution)/shard_map/ppermute | solution.py:86
  125.5 2.7 %collective-permute-done.8 = bf16[176,256]{1,0:T(8,128)(2,1)S(1)} collective-permute-done((bf16[176,256]{1,0:T(8,128)(2,1)S(1)}, bf16[176,256]{1,0:T(8,128)(2,1)S(1)}, u32[]{:S(2)}, u32[]{:S(2)}) %collective-permute-start.8) | collective-permute-done | bytes 90144 | tf_op jit(solution)/shard_map/ppermute | solution.py:86
  128.2 3.0 %collective-permute-start.10 = (bf16[176,256]{1,0:T(8,128)(2,1)S(1)}, bf16[176,256]{1,0:T(8,128)(2,1)S(1)}, u32[]{:S(2)}, u32[]{:S(2)}) collective-permute-start(bf16[176,256]{1,0:T(8,128)(2,1)S(1)} %add_convert_fusion.1), channel_id=1, source_target_pairs={{0,8},{1,9},{2,10},{3,11},{4,12},{5,13},{6,14},{7,15},{8,0},{9,1},... | collective-permute-start | bytes 270344 | tf_op jit(solution)/shard_map/ppermute | solution.py:86
  132.0 17.3 %collective-permute-done.10 = bf16[176,256]{1,0:T(8,128)(2,1)S(1)} collective-permute-done((bf16[176,256]{1,0:T(8,128)(2,1)S(1)}, bf16[176,256]{1,0:T(8,128)(2,1)S(1)}, u32[]{:S(2)}, u32[]{:S(2)}) %collective-permute-start.10) | collective-permute-done | bytes 90144 | tf_op jit(solution)/shard_map/ppermute | solution.py:86
  149.3 4.0 %collective-permute-done.11 = bf16[176,256]{1,0:T(8,128)(2,1)S(1)} collective-permute-done((bf16[176,256]{1,0:T(8,128)(2,1)S(1)}, bf16[176,256]{1,0:T(8,128)(2,1)S(1)}, u32[]{:S(2)}, u32[]{:S(2)}) %collective-permute-start.11) | collective-permute-done | bytes 90144 | tf_op jit(solution)/shard_map/ppermute | solution.py:86
  154.4 6.9 %all-to-all-start.4 = ((bf16[16,96,256]{2,1,0:T(8,128)(2,1)}), bf16[16,96,256]{2,1,0:T(8,128)(2,1)S(1)}, u32[]{:S(2)}, u32[]{:S(2)}) async-start(bf16[16,96,256]{2,1,0:T(8,128)(2,1)} %broadcast_in_dim.8), calls=%async_computation.4 | async-start | bytes 1572864 | tf_op jit(solution)/shard_map/all_to_all | solution.py:76
  161.3 1.9 %fusion.5 = bf16[1024,256]{1,0:T(8,128)(2,1)S(1)} fusion(bf16[1024,256]{1,0:T(8,128)(2,1)} %collective-permute-done.2, bf16[1024,256]{1,0:T(8,128)(2,1)} %collective-permute-done.1, bf16[1024,256]{1,0:T(8,128)(2,1)} %collective-permute-done, bf16[4,1024,256]{2,1,0:T(8,128)(2,1)} %bitcast.130, s32[]{:T(128)S(6)} %select_n.56), kind=kLoop, calls=%fused_computation.26 | loop fusion | flops 2097152 | bytes 2621444 | tf_op jit(solution)/shard_map/convert_element_type | solution.py:222
  164.8 4.2 %collective-permute-start.4 = (bf16[256,256]{1,0:T(8,128)(2,1)S(1)}, bf16[256,256]{1,0:T(8,128)(2,1)S(1)}, u32[]{:S(2)}, u32[]{:S(2)}) collective-permute-start(bf16[256,256]{1,0:T(8,128)(2,1)S(1)} %get-tuple-element.32), channel_id=1, source_target_pairs={{0,2},{1,3},{2,0},{3,1},{4,6},{5,7},{6,4},{7,5},{8,10},{9,11},{10,... | collective-permute-start | bytes 393224 | tf_op jit(solution)/shard_map/ppermute | solution.py:86
  170.7 2.4 %collective-permute-done.3 = bf16[256,256]{1,0:T(8,128)(2,1)S(1)} collective-permute-done((bf16[256,256]{1,0:T(8,128)(2,1)S(1)}, bf16[256,256]{1,0:T(8,128)(2,1)S(1)}, u32[]{:S(2)}, u32[]{:S(2)}) %collective-permute-start.3) | collective-permute-done | bytes 131104 | tf_op jit(solution)/shard_map/ppermute | solution.py:86
  173.1 13.7 %collective-permute-done.4 = bf16[256,256]{1,0:T(8,128)(2,1)S(1)} collective-permute-done((bf16[256,256]{1,0:T(8,128)(2,1)S(1)}, bf16[256,256]{1,0:T(8,128)(2,1)S(1)}, u32[]{:S(2)}, u32[]{:S(2)}) %collective-permute-start.4) | collective-permute-done | bytes 131104 | tf_op jit(solution)/shard_map/ppermute | solution.py:86
  (89 shorter events, 36.2 us)
Async XLA Ops:
  0.6 52.2 %copy-start = (bf16[2,1024,256]{2,1,0:T(8,128)(2,1)S(1)}, bf16[2,1024,256]{2,1,0:T(8,128)(2,1)}, u32[]{:S(2)}) copy-start(bf16[2,1024,256]{2,1,0:T(8,128)(2,1)} %param.15) | copy-start | bytes 3145732
  2.3 25.7 %all-to-all-start = ((bf16[16,64,256]{2,1,0:T(8,128)(2,1)}), bf16[16,64,256]{2,1,0:T(8,128)(2,1)S(1)}, u32[]{:S(2)}, u32[]{:S(2)}) async-start(bf16[16,64,256]{2,1,0:T(8,128)(2,1)} %broadcast_in_dim.6), calls=%async_computation | async-start | bytes 1048576 | tf_op jit(solution)/shard_map/all_to_all | solution.py:76
  28.1 21.1 %copy-start.3 = (bf16[16,64,256]{2,1,0:T(8,128)(2,1)}, bf16[16,64,256]{2,1,0:T(8,128)(2,1)S(1)}, u32[]{:S(2)}) copy-start(bf16[16,64,256]{2,1,0:T(8,128)(2,1)S(1)} %all-to-all-done) | copy-start | bytes 1572868
  50.3 1.0 copy-start.7
  56.8 1.3 copy-start.1
  56.8 2.0 %copy-start.2 = (bf16[2048,512]{1,0:T(8,128)(2,1)}, bf16[2048,512]{1,0:T(8,128)(2,1)S(1)}, u32[]{:S(2)}) copy-start(bf16[2048,512]{1,0:T(8,128)(2,1)S(1)} %get-tuple-element.21) | copy-start | bytes 6291460
  60.9 1.0 copy-start.4
  63.5 23.3 %all-to-all-start.2 = ((bf16[16,2,64,256]{3,2,1,0:T(8,128)(2,1)}), bf16[16,2,64,256]{3,2,1,0:T(8,128)(2,1)}, u32[]{:S(2)}, u32[]{:S(2)}) async-start(bf16[16,2,64,256]{3,2,1,0:T(8,128)(2,1)} %bitcast.124), calls=%async_computation.2 | async-start | bytes 2097152 | tf_op jit(solution)/shard_map/all_to_all | solution.py:76
  86.8 25.7 %all-to-all-start.3 = ((bf16[16,176,256]{2,1,0:T(8,128)(2,1)}), bf16[16,176,256]{2,1,0:T(8,128)(2,1)S(1)}, u32[]{:S(2)}, u32[]{:S(2)}) async-start(bf16[16,176,256]{2,1,0:T(8,128)(2,1)} %broadcast_dynamic-update-slice_fusion), calls=%async_computation.3 | async-start | bytes 2883584 | tf_op jit(solution)/shard_map/all_to_all | solution.py:76
  112.8 12.8 %collective-permute-start.6 = (bf16[176,256]{1,0:T(8,128)(2,1)S(1)}, bf16[176,256]{1,0:T(8,128)(2,1)S(1)}, u32[]{:S(2)}, u32[]{:S(2)}) collective-permute-start(bf16[176,256]{1,0:T(8,128)(2,1)S(1)} %reduce_sum.42), channel_id=1, source_target_pairs={{0,1},{1,0},{2,3},{3,2},{4,5},{5,4},{6,7},{7,6},{8,9},{9,8},{10,11... | collective-permute-start | bytes 270344 | tf_op jit(solution)/shard_map/ppermute | solution.py:86
  115.8 9.7 %collective-permute-start.7 = (bf16[176,256]{1,0:T(8,128)(2,1)S(1)}, bf16[176,256]{1,0:T(8,128)(2,1)S(1)}, u32[]{:S(2)}, u32[]{:S(2)}) collective-permute-start(bf16[176,256]{1,0:T(8,128)(2,1)S(1)} %reduce_sum.42), channel_id=1, source_target_pairs={{0,2},{1,3},{2,0},{3,1},{4,6},{5,7},{6,4},{7,5},{8,10},{9,11},{10,... | collective-permute-start | bytes 270344 | tf_op jit(solution)/shard_map/ppermute | solution.py:86
  120.1 8.1 %collective-permute-start.8 = (bf16[176,256]{1,0:T(8,128)(2,1)S(1)}, bf16[176,256]{1,0:T(8,128)(2,1)S(1)}, u32[]{:S(2)}, u32[]{:S(2)}) collective-permute-start(bf16[176,256]{1,0:T(8,128)(2,1)S(1)} %reduce_sum.42), channel_id=1, source_target_pairs={{0,3},{1,2},{2,1},{3,0},{4,7},{5,6},{6,5},{7,4},{8,11},{9,10},{10,... | collective-permute-start | bytes 270344 | tf_op jit(solution)/shard_map/ppermute | solution.py:86
  121.5 39.7 %collective-permute-start = (bf16[1024,256]{1,0:T(8,128)(2,1)S(1)}, bf16[1024,256]{1,0:T(8,128)(2,1)}, u32[]{:S(2)}, u32[]{:S(2)}) collective-permute-start(bf16[1024,256]{1,0:T(8,128)(2,1)S(1)} %get-tuple-element.24), channel_id=1, source_target_pairs={{0,4},{1,5},{2,6},{3,7},{4,0},{5,1},{6,2},{7,3},{8,12},{9,13},{10,... | collective-permute-start | bytes 1572872 | tf_op jit(solution)/shard_map/ppermute | solution.py:86
  122.9 38.4 %collective-permute-start.1 = (bf16[1024,256]{1,0:T(8,128)(2,1)S(1)}, bf16[1024,256]{1,0:T(8,128)(2,1)}, u32[]{:S(2)}, u32[]{:S(2)}) collective-permute-start(bf16[1024,256]{1,0:T(8,128)(2,1)S(1)} %get-tuple-element.26), channel_id=1, source_target_pairs={{0,8},{1,9},{2,10},{3,11},{4,12},{5,13},{6,14},{7,15},{8,0},{9,1},... | collective-permute-start | bytes 1572872 | tf_op jit(solution)/shard_map/ppermute | solution.py:86
  125.5 35.8 %collective-permute-start.2 = (bf16[1024,256]{1,0:T(8,128)(2,1)S(1)}, bf16[1024,256]{1,0:T(8,128)(2,1)}, u32[]{:S(2)}, u32[]{:S(2)}) collective-permute-start(bf16[1024,256]{1,0:T(8,128)(2,1)S(1)} %get-tuple-element.25), channel_id=1, source_target_pairs={{0,12},{1,13},{2,14},{3,15},{4,8},{5,9},{6,10},{7,11},{8,4},{9,5},... | collective-permute-start | bytes 1572872 | tf_op jit(solution)/shard_map/ppermute | solution.py:86
  128.2 21.1 %collective-permute-start.10 = (bf16[176,256]{1,0:T(8,128)(2,1)S(1)}, bf16[176,256]{1,0:T(8,128)(2,1)S(1)}, u32[]{:S(2)}, u32[]{:S(2)}) collective-permute-start(bf16[176,256]{1,0:T(8,128)(2,1)S(1)} %add_convert_fusion.1), channel_id=1, source_target_pairs={{0,8},{1,9},{2,10},{3,11},{4,12},{5,13},{6,14},{7,15},{8,0},{9,1},... | collective-permute-start | bytes 270344 | tf_op jit(solution)/shard_map/ppermute | solution.py:86
  131.2 22.1 %collective-permute-start.11 = (bf16[176,256]{1,0:T(8,128)(2,1)S(1)}, bf16[176,256]{1,0:T(8,128)(2,1)S(1)}, u32[]{:S(2)}, u32[]{:S(2)}) collective-permute-start(bf16[176,256]{1,0:T(8,128)(2,1)S(1)} %add_convert_fusion.1), channel_id=1, source_target_pairs={{0,12},{1,13},{2,14},{3,15},{4,8},{5,9},{6,10},{7,11},{8,4},{9,5},... | collective-permute-start | bytes 270344 | tf_op jit(solution)/shard_map/ppermute | solution.py:86
  149.3 4.0 %collective-permute-start.9 = (bf16[176,256]{1,0:T(8,128)(2,1)S(1)}, bf16[176,256]{1,0:T(8,128)(2,1)S(1)}, u32[]{:S(2)}, u32[]{:S(2)}) collective-permute-start(bf16[176,256]{1,0:T(8,128)(2,1)S(1)} %add_convert_fusion.1), channel_id=1, source_target_pairs={{0,4},{1,5},{2,6},{3,7},{4,0},{5,1},{6,2},{7,3},{8,12},{9,13},{10,... | collective-permute-start | bytes 270344 | tf_op jit(solution)/shard_map/ppermute | solution.py:86
  154.4 34.4 %all-to-all-start.4 = ((bf16[16,96,256]{2,1,0:T(8,128)(2,1)}), bf16[16,96,256]{2,1,0:T(8,128)(2,1)S(1)}, u32[]{:S(2)}, u32[]{:S(2)}) async-start(bf16[16,96,256]{2,1,0:T(8,128)(2,1)} %broadcast_in_dim.8), calls=%async_computation.4 | async-start | bytes 1572864 | tf_op jit(solution)/shard_map/all_to_all | solution.py:76
  161.2 7.8 %copy-start.5 = (bf16[2048,512]{1,0:T(8,128)(2,1)S(1)}, bf16[2048,512]{1,0:T(8,128)(2,1)}, u32[]{:S(2)}) copy-start(bf16[2048,512]{1,0:T(8,128)(2,1)} %get-tuple-element.23) | copy-start | bytes 6291460
  161.2 7.8 %copy-start.10 = (bf16[512,256]{1,0:T(8,128)(2,1)S(1)}, bf16[512,256]{1,0:T(8,128)(2,1)}, u32[]{:S(2)}) copy-start(bf16[512,256]{1,0:T(8,128)(2,1)} %param.14) | copy-start | bytes 786436
  163.3 9.8 %collective-permute-start.3 = (bf16[256,256]{1,0:T(8,128)(2,1)S(1)}, bf16[256,256]{1,0:T(8,128)(2,1)S(1)}, u32[]{:S(2)}, u32[]{:S(2)}) collective-permute-start(bf16[256,256]{1,0:T(8,128)(2,1)S(1)} %get-tuple-element.30), channel_id=1, source_target_pairs={{0,1},{1,0},{2,3},{3,2},{4,5},{5,4},{6,7},{7,6},{8,9},{9,8},{10,11... | collective-permute-start | bytes 393224 | tf_op jit(solution)/shard_map/ppermute | solution.py:86
  164.8 22.0 %collective-permute-start.4 = (bf16[256,256]{1,0:T(8,128)(2,1)S(1)}, bf16[256,256]{1,0:T(8,128)(2,1)S(1)}, u32[]{:S(2)}, u32[]{:S(2)}) collective-permute-start(bf16[256,256]{1,0:T(8,128)(2,1)S(1)} %get-tuple-element.32), channel_id=1, source_target_pairs={{0,2},{1,3},{2,0},{3,1},{4,6},{5,7},{6,4},{7,5},{8,10},{9,11},{10,... | collective-permute-start | bytes 393224 | tf_op jit(solution)/shard_map/ppermute | solution.py:86
  169.0 17.8 %collective-permute-start.5 = (bf16[256,256]{1,0:T(8,128)(2,1)S(1)}, bf16[256,256]{1,0:T(8,128)(2,1)S(1)}, u32[]{:S(2)}, u32[]{:S(2)}) collective-permute-start(bf16[256,256]{1,0:T(8,128)(2,1)S(1)} %get-tuple-element.31), channel_id=1, source_target_pairs={{0,3},{1,2},{2,1},{3,0},{4,7},{5,6},{6,5},{7,4},{8,11},{9,10},{10,... | collective-permute-start | bytes 393224 | tf_op jit(solution)/shard_map/ppermute | solution.py:86
  (3 other events, 2.6 us)

commit v2 on v1

v2 whole, which is shorter than its diff:
```python
import functools

import jax
import jax.numpy as jnp
from jax import lax
from jax.experimental import pallas as pl
from jax.experimental.pallas import tpu as pltpu
from jax.sharding import PartitionSpec as P

epsilon = 1e-06
BF = jnp.bfloat16
F32 = jnp.float32
STEPS = {"y": 4, "z": 1}


def contract(left, right, left_dim, right_dim):
    return lax.dot_general(
        left, right, (((left_dim,), (right_dim,)), ((), ())), preferred_element_type=F32
    )


def lookup_kernel(high_ref, low_ref, table_ref, counts_ref, embeds_ref):
    groups = high_ref.shape[0]
    slot = lax.broadcasted_iota(jnp.int32, (256, 128), 0)

    def step(g, carry):
        left = jnp.where(slot == high_ref[pl.ds(g, 1), :], 1.0, 0.0).astype(BF)
        right = jnp.where(slot == low_ref[pl.ds(g, 1), :], 1.0, 0.0).astype(BF)
        both = contract(left, right, 1, 1).astype(BF)
        for h in range(16):
            counts_ref[pl.ds(pl.multiple_of(g * 16, 16), 16), h * 256 : (h + 1) * 256] = both[
                h * 16 : (h + 1) * 16
            ]
        return carry

    lax.fori_loop(0, groups, step, 0, unroll=8)
    embeds_ref[...] = jnp.dot(
        counts_ref[...], table_ref[...], preferred_element_type=F32
    ).astype(BF)


def lookup(emb_table, feature_ids):
    samples, feats, pool = feature_ids.shape
    rows = samples * feats
    lanes = (
        feature_ids.reshape(samples, feats // 16, 16, pool)
        .transpose(0, 1, 3, 2)
        .reshape(rows // 16, 128)
    )
    high = (lanes // 256) * 16 + lax.broadcasted_iota(jnp.int32, lanes.shape, 1) % 16
    low = lanes % 256
    steps = 1
    return pl.pallas_call(
        lookup_kernel,
        grid=(steps,),
        in_specs=[
            pl.BlockSpec((rows // 16 // steps, 128), lambda i: (i, 0)),
            pl.BlockSpec((rows // 16 // steps, 128), lambda i: (i, 0)),
            pl.BlockSpec(emb_table.shape, lambda i: (0, 0)),
        ],
        out_specs=[
            pl.BlockSpec((rows // steps, emb_table.shape[0]), lambda i: (i, 0)),
            pl.BlockSpec((rows // steps, emb_table.shape[1]), lambda i: (i, 0)),
        ],
        out_shape=[
            jax.ShapeDtypeStruct((rows, emb_table.shape[0]), BF),
            jax.ShapeDtypeStruct((rows, emb_table.shape[1]), BF),
        ],
        cost_estimate=pl.CostEstimate(
            flops=4 * rows * emb_table.shape[0] * emb_table.shape[1],
            bytes_accessed=2 * rows * emb_table.shape[0] + 4 * emb_table.size,
            transcendentals=0,
        ),
        name="lookup",
    )(high, low, emb_table)


def exchange(values, axis):
    return lax.all_to_all(values, axis, 0, 0)


def place(part):
    batch = lax.axis_index("batch")
    return batch // 4 if part == "y" else batch % 4


def swap(values, part, offset):
    pairs = [(b, b ^ (STEPS[part] * offset)) for b in range(16)]
    return lax.ppermute(values, "batch", pairs)


def sum_scattered(values, part):
    mine = place(part)
    take = lambda i: lax.dynamic_index_in_dim(values, i, 0, keepdims=False)
    came = [swap(take(mine ^ k), part, k) for k in (1, 2, 3)]
    return sum((c.astype(F32) for c in came), take(mine).astype(F32))


def sum_all(values, part):
    came = [swap(values, part, k) for k in (1, 2, 3)]
    return sum((c.astype(F32) for c in came), values.astype(F32)).astype(BF)


def gathered(values, axis, size):
    return exchange(jnp.broadcast_to(values[None], (size,) + values.shape), axis)


CHUNK = 256


def sample_kernel(
    which,
    x_ref,
    proj_ref,
    grad_ref,
    gain_ref,
    gate_ref,
    up_ref,
    down_ref,
    embed_ref,
    scaled_ref,
    gate_grad_ref,
    up_grad_ref,
    hidden_ref,
    inter_grad_ref,
    gain_grad_ref,
    interact_grad_ref,
):
    inter_map = contract(x_ref[...], proj_ref[...], 0, 0).astype(BF)
    gain_grad_ref[...] = jnp.zeros_like(gain_grad_ref)

    def step(i, carry):
        rows = pl.ds(pl.multiple_of(i * CHUNK, CHUNK), CHUNK)
        interact = jnp.dot(x_ref[rows, :], inter_map, preferred_element_type=F32)
        inv_rms = lax.rsqrt(jnp.mean(interact * interact, axis=-1, keepdims=True) + epsilon)
        normed = interact * inv_rms
        scaled = (normed * gain_ref[...]).astype(BF)
        scaled_ref[rows, :] = scaled
        scaled_grad = jnp.zeros((CHUNK, scaled.shape[1]), F32)
        for h in range(2):
            cols = slice(h * 256, (h + 1) * 256)
            gate_pre = jnp.dot(scaled, gate_ref[:, cols], preferred_element_type=F32)
            up_pre = jnp.dot(scaled, up_ref[:, cols], preferred_element_type=F32)
            hidden_grad = contract(grad_ref[which, rows, :], down_ref[cols, :], 1, 1)
            sigmoid = 1.0 / (1.0 + jnp.exp(-gate_pre))
            silu = gate_pre * sigmoid
            hidden_ref[rows, cols] = (silu * up_pre).astype(BF)
            up_grad = (hidden_grad * silu).astype(BF)
            up_grad_ref[rows, cols] = up_grad
            gate_grad = (
                hidden_grad * up_pre * sigmoid * (1.0 + gate_pre * (1.0 - sigmoid))
            ).astype(BF)
            gate_grad_ref[rows, cols] = gate_grad
            scaled_grad += contract(gate_grad, gate_ref[:, cols], 1, 1)
            scaled_grad += contract(up_grad, up_ref[:, cols], 1, 1)
        times_normed = scaled_grad * normed
        gain_grad_ref[...] += jnp.sum(times_normed.reshape(CHUNK // 8, 8, -1), axis=0)
        mean = jnp.mean(times_normed * gain_ref[...], axis=-1, keepdims=True)
        interact_grad_ref[rows, :] = (
            inv_rms * (scaled_grad * gain_ref[...] - normed * mean)
        ).astype(BF)
        return carry

    lax.fori_loop(0, x_ref.shape[0] // CHUNK, step, 0)
    inter_grad = contract(x_ref[...], interact_grad_ref[...], 0, 0).astype(BF)
    inter_grad_ref[...] = inter_grad
    embed_ref[...] = (
        contract(interact_grad_ref[...], inter_map, 1, 1) + contract(proj_ref[...], inter_grad, 1, 1)
    ).astype(BF)


def sample_pass(which, x, proj, out_grad, norm_gain, gate_weight, up_weight, down_weight):
    rows, width = x.shape
    hidden = gate_weight.shape[1]
    shape = jax.ShapeDtypeStruct
    return pl.pallas_call(
        functools.partial(sample_kernel, which),
        out_shape=[
            shape((rows, width), BF),
            shape((rows, width), BF),
            shape((rows, hidden), BF),
            shape((rows, hidden), BF),
            shape((rows, hidden), BF),
            shape((width, width), BF),
            shape((8, width), F32),
        ],
        in_specs=[pl.BlockSpec(memory_space=pltpu.VMEM)] * 7,
        out_specs=[pl.BlockSpec(memory_space=pltpu.VMEM)] * 7,
        scratch_shapes=[pltpu.VMEM((rows, width), BF)],
        cost_estimate=pl.CostEstimate(
            flops=9000000000, bytes_accessed=8 * rows * width * 2, transcendentals=rows * hidden
        ),
        compiler_params=pltpu.CompilerParams(vmem_limit_bytes=40 << 20),
        name="sample_pass",
    )(x, proj, out_grad, norm_gain[None], gate_weight, up_weight, down_weight)


def parts_kernel(*refs):
    (x0, x1, grads, down, s0, g0, u0, h0, z0, n0, s1, g1, u1, h1, z1, n1, out_ref, parts_ref) = refs

    def over(a0, b0, a1, b1):
        return contract(a0[...], b0[...], 0, 0) + contract(a1[...], b1[...], 0, 0)

    for at, part in ((0, over(s0, g0, s1, g1)), (32, over(s0, u0, s1, u1))):
        part = part.astype(BF).reshape(16, 16, 512)
        parts_ref[:, at : at + 16, :] = part[:, :, :256]
        parts_ref[:, at + 16 : at + 32, :] = part[:, :, 256:]
    part = over(h0, grads.at[0], h1, grads.at[1]).astype(BF)
    parts_ref[:, 64:96, :] = part.reshape(16, 32, 256)
    part = jnp.dot(x0[...], z0[...], preferred_element_type=F32) + jnp.dot(
        x1[...], z1[...], preferred_element_type=F32
    )
    parts_ref[:, 96:160, :] = part.astype(BF).reshape(16, 64, 256)
    part = jnp.sum(n0[...] + n1[...], axis=0, keepdims=True)
    parts_ref[:, 160:176, :] = jnp.broadcast_to(part[None], (16, 16, 256)).astype(BF)
    for s, hidden in enumerate((h0, h1)):
        out_ref[s] = jnp.dot(hidden[...], down[...], preferred_element_type=F32).astype(BF)


def parts_of(xs, out_grad, down_weight, passes):
    saved = [v for p in passes for v in p[1:]]
    return pl.pallas_call(
        parts_kernel,
        out_shape=[
            jax.ShapeDtypeStruct(out_grad.shape, BF),
            jax.ShapeDtypeStruct((16, 176, out_grad.shape[2]), BF),
        ],
        in_specs=[pl.BlockSpec(memory_space=pltpu.VMEM)] * (4 + len(saved)),
        out_specs=[pl.BlockSpec(memory_space=pltpu.VMEM)] * 2,
        cost_estimate=pl.CostEstimate(
            flops=6000000000, bytes_accessed=16000000, transcendentals=0
        ),
        compiler_params=pltpu.CompilerParams(vmem_limit_bytes=40 << 20),
        name="parts",
    )(*xs, out_grad, down_weight, *saved)


def per_device(
    emb_table, feature_ids, projection, norm_gain, gate_weight, up_weight, down_weight, out_grad
):
    samples, feats, pool = feature_ids.shape
    shards = 16
    own = samples // shards
    width = emb_table.shape[1]
    rank = projection.shape[1]
    all_feats = shards * feats
    proj = gathered(projection, "table", shards).reshape(all_feats, rank)
    ids = feature_ids.reshape(shards, own, feats, pool)
    counts, xs, passes, backs = [], [], [], []
    for c in range(own):
        count, embeds = lookup(emb_table, ids[:, c])
        if c == 0:
            embeds, proj = lax.optimization_barrier((embeds, proj))
        x = exchange(embeds.reshape(shards, feats, width), "table")
        counts.append(count)
        xs.append(x.reshape(all_feats, width))
        passes.append(
            sample_pass(c, xs[c], proj, out_grad, norm_gain, gate_weight, up_weight, down_weight)
        )
        back = exchange(passes[c][0].reshape(shards, feats, width), "table")
        backs.append(back.reshape(-1, width))

    block_out, parts = parts_of(xs, out_grad, down_weight, passes)
    parts, backs[-1] = lax.optimization_barrier((parts, backs[-1]))
    parts = exchange(parts, "table")
    parts = jnp.sum(parts.astype(F32), axis=0).astype(BF)
    parts = sum_all(parts, "z")
    parts = sum_all(parts, "y")
    projection_grad = parts[96:160].astype(F32)
    gain_grad = parts[160].astype(F32)
    weights = gathered(parts[:96], "table", shards)
    weights = weights.astype(F32)

    def joined(piece):
        return (
            piece.reshape(shards, 2, rank // shards, hidden_width // 2)
            .transpose(0, 2, 1, 3)
            .reshape(rank, hidden_width)
        )

    hidden_width = gate_weight.shape[1]
    gate_grad = joined(weights[:, :32])
    up_grad = joined(weights[:, 32:64])
    down_grad = weights[:, 64:96].reshape(hidden_width, width)

    table_term = contract(counts[0], backs[0], 0, 0)
    for c in range(1, own):
        table_term = table_term + contract(counts[c], backs[c], 0, 0)
    table_term = table_term.astype(BF)
    here = table_term.shape[0] // 16
    table_term = sum_scattered(table_term.reshape(4, 4 * here, width), "y").astype(BF)
    table_grad = sum_scattered(table_term.reshape(4, here, width), "z")
    return (block_out, table_grad, projection_grad, gain_grad, gate_grad, up_grad, down_grad)


def solution(mesh):
    return jax.shard_map(
        per_device,
        mesh=mesh,
        in_specs=(
            P("table", None),
            P("batch", "table", None),
            P("table", None),
            P(),
            P(),
            P(),
            P(),
            P(("batch", "table"), None, None),
        ),
        out_specs=(
            P(("batch", "table"), None, None),
            P(("table", "batch"), None),
            P("table", None),
            P(),
            P(),
            P(),
            P(),
        ),
        check_vma=False,
    )
```

time: 193 us -> 188 us (0.974)
  the two profiles are of different devices: /device:TPU:1 before, /device:TPU:38 now
where the time goes in v2:
time: 188 us; the launch traced here: 186 us
  starting transfers between devices  63.8 us (34%)
  waiting for transfers between devices  38.9 us (21%)
  Pallas kernels  34.5 us (18%)
  local copies, waits for them, and re-layouts  28.5 us (15%)
  matrix products  15.3 us (8%)
  other arithmetic  4.6 us (2%)
    all_to_all x7, starting transfers between devices, exchange(): return lax.all_to_all(values, axis, 0, 0)  39.9 us
    ppermute x12, waiting for transfers between devices, swap(): return lax.ppermute(values, 'batch', pairs)  28.2 us
    ppermute x12, starting transfers between devices, swap(): return lax.ppermute(values, 'batch', pairs)  23.9 us
    unnamed x53, local copies, waits for them, and re-layouts  22.3 us
    pallas_call x2, Pallas kernels, lookup(): pl.pallas_call(lookup_kernel, grid=(steps,), in_specs=[pl.BlockSpec((rows...  17.9 us
    dot_general x2, matrix products, contract(): lax.dot_general(left, right, (((left_dim,), (right_dim,)), ((), ())), pre...  15.3 us
    pallas_call x2, Pallas kernels, sample_pass(): pl.pallas_call(functools.partial(sample_kernel, which), out_shape=[shape(...  12.6 us
    all_to_all x7, waiting for transfers between devices, exchange(): return lax.all_to_all(values, axis, 0, 0)  10.7 us
  transfers between devices with their start and end apart: 19, of which 8 were waited for; matrix products, arithmetic and copies ran while one was open for 12% of the time, Pallas kernels for 18%

profile of v2, /device:TPU:38, one launch (start us, length us, event | category | flops | bytes accessed | tf_op | source)
XLA Modules:
  0.0 186.5 jit_solution(7028517557256744693)
XLA Ops:
  2.2 5.7 %all-to-all-start = ((bf16[16,64,256]{2,1,0:T(8,128)(2,1)}), bf16[16,64,256]{2,1,0:T(8,128)(2,1)S(1)}, u32[]{:S(2)}, u32[]{:S(2)}) async-start(bf16[16,64,256]{2,1,0:T(8,128)(2,1)} %broadcast_in_dim.6), calls=%async_computation | async-start | bytes 1048576 | tf_op jit(solution)/shard_map/all_to_all | solution.py:79
  10.2 8.9 %lookup.3 = (bf16[1024,4096]{1,0:T(8,128)(2,1)}, bf16[1024,256]{1,0:T(8,128)(2,1)}) custom-call(s32[64,128]{1,0:T(8,128)} %get-tuple-element.67.high_ref, s32[64,128]{1,0:T(8,128)} %get-tuple-element.66.low_ref, bf16[4096,256]{1,0:T(8,128)(2,1)} %table_ref.3), custom_call_target="tpu_custom_call" | custom-call | flops 4294967296 | bytes 12582912 | tf_op jit(solution)/shard_map/lookup/pallas_call | solution.py:53
  19.1 5.7 %all-to-all-start.2 = ((bf16[16,64,256]{2,1,0:T(8,128)(2,1)}), bf16[16,64,256]{2,1,0:T(8,128)(2,1)S(1)}, u32[]{:S(2)}, u32[]{:S(2)}) async-start(bf16[16,64,256]{2,1,0:T(8,128)(2,1)} %bitcast.86), calls=%async_computation.2 | async-start | bytes 1048576 | tf_op jit(solution)/shard_map/all_to_all | solution.py:79
  24.9 9.0 %lookup.2 = (bf16[1024,4096]{1,0:T(8,128)(2,1)}, bf16[1024,256]{1,0:T(8,128)(2,1)}) custom-call(s32[64,128]{1,0:T(8,128)} %get-tuple-element.70.high_ref, s32[64,128]{1,0:T(8,128)} %get-tuple-element.71.low_ref, bf16[4096,256]{1,0:T(8,128)(2,1)} %table_ref.3), custom_call_target="tpu_custom_call" | custom-call | flops 4294967296 | bytes 12582912 | tf_op jit(solution)/shard_map/lookup/pallas_call | solution.py:53
  33.9 5.7 %all-to-all-start.1 = ((bf16[16,64,256]{2,1,0:T(8,128)(2,1)}), bf16[16,64,256]{2,1,0:T(8,128)(2,1)S(1)}, u32[]{:S(2)}, u32[]{:S(2)}) async-start(bf16[16,64,256]{2,1,0:T(8,128)(2,1)} %bitcast.84), calls=%async_computation.1 | async-start | bytes 1048576 | tf_op jit(solution)/shard_map/all_to_all | solution.py:79
  39.7 6.3 %sample_pass.3 = (bf16[1024,256]{1,0:T(8,128)(2,1)}, bf16[1024,256]{1,0:T(8,128)(2,1)S(1)}, bf16[1024,512]{1,0:T(8,128)(2,1)S(1)}, bf16[1024,512]{1,0:T(8,128)(2...) custom-call(bf16[1024,256]{1,0:T(8,128)(2,1)S(1)} %bitcast.67, ...), custom_call_target="tpu_custom_call" | custom-call | flops 8999999488 | bytes 4194304 | tf_op jit(solution)/shard_map/sample_pass/pallas_call | solution.py:176
  49.7 5.7 %all-to-all-start.4 = ((bf16[16,64,256]{2,1,0:T(8,128)(2,1)}), bf16[16,64,256]{2,1,0:T(8,128)(2,1)}, u32[]{:S(2)}, u32[]{:S(2)}) async-start(bf16[16,64,256]{2,1,0:T(8,128)(2,1)} %bitcast.11), calls=%async_computation.4 | async-start | bytes 1048576 | tf_op jit(solution)/shard_map/all_to_all | solution.py:79
  55.4 6.3 %sample_pass.2 = (bf16[1024,256]{1,0:T(8,128)(2,1)}, bf16[1024,256]{1,0:T(8,128)(2,1)S(1)}, bf16[1024,512]{1,0:T(8,128)(2,1)S(1)}, bf16[1024,512]{1,0:T(8,128)(2...) custom-call(bf16[1024,256]{1,0:T(8,128)(2,1)S(1)} %bitcast.69, ...), custom_call_target="tpu_custom_call" | custom-call | flops 8999999488 | bytes 4194304 | tf_op jit(solution)/shard_map/sample_pass/pallas_call | solution.py:176
  66.7 5.7 %all-to-all-start.3 = ((bf16[16,64,256]{2,1,0:T(8,128)(2,1)}), bf16[16,64,256]{2,1,0:T(8,128)(2,1)S(1)}, u32[]{:S(2)}, u32[]{:S(2)}) async-start(bf16[16,64,256]{2,1,0:T(8,128)(2,1)} %bitcast.9), calls=%async_computation.3 | async-start | bytes 1048576 | tf_op jit(solution)/shard_map/all_to_all | solution.py:79
  83.5 4.0 %parts.1 = (bf16[2,1024,256]{2,1,0:T(8,128)(2,1)}, bf16[16,176,256]{2,1,0:T(8,128)(2,1)}) custom-call(bf16[1024,256]{1,0:T(8,128)(2,1)S(1)} %bitcast.70, bf16[1024,256]{1,0:T(8,128)(2,1)S(1)} %bitcast.68, bf16[2,1024,256]{2,1,0:T(8,128)(2,1)S(1)} %copy-done, bf16[512,256]{1,0:T(8,128)(2,1)S(1)} %copy-done.3, bf16[1024,256]{1,0:T(8,128)(2,1)S(1)} %copy-done.20, ...), custom_call_target="tpu_custom_call" | custom-call | flops 6000000000 | bytes 16000000 | tf_op jit(solution)/shard_map/parts/pallas_call | solution.py:222
  87.5 5.7 %all-to-all-start.5 = ((bf16[16,176,256]{2,1,0:T(8,128)(2,1)}), bf16[16,176,256]{2,1,0:T(8,128)(2,1)S(1)}, u32[]{:S(2)}, u32[]{:S(2)}) async-start(bf16[16,176,256]{2,1,0:T(8,128)(2,1)} %get-tuple-element.54), calls=%async_computation.5 | async-start | bytes 2883584 | tf_op jit(solution)/shard_map/all_to_all | solution.py:79
  93.2 7.9 %fusion.13 = f32[4096,256]{1,0:T(8,128)} fusion(bf16[1024,4096]{1,0:T(8,128)(2,1)} %get-tuple-element.48, bf16[1024,256]{1,0:T(8,128)(2,1)S(1)} %bitcast.83), kind=kOutput, calls=%fused_computation.45 | convolution fusion | flops 2147483648 | bytes 13107200 | tf_op jit(solution)/shard_map/dot_general | solution.py:17
  101.1 10.7 %all-to-all-done.5 = bf16[16,176,256]{2,1,0:T(8,128)(2,1)S(1)} async-done(((bf16[16,176,256]{2,1,0:T(8,128)(2,1)}), bf16[16,176,256]{2,1,0:T(8,128)(2,1)S(1)}, u32[]{:S(2)}, u32[]{:S(2)}) %all-to-all-start.5) | async-done | bytes 1441824 | tf_op jit(solution)/shard_map/all_to_all | solution.py:79
  111.9 5.5 %collective-permute-start.8 = (bf16[176,256]{1,0:T(8,128)(2,1)S(1)}, bf16[176,256]{1,0:T(8,128)(2,1)S(1)}, u32[]{:S(2)}, u32[]{:S(2)}) collective-permute-start(bf16[176,256]{1,0:T(8,128)(2,1)S(1)} %reduce_sum.12), channel_id=1, source_target_pairs={{0,3},{1,2},{2,1},{3,0},{4,7},{5,6},{6,5},{7,4},{8,11},{9,10},{10,... | collective-permute-start | bytes 270344 | tf_op jit(solution)/shard_map/ppermute | solution.py:89
  119.9 7.5 %fusion = bf16[4096,256]{1,0:T(8,128)(2,1)S(1)} fusion(f32[4096,256]{1,0:T(8,128)} %fusion.13, bf16[1024,4096]{1,0:T(8,128)(2,1)} %get-tuple-element.50, bf16[1024,256]{1,0:T(8,128)(2,1)} %bitcast.12), kind=kOutput, calls=%fused_computation.1 | convolution fusion | flops 2149580800 | bytes 15204352 | tf_op jit(solution)/shard_map/dot_general | solution.py:17
  129.2 3.1 %collective-permute-start.11 = (bf16[176,256]{1,0:T(8,128)(2,1)S(1)}, bf16[176,256]{1,0:T(8,128)(2,1)S(1)}, u32[]{:S(2)}, u32[]{:S(2)}) collective-permute-start(bf16[176,256]{1,0:T(8,128)(2,1)S(1)} %add_convert_fusion.1), channel_id=1, source_target_pairs={{0,12},{1,13},{2,14},{3,15},{4,8},{5,9},{6,10},{7,11},{8,4},{9,5},... | collective-permute-start | bytes 270344 | tf_op jit(solution)/shard_map/ppermute | solution.py:89
  140.3 5.6 %all-to-all-start.6 = ((bf16[16,96,256]{2,1,0:T(8,128)(2,1)}), bf16[16,96,256]{2,1,0:T(8,128)(2,1)S(1)}, u32[]{:S(2)}, u32[]{:S(2)}) async-start(bf16[16,96,256]{2,1,0:T(8,128)(2,1)} %broadcast_in_dim.8), calls=%async_computation.6 | async-start | bytes 1572864 | tf_op jit(solution)/shard_map/all_to_all | solution.py:79
  145.9 4.0 %collective-permute-done = bf16[1024,256]{1,0:T(8,128)(2,1)} collective-permute-done((bf16[1024,256]{1,0:T(8,128)(2,1)}, bf16[1024,256]{1,0:T(8,128)(2,1)}, u32[]{:S(2)}, u32[]{:S(2)}) %collective-permute-start) | collective-permute-done | bytes 524320 | tf_op jit(solution)/shard_map/ppermute | solution.py:89
  150.6 11.2 %collective-permute-done.1 = bf16[1024,256]{1,0:T(8,128)(2,1)} collective-permute-done((bf16[1024,256]{1,0:T(8,128)(2,1)S(1)}, bf16[1024,256]{1,0:T(8,128)(2,1)}, u32[]{:S(2)}, u32[]{:S(2)}) %collective-permute-start.1) | collective-permute-done | bytes 524320 | tf_op jit(solution)/shard_map/ppermute | solution.py:89
  163.5 2.5 %collective-permute-start.3 = (bf16[256,256]{1,0:T(8,128)(2,1)S(1)}, bf16[256,256]{1,0:T(8,128)(2,1)S(1)}, u32[]{:S(2)}, u32[]{:S(2)}) collective-permute-start(bf16[256,256]{1,0:T(8,128)(2,1)S(1)} %get-tuple-element.61), channel_id=1, source_target_pairs={{0,1},{1,0},{2,3},{3,2},{4,5},{5,4},{6,7},{7,6},{8,9},{9,8},{10,11... | collective-permute-start | bytes 393224 | tf_op jit(solution)/shard_map/ppermute | solution.py:89
  166.0 2.6 %collective-permute-start.5 = (bf16[256,256]{1,0:T(8,128)(2,1)S(1)}, bf16[256,256]{1,0:T(8,128)(2,1)S(1)}, u32[]{:S(2)}, u32[]{:S(2)}) collective-permute-start(bf16[256,256]{1,0:T(8,128)(2,1)S(1)} %get-tuple-element.62), channel_id=1, source_target_pairs={{0,3},{1,2},{2,1},{3,0},{4,7},{5,6},{6,5},{7,4},{8,11},{9,10},{10,... | collective-permute-start | bytes 393224 | tf_op jit(solution)/shard_map/ppermute | solution.py:89
  168.6 2.3 %collective-permute-start.4 = (bf16[256,256]{1,0:T(8,128)(2,1)S(1)}, bf16[256,256]{1,0:T(8,128)(2,1)S(1)}, u32[]{:S(2)}, u32[]{:S(2)}) collective-permute-start(bf16[256,256]{1,0:T(8,128)(2,1)S(1)} %get-tuple-element.63), channel_id=1, source_target_pairs={{0,2},{1,3},{2,0},{3,1},{4,6},{5,7},{6,4},{7,5},{8,10},{9,11},{10,... | collective-permute-start | bytes 393224 | tf_op jit(solution)/shard_map/ppermute | solution.py:89
  170.9 4.3 %collective-permute-done.5 = bf16[256,256]{1,0:T(8,128)(2,1)S(1)} collective-permute-done((bf16[256,256]{1,0:T(8,128)(2,1)S(1)}, bf16[256,256]{1,0:T(8,128)(2,1)S(1)}, u32[]{:S(2)}, u32[]{:S(2)}) %collective-permute-start.5) | collective-permute-done | bytes 131104 | tf_op jit(solution)/shard_map/ppermute | solution.py:89
  175.2 5.9 %collective-permute-done.4 = bf16[256,256]{1,0:T(8,128)(2,1)S(1)} collective-permute-done((bf16[256,256]{1,0:T(8,128)(2,1)S(1)}, bf16[256,256]{1,0:T(8,128)(2,1)S(1)}, u32[]{:S(2)}, u32[]{:S(2)}) %collective-permute-start.4) | collective-permute-done | bytes 131104 | tf_op jit(solution)/shard_map/ppermute | solution.py:89
  (99 shorter events, 43.9 us)
Async XLA Ops:
  2.2 16.9 %all-to-all-start = ((bf16[16,64,256]{2,1,0:T(8,128)(2,1)}), bf16[16,64,256]{2,1,0:T(8,128)(2,1)S(1)}, u32[]{:S(2)}, u32[]{:S(2)}) async-start(bf16[16,64,256]{2,1,0:T(8,128)(2,1)} %broadcast_in_dim.6), calls=%async_computation | async-start | bytes 1048576 | tf_op jit(solution)/shard_map/all_to_all | solution.py:79
  19.1 14.8 %all-to-all-start.2 = ((bf16[16,64,256]{2,1,0:T(8,128)(2,1)}), bf16[16,64,256]{2,1,0:T(8,128)(2,1)S(1)}, u32[]{:S(2)}, u32[]{:S(2)}) async-start(bf16[16,64,256]{2,1,0:T(8,128)(2,1)} %bitcast.86), calls=%async_computation.2 | async-start | bytes 1048576 | tf_op jit(solution)/shard_map/all_to_all | solution.py:79
  24.8 14.8 %copy-start = (bf16[2,1024,256]{2,1,0:T(8,128)(2,1)S(1)}, bf16[2,1024,256]{2,1,0:T(8,128)(2,1)}, u32[]{:S(2)}) copy-start(bf16[2,1024,256]{2,1,0:T(8,128)(2,1)} %refs_2_.1) | copy-start | bytes 3145732
  24.8 14.8 %copy-start.1 = (bf16[256,512]{1,0:T(8,128)(2,1)S(1)}, bf16[256,512]{1,0:T(8,128)(2,1)}, u32[]{:S(2)}) copy-start(bf16[256,512]{1,0:T(8,128)(2,1)} %gate_ref.3) | copy-start | bytes 786436
  24.8 14.8 %copy-start.2 = (bf16[256,512]{1,0:T(8,128)(2,1)S(1)}, bf16[256,512]{1,0:T(8,128)(2,1)}, u32[]{:S(2)}) copy-start(bf16[256,512]{1,0:T(8,128)(2,1)} %up_ref.3) | copy-start | bytes 786436
  24.8 14.8 %copy-start.3 = (bf16[512,256]{1,0:T(8,128)(2,1)S(1)}, bf16[512,256]{1,0:T(8,128)(2,1)}, u32[]{:S(2)}) copy-start(bf16[512,256]{1,0:T(8,128)(2,1)} %refs_3_.1) | copy-start | bytes 786436
  24.9 14.8 %copy-start.4 = (f32[256]{0:T(256)S(1)}, f32[256]{0:T(256)}, u32[]{:S(2)}) copy-start(f32[256]{0:T(256)} %param.11) | copy-start | bytes 3076
  33.9 15.8 %all-to-all-start.1 = ((bf16[16,64,256]{2,1,0:T(8,128)(2,1)}), bf16[16,64,256]{2,1,0:T(8,128)(2,1)S(1)}, u32[]{:S(2)}, u32[]{:S(2)}) async-start(bf16[16,64,256]{2,1,0:T(8,128)(2,1)} %bitcast.84), calls=%async_computation.1 | async-start | bytes 1048576 | tf_op jit(solution)/shard_map/all_to_all | solution.py:79
  49.7 17.0 %all-to-all-start.4 = ((bf16[16,64,256]{2,1,0:T(8,128)(2,1)}), bf16[16,64,256]{2,1,0:T(8,128)(2,1)}, u32[]{:S(2)}, u32[]{:S(2)}) async-start(bf16[16,64,256]{2,1,0:T(8,128)(2,1)} %bitcast.11), calls=%async_computation.4 | async-start | bytes 1048576 | tf_op jit(solution)/shard_map/all_to_all | solution.py:79
  66.7 20.8 %all-to-all-start.3 = ((bf16[16,64,256]{2,1,0:T(8,128)(2,1)}), bf16[16,64,256]{2,1,0:T(8,128)(2,1)S(1)}, u32[]{:S(2)}, u32[]{:S(2)}) async-start(bf16[16,64,256]{2,1,0:T(8,128)(2,1)} %bitcast.9), calls=%async_computation.3 | async-start | bytes 1048576 | tf_op jit(solution)/shard_map/all_to_all | solution.py:79
  87.5 24.2 %all-to-all-start.5 = ((bf16[16,176,256]{2,1,0:T(8,128)(2,1)}), bf16[16,176,256]{2,1,0:T(8,128)(2,1)S(1)}, u32[]{:S(2)}, u32[]{:S(2)}) async-start(bf16[16,176,256]{2,1,0:T(8,128)(2,1)} %get-tuple-element.54), calls=%async_computation.5 | async-start | bytes 2883584 | tf_op jit(solution)/shard_map/all_to_all | solution.py:79
  111.9 15.4 %collective-permute-start.8 = (bf16[176,256]{1,0:T(8,128)(2,1)S(1)}, bf16[176,256]{1,0:T(8,128)(2,1)S(1)}, u32[]{:S(2)}, u32[]{:S(2)}) collective-permute-start(bf16[176,256]{1,0:T(8,128)(2,1)S(1)} %reduce_sum.12), channel_id=1, source_target_pairs={{0,3},{1,2},{2,1},{3,0},{4,7},{5,6},{6,5},{7,4},{8,11},{9,10},{10,... | collective-permute-start | bytes 270344 | tf_op jit(solution)/shard_map/ppermute | solution.py:89
  117.4 11.7 %collective-permute-start.7 = (bf16[176,256]{1,0:T(8,128)(2,1)S(1)}, bf16[176,256]{1,0:T(8,128)(2,1)S(1)}, u32[]{:S(2)}, u32[]{:S(2)}) collective-permute-start(bf16[176,256]{1,0:T(8,128)(2,1)S(1)} %reduce_sum.12), channel_id=1, source_target_pairs={{0,2},{1,3},{2,0},{3,1},{4,6},{5,7},{6,4},{7,5},{8,10},{9,11},{10,... | collective-permute-start | bytes 270344 | tf_op jit(solution)/shard_map/ppermute | solution.py:89
  118.9 10.3 %collective-permute-start.6 = (bf16[176,256]{1,0:T(8,128)(2,1)S(1)}, bf16[176,256]{1,0:T(8,128)(2,1)S(1)}, u32[]{:S(2)}, u32[]{:S(2)}) collective-permute-start(bf16[176,256]{1,0:T(8,128)(2,1)S(1)} %reduce_sum.12), channel_id=1, source_target_pairs={{0,1},{1,0},{2,3},{3,2},{4,5},{5,4},{6,7},{7,6},{8,9},{9,8},{10,11... | collective-permute-start | bytes 270344 | tf_op jit(solution)/shard_map/ppermute | solution.py:89
  129.2 9.0 %collective-permute-start.11 = (bf16[176,256]{1,0:T(8,128)(2,1)S(1)}, bf16[176,256]{1,0:T(8,128)(2,1)S(1)}, u32[]{:S(2)}, u32[]{:S(2)}) collective-permute-start(bf16[176,256]{1,0:T(8,128)(2,1)S(1)} %add_convert_fusion.1), channel_id=1, source_target_pairs={{0,12},{1,13},{2,14},{3,15},{4,8},{5,9},{6,10},{7,11},{8,4},{9,5},... | collective-permute-start | bytes 270344 | tf_op jit(solution)/shard_map/ppermute | solution.py:89
  132.3 6.9 %collective-permute-start.10 = (bf16[176,256]{1,0:T(8,128)(2,1)S(1)}, bf16[176,256]{1,0:T(8,128)(2,1)S(1)}, u32[]{:S(2)}, u32[]{:S(2)}) collective-permute-start(bf16[176,256]{1,0:T(8,128)(2,1)S(1)} %add_convert_fusion.1), channel_id=1, source_target_pairs={{0,8},{1,9},{2,10},{3,11},{4,12},{5,13},{6,14},{7,15},{8,0},{9,1},... | collective-permute-start | bytes 270344 | tf_op jit(solution)/shard_map/ppermute | solution.py:89
  132.9 6.3 %collective-permute-start.9 = (bf16[176,256]{1,0:T(8,128)(2,1)S(1)}, bf16[176,256]{1,0:T(8,128)(2,1)S(1)}, u32[]{:S(2)}, u32[]{:S(2)}) collective-permute-start(bf16[176,256]{1,0:T(8,128)(2,1)S(1)} %add_convert_fusion.1), channel_id=1, source_target_pairs={{0,4},{1,5},{2,6},{3,7},{4,0},{5,1},{6,2},{7,3},{8,12},{9,13},{10,... | collective-permute-start | bytes 270344 | tf_op jit(solution)/shard_map/ppermute | solution.py:89
  134.5 15.5 %collective-permute-start = (bf16[1024,256]{1,0:T(8,128)(2,1)}, bf16[1024,256]{1,0:T(8,128)(2,1)}, u32[]{:S(2)}, u32[]{:S(2)}) collective-permute-start(bf16[1024,256]{1,0:T(8,128)(2,1)} %get-tuple-element.55), channel_id=1, source_target_pairs={{0,4},{1,5},{2,6},{3,7},{4,0},{5,1},{6,2},{7,3},{8,12},{9,13},{10,... | collective-permute-start | bytes 1572872 | tf_op jit(solution)/shard_map/ppermute | solution.py:89
  136.0 14.6 %collective-permute-start.2 = (bf16[1024,256]{1,0:T(8,128)(2,1)}, bf16[1024,256]{1,0:T(8,128)(2,1)}, u32[]{:S(2)}, u32[]{:S(2)}) collective-permute-start(bf16[1024,256]{1,0:T(8,128)(2,1)} %get-tuple-element.56), channel_id=1, source_target_pairs={{0,12},{1,13},{2,14},{3,15},{4,8},{5,9},{6,10},{7,11},{8,4},{9,5},... | collective-permute-start | bytes 1572872 | tf_op jit(solution)/shard_map/ppermute | solution.py:89
  138.2 23.7 %collective-permute-start.1 = (bf16[1024,256]{1,0:T(8,128)(2,1)S(1)}, bf16[1024,256]{1,0:T(8,128)(2,1)}, u32[]{:S(2)}, u32[]{:S(2)}) collective-permute-start(bf16[1024,256]{1,0:T(8,128)(2,1)S(1)} %get-tuple-element.57), channel_id=1, source_target_pairs={{0,8},{1,9},{2,10},{3,11},{4,12},{5,13},{6,14},{7,15},{8,0},{9,1},... | collective-permute-start | bytes 1572872 | tf_op jit(solution)/shard_map/ppermute | solution.py:89
  140.3 42.7 %all-to-all-start.6 = ((bf16[16,96,256]{2,1,0:T(8,128)(2,1)}), bf16[16,96,256]{2,1,0:T(8,128)(2,1)S(1)}, u32[]{:S(2)}, u32[]{:S(2)}) async-start(bf16[16,96,256]{2,1,0:T(8,128)(2,1)} %broadcast_in_dim.8), calls=%async_computation.6 | async-start | bytes 1572864 | tf_op jit(solution)/shard_map/all_to_all | solution.py:79
  163.5 7.4 %collective-permute-start.3 = (bf16[256,256]{1,0:T(8,128)(2,1)S(1)}, bf16[256,256]{1,0:T(8,128)(2,1)S(1)}, u32[]{:S(2)}, u32[]{:S(2)}) collective-permute-start(bf16[256,256]{1,0:T(8,128)(2,1)S(1)} %get-tuple-element.61), channel_id=1, source_target_pairs={{0,1},{1,0},{2,3},{3,2},{4,5},{5,4},{6,7},{7,6},{8,9},{9,8},{10,11... | collective-permute-start | bytes 393224 | tf_op jit(solution)/shard_map/ppermute | solution.py:89
  166.0 9.2 %collective-permute-start.5 = (bf16[256,256]{1,0:T(8,128)(2,1)S(1)}, bf16[256,256]{1,0:T(8,128)(2,1)S(1)}, u32[]{:S(2)}, u32[]{:S(2)}) collective-permute-start(bf16[256,256]{1,0:T(8,128)(2,1)S(1)} %get-tuple-element.62), channel_id=1, source_target_pairs={{0,3},{1,2},{2,1},{3,0},{4,7},{5,6},{6,5},{7,4},{8,11},{9,10},{10,... | collective-permute-start | bytes 393224 | tf_op jit(solution)/shard_map/ppermute | solution.py:89
  168.6 12.4 %collective-permute-start.4 = (bf16[256,256]{1,0:T(8,128)(2,1)S(1)}, bf16[256,256]{1,0:T(8,128)(2,1)S(1)}, u32[]{:S(2)}, u32[]{:S(2)}) collective-permute-start(bf16[256,256]{1,0:T(8,128)(2,1)S(1)} %get-tuple-element.63), channel_id=1, source_target_pairs={{0,2},{1,3},{2,0},{3,1},{4,6},{5,7},{6,4},{7,5},{8,10},{9,11},{10,... | collective-permute-start | bytes 393224 | tf_op jit(solution)/shard_map/ppermute | solution.py:89
  (20 other events, 19.8 us)

commit v3 on v2

--- a/solution.py
+++ b/solution.py
@@ -108,26 +108,13 @@
 CHUNK = 256
 
 
-def sample_kernel(
-    which,
-    x_ref,
-    proj_ref,
-    grad_ref,
-    gain_ref,
-    gate_ref,
-    up_ref,
-    down_ref,
-    embed_ref,
-    scaled_ref,
-    gate_grad_ref,
-    up_grad_ref,
-    hidden_ref,
-    inter_grad_ref,
-    gain_grad_ref,
-    interact_grad_ref,
-):
+def sample_kernel(which, *refs):
+    (x_ref, proj_ref, grad_ref, gain_ref, gate_ref, up_ref, down_ref), refs = refs[:7], refs[7:]
+    before, refs = (refs[:6], refs[6:]) if which else (None, refs)
+    embed_ref, out_ref, *sums, scaled_ref, gate_grad_ref, up_grad_ref, hidden_ref = refs[:-2]
+    interact_grad_ref, gain_sum_ref = refs[-2:]
     inter_map = contract(x_ref[...], proj_ref[...], 0, 0).astype(BF)
-    gain_grad_ref[...] = jnp.zeros_like(gain_grad_ref)
+    gain_sum_ref[...] = before[5][...] if which else jnp.zeros_like(gain_sum_ref)
 
     def step(i, carry):
         rows = pl.ds(pl.multiple_of(i * CHUNK, CHUNK), CHUNK)
@@ -154,7 +141,7 @@
             scaled_grad += contract(gate_grad, gate_ref[:, cols], 1, 1)
             scaled_grad += contract(up_grad, up_ref[:, cols], 1, 1)
         times_normed = scaled_grad * normed
-        gain_grad_ref[...] += jnp.sum(times_normed.reshape(CHUNK // 8, 8, -1), axis=0)
+        gain_sum_ref[...] += jnp.sum(times_normed.reshape(CHUNK // 8, 8, -1), axis=0)
         mean = jnp.mean(times_normed * gain_ref[...], axis=-1, keepdims=True)
         interact_grad_ref[rows, :] = (
             inv_rms * (scaled_grad * gain_ref[...] - normed * mean)
@@ -163,76 +150,72 @@
 
     lax.fori_loop(0, x_ref.shape[0] // CHUNK, step, 0)
     inter_grad = contract(x_ref[...], interact_grad_ref[...], 0, 0).astype(BF)
-    inter_grad_ref[...] = inter_grad
     embed_ref[...] = (
         contract(interact_grad_ref[...], inter_map, 1, 1) + contract(proj_ref[...], inter_grad, 1, 1)
     ).astype(BF)
-
-
-def sample_pass(which, x, proj, out_grad, norm_gain, gate_weight, up_weight, down_weight):
+    out = jnp.dot(hidden_ref[...], down_ref[...], preferred_element_type=F32).astype(BF)
+    gate_part = contract(scaled_ref[...], gate_grad_ref[...], 0, 0)
+    up_part = contract(scaled_ref[...], up_grad_ref[...], 0, 0)
+    down_part = contract(hidden_ref[...], grad_ref[which], 0, 0)
+    proj_part = jnp.dot(x_ref[...], inter_grad, preferred_element_type=F32)
+    if not which:
+        out_ref[...] = out
+        for ref, part in zip(sums, (gate_part, up_part, down_part, proj_part)):
+            ref[...] = part
+        sums[4][...] = gain_sum_ref[...]
+        return
+    out_ref[0] = before[0][...]
+    out_ref[1] = out
+    (parts_ref,) = sums
+
+    def put(at, part):
+        piece = part.astype(BF)
+        size = piece.shape[0] // 16
+        for t in range(16):
+            parts_ref[t % 2, t // 2, at : at + size, :] = piece[t * size : (t + 1) * size]
+
+    for at, part in ((0, gate_part + before[1][...]), (32, up_part + before[2][...])):
+        put(at, part[:, :256])
+        put(at + 16, part[:, 256:])
+    put(64, down_part + before[3][...])
+    put(96, proj_part + before[4][...])
+    gain = jnp.sum(gain_sum_ref[...], axis=0, keepdims=True)
+    put(160, jnp.broadcast_to(gain, (256, gain.shape[1])))
+
+
+def sample_pass(which, x, proj, out_grad, norm_gain, gate_weight, up_weight, down_weight, before):
     rows, width = x.shape
     hidden = gate_weight.shape[1]
     shape = jax.ShapeDtypeStruct
+    if which:
+        after = [shape(out_grad.shape, BF), shape((2, 8, 176, width), BF)]
+    else:
+        after = [
+            shape((rows, width), BF),
+            shape((width, hidden), F32),
+            shape((width, hidden), F32),
+            shape((hidden, width), F32),
+            shape((rows, width), F32),
+            shape((8, width), F32),
+        ]
     return pl.pallas_call(
         functools.partial(sample_kernel, which),
-        out_shape=[
-            shape((rows, width), BF),
-            shape((rows, width), BF),
-            shape((rows, hidden), BF),
-            shape((rows, hidden), BF),
-            shape((rows, hidden), BF),
-            shape((width, width), BF),
-            shape((8, width), F32),
+        out_shape=[shape((rows, width), BF)] + after,
+        in_specs=[pl.BlockSpec(memory_space=pltpu.VMEM)] * (7 + len(before)),
+        out_specs=[pl.BlockSpec(memory_space=pltpu.VMEM)] * (1 + len(after)),
+        scratch_shapes=[
+            pltpu.VMEM((rows, width), BF),
+            pltpu.VMEM((rows, hidden), BF),
+            pltpu.VMEM((rows, hidden), BF),
+            pltpu.VMEM((rows, hidden), BF),
+            pltpu.VMEM((rows, width), BF),
+            pltpu.VMEM((8, width), F32),
         ],
-        in_specs=[pl.BlockSpec(memory_space=pltpu.VMEM)] * 7,
-        out_specs=[pl.BlockSpec(memory_space=pltpu.VMEM)] * 7,
-        scratch_shapes=[pltpu.VMEM((rows, width), BF)],
         cost_estimate=pl.CostEstimate(
-            flops=9000000000, bytes_accessed=8 * rows * width * 2, transcendentals=rows * hidden
+            flops=10000000000, bytes_accessed=8 * rows * width * 2, transcendentals=rows * hidden
         ),
-        compiler_params=pltpu.CompilerParams(vmem_limit_bytes=40 << 20),
         name="sample_pass",
-    )(x, proj, out_grad, norm_gain[None], gate_weight, up_weight, down_weight)
-
-
-def parts_kernel(*refs):
-    (x0, x1, grads, down, s0, g0, u0, h0, z0, n0, s1, g1, u1, h1, z1, n1, out_ref, parts_ref) = refs
-
-    def over(a0, b0, a1, b1):
-        return contract(a0[...], b0[...], 0, 0) + contract(a1[...], b1[...], 0, 0)
-
-    for at, part in ((0, over(s0, g0, s1, g1)), (32, over(s0, u0, s1, u1))):
-        part = part.astype(BF).reshape(16, 16, 512)
-        parts_ref[:, at : at + 16, :] = part[:, :, :256]
-        parts_ref[:, at + 16 : at + 32, :] = part[:, :, 256:]
-    part = over(h0, grads.at[0], h1, grads.at[1]).astype(BF)
-    parts_ref[:, 64:96, :] = part.reshape(16, 32, 256)
-    part = jnp.dot(x0[...], z0[...], preferred_element_type=F32) + jnp.dot(
-        x1[...], z1[...], preferred_element_type=F32
-    )
-    parts_ref[:, 96:160, :] = part.astype(BF).reshape(16, 64, 256)
-    part = jnp.sum(n0[...] + n1[...], axis=0, keepdims=True)
-    parts_ref[:, 160:176, :] = jnp.broadcast_to(part[None], (16, 16, 256)).astype(BF)
-    for s, hidden in enumerate((h0, h1)):
-        out_ref[s] = jnp.dot(hidden[...], down[...], preferred_element_type=F32).astype(BF)
-
-
-def parts_of(xs, out_grad, down_weight, passes):
-    saved = [v for p in passes for v in p[1:]]
-    return pl.pallas_call(
-        parts_kernel,
-        out_shape=[
-            jax.ShapeDtypeStruct(out_grad.shape, BF),
-            jax.ShapeDtypeStruct((16, 176, out_grad.shape[2]), BF),
-        ],
-        in_specs=[pl.BlockSpec(memory_space=pltpu.VMEM)] * (4 + len(saved)),
-        out_specs=[pl.BlockSpec(memory_space=pltpu.VMEM)] * 2,
-        cost_estimate=pl.CostEstimate(
-            flops=6000000000, bytes_accessed=16000000, transcendentals=0
-        ),
-        compiler_params=pltpu.CompilerParams(vmem_limit_bytes=40 << 20),
-        name="parts",
-    )(*xs, out_grad, down_weight, *saved)
+    )(x, proj, out_grad, norm_gain[None], gate_weight, up_weight, down_weight, *before)
 
 
 def per_device(
@@ -246,23 +229,36 @@
     all_feats = shards * feats
     proj = gathered(projection, "table", shards).reshape(all_feats, rank)
     ids = feature_ids.reshape(shards, own, feats, pool)
-    counts, xs, passes, backs = [], [], [], []
+    counts, backs, carried = [], [], ()
     for c in range(own):
         count, embeds = lookup(emb_table, ids[:, c])
         if c == 0:
             embeds, proj = lax.optimization_barrier((embeds, proj))
         x = exchange(embeds.reshape(shards, feats, width), "table")
         counts.append(count)
-        xs.append(x.reshape(all_feats, width))
-        passes.append(
-            sample_pass(c, xs[c], proj, out_grad, norm_gain, gate_weight, up_weight, down_weight)
+        embed_grad, *carried = sample_pass(
+            c,
+            x.reshape(all_feats, width),
+            proj,
+            out_grad,
+            norm_gain,
+            gate_weight,
+            up_weight,
+            down_weight,
+            carried,
         )
-        back = exchange(passes[c][0].reshape(shards, feats, width), "table")
+        back = exchange(embed_grad.reshape(shards, feats, width), "table")
         backs.append(back.reshape(-1, width))
 
-    block_out, parts = parts_of(xs, out_grad, down_weight, passes)
+    block_out, parts = carried
+    core = lax.axis_index("table") % 2
+    take = lambda i: lax.dynamic_index_in_dim(parts, i, 0, keepdims=False)
+    came = lax.ppermute(take(1 - core), "table", [(t, t ^ 1) for t in range(shards)])
+    parts = (take(core).astype(F32) + came.astype(F32)).astype(BF)
     parts, backs[-1] = lax.optimization_barrier((parts, backs[-1]))
-    parts = exchange(parts, "table")
+    parts = lax.all_to_all(
+        parts, "table", 0, 0, axis_index_groups=[list(range(c, shards, 2)) for c in (0, 1)]
+    )
     parts = jnp.sum(parts.astype(F32), axis=0).astype(BF)
     parts = sum_all(parts, "z")
     parts = sum_all(parts, "y")

time: 188 us -> 180 us (0.957)
  the two profiles are of different devices: /device:TPU:38 before, /device:TPU:34 now
where the time goes in v3:
time: 180 us; the launch traced here: 178 us
  starting transfers between devices  64 us (36%)
  waiting for transfers between devices  43.2 us (24%)
  Pallas kernels  38.2 us (21%)
  matrix products  15 us (8%)
  local copies, waits for them, and re-layouts  10.6 us (6%)
  other arithmetic  6.65 us (4%)
    all_to_all x6, starting transfers between devices, exchange(): return lax.all_to_all(values, axis, 0, 0)  34.3 us
    ppermute x12, waiting for transfers between devices, swap(): return lax.ppermute(values, 'batch', pairs)  28.5 us
    ppermute x12, starting transfers between devices, swap(): return lax.ppermute(values, 'batch', pairs)  23.2 us
    pallas_call x2, Pallas kernels, sample_pass(): pl.pallas_call(functools.partial(sample_kernel, which), out_shape=[shape(...  20.4 us
    pallas_call x2, Pallas kernels, lookup(): pl.pallas_call(lookup_kernel, grid=(steps,), in_specs=[pl.BlockSpec((rows...  17.8 us
    dot_general x2, matrix products, contract(): lax.dot_general(left, right, (((left_dim,), (right_dim,)), ((), ())), pre...  15 us
    all_to_all x6, waiting for transfers between devices, exchange(): return lax.all_to_all(values, axis, 0, 0)  10.6 us
    all_to_all x1, starting transfers between devices, per_device(): lax.all_to_all(parts, 'table', 0, 0, axis_index_groups=[list(range(c, sha...  6.35 us
  transfers between devices with their start and end apart: 20, of which 12 were waited for; matrix products, arithmetic and copies ran while one was open for 15% of the time, Pallas kernels for 15%

profile of v3, /device:TPU:34, one launch (start us, length us, event | category | flops | bytes accessed | tf_op | source)
XLA Modules:
  0.0 178.5 jit_solution(1183173529503512398)
XLA Ops:
  2.2 5.8 %all-to-all-start.1 = ((bf16[16,64,256]{2,1,0:T(8,128)(2,1)}), bf16[16,64,256]{2,1,0:T(8,128)(2,1)S(1)}, u32[]{:S(2)}, u32[]{:S(2)}) async-start(bf16[16,64,256]{2,1,0:T(8,128)(2,1)} %broadcast_in_dim.6), calls=%async_computation.1 | async-start | bytes 1048576 | tf_op jit(solution)/shard_map/all_to_all | solution.py:79
  10.3 8.9 %lookup.3 = (bf16[1024,4096]{1,0:T(8,128)(2,1)}, bf16[1024,256]{1,0:T(8,128)(2,1)}) custom-call(s32[64,128]{1,0:T(8,128)} %get-tuple-element.55.high_ref, s32[64,128]{1,0:T(8,128)} %get-tuple-element.54.low_ref, bf16[4096,256]{1,0:T(8,128)(2,1)} %table_ref.3), custom_call_target="tpu_custom_call" | custom-call | flops 4294967296 | bytes 12582912 | tf_op jit(solution)/shard_map/lookup/pallas_call | solution.py:53
  19.1 5.7 %all-to-all-start.2 = ((bf16[16,64,256]{2,1,0:T(8,128)(2,1)}), bf16[16,64,256]{2,1,0:T(8,128)(2,1)S(1)}, u32[]{:S(2)}, u32[]{:S(2)}) async-start(bf16[16,64,256]{2,1,0:T(8,128)(2,1)} %bitcast.89), calls=%async_computation.2 | async-start | bytes 1048576 | tf_op jit(solution)/shard_map/all_to_all | solution.py:79
  24.9 8.9 %lookup.2 = (bf16[1024,4096]{1,0:T(8,128)(2,1)}, bf16[1024,256]{1,0:T(8,128)(2,1)}) custom-call(s32[64,128]{1,0:T(8,128)} %get-tuple-element.58.high_ref, s32[64,128]{1,0:T(8,128)} %get-tuple-element.59.low_ref, bf16[4096,256]{1,0:T(8,128)(2,1)} %table_ref.3), custom_call_target="tpu_custom_call" | custom-call | flops 4294967296 | bytes 12582912 | tf_op jit(solution)/shard_map/lookup/pallas_call | solution.py:53
  33.8 5.7 %all-to-all-start = ((bf16[16,64,256]{2,1,0:T(8,128)(2,1)}), bf16[16,64,256]{2,1,0:T(8,128)(2,1)S(1)}, u32[]{:S(2)}, u32[]{:S(2)}) async-start(bf16[16,64,256]{2,1,0:T(8,128)(2,1)} %bitcast.86), calls=%async_computation | async-start | bytes 1048576 | tf_op jit(solution)/shard_map/all_to_all | solution.py:79
  39.5 9.6 %sample_pass.2 = (bf16[1024,256]{1,0:T(8,128)(2,1)}, bf16[1024,256]{1,0:T(8,128)(2,1)}, f32[256,512]{1,0:T(8,128)}, f32[256,512]{1,0:T(8,128)}, f32[512,256]{1,0...) custom-call(bf16[1024,256]{1,0:T(8,128)(2,1)} %bitcast.85, bf16[1024,256]{1,0:T(8,128)(2,1)} %bitcast.82, ...), custom_call_target="tpu_custom_call" | custom-call | flops 10000000000 | bytes 4194304 | tf_op jit(solution)/shard_map/sample_pass/pallas_call | solution.py:201
  49.9 10.9 %sample_pass.3 = (bf16[1024,256]{1,0:T(8,128)(2,1)}, bf16[2,1024,256]{2,1,0:T(8,128)(2,1)}, bf16[2,8,176,256]{3,2,1,0:T(8,128)(2,1)}) custom-call(bf16[1024,256]{1,0:T(8,128)(2,1)} %bitcast.87, bf16[1024,256]{1,0:T(8,128)(2,1)} %bitcast.83, bf16[2,1024,256]{2,1,0:T(8,128)(2,1)} %refs_2_.3, f32[1,256]{1,0:T(1,128)} %bitcast.95, bf16[256,512]{1,0:T(8,128)(2,1)} %refs_4_.3, ...), custom_call_target="tpu_custom_call" | custom-call | flops 10000000000 | bytes 4194304 | tf_op jit(solution)/shard_map/sample_pass/pallas_call | solution.py:201
  60.8 5.7 %all-to-all-start.4 = ((bf16[16,64,256]{2,1,0:T(8,128)(2,1)}), bf16[16,64,256]{2,1,0:T(8,128)(2,1)S(1)}, u32[]{:S(2)}, u32[]{:S(2)}) async-start(bf16[16,64,256]{2,1,0:T(8,128)(2,1)} %bitcast.84), calls=%async_computation.4 | async-start | bytes 1048576 | tf_op jit(solution)/shard_map/all_to_all | solution.py:79
  66.5 8.1 %all-to-all-done.4 = bf16[16,64,256]{2,1,0:T(8,128)(2,1)S(1)} async-done(((bf16[16,64,256]{2,1,0:T(8,128)(2,1)}), bf16[16,64,256]{2,1,0:T(8,128)(2,1)S(1)}, u32[]{:S(2)}, u32[]{:S(2)}) %all-to-all-start.4) | async-done | bytes 524320 | tf_op jit(solution)/shard_map/all_to_all | solution.py:79
  74.6 6.4 %all-to-all-start.3 = ((bf16[16,64,256]{2,1,0:T(8,128)(2,1)}), bf16[16,64,256]{2,1,0:T(8,128)(2,1)S(1)}, u32[]{:S(2)}, u32[]{:S(2)}) async-start(bf16[16,64,256]{2,1,0:T(8,128)(2,1)} %bitcast.9), calls=%async_computation.3 | async-start | bytes 1048576 | tf_op jit(solution)/shard_map/all_to_all | solution.py:79
  86.6 2.5 %all-to-all-done.3 = bf16[16,64,256]{2,1,0:T(8,128)(2,1)S(1)} async-done(((bf16[16,64,256]{2,1,0:T(8,128)(2,1)}), bf16[16,64,256]{2,1,0:T(8,128)(2,1)S(1)}, u32[]{:S(2)}, u32[]{:S(2)}) %all-to-all-start.3) | async-done | bytes 524320 | tf_op jit(solution)/shard_map/all_to_all | solution.py:79
  89.1 6.3 %all-to-all-start.5 = ((bf16[8,176,256]{2,1,0:T(8,128)(2,1)}), bf16[8,176,256]{2,1,0:T(8,128)(2,1)S(1)}, u32[]{:S(2)}, u32[]{:S(2)}) async-start(bf16[8,176,256]{2,1,0:T(8,128)(2,1)} %fusion.1), calls=%async_computation.5 | async-start | bytes 1441792 | tf_op jit(solution)/shard_map/all_to_all | solution.py:259
  95.4 7.8 %fusion.14 = f32[4096,256]{1,0:T(8,128)} fusion(bf16[1024,4096]{1,0:T(8,128)(2,1)} %get-tuple-element.36, bf16[1024,256]{1,0:T(8,128)(2,1)S(1)} %bitcast.81), kind=kOutput, calls=%fused_computation.48 | convolution fusion | flops 2147483648 | bytes 13107200 | tf_op jit(solution)/shard_map/dot_general | solution.py:17
  105.3 5.5 %collective-permute-start.9 = (bf16[176,256]{1,0:T(8,128)(2,1)S(1)}, bf16[176,256]{1,0:T(8,128)(2,1)S(1)}, u32[]{:S(2)}, u32[]{:S(2)}) collective-permute-start(bf16[176,256]{1,0:T(8,128)(2,1)S(1)} %reduce_sum.12), channel_id=1, source_target_pairs={{0,3},{1,2},{2,1},{3,0},{4,7},{5,6},{6,5},{7,4},{8,11},{9,10},{10,... | collective-permute-start | bytes 270344 | tf_op jit(solution)/shard_map/ppermute | solution.py:89
  113.3 7.2 %fusion = bf16[4096,256]{1,0:T(8,128)(2,1)S(1)} fusion(f32[4096,256]{1,0:T(8,128)} %fusion.14, bf16[1024,4096]{1,0:T(8,128)(2,1)} %get-tuple-element.38, bf16[1024,256]{1,0:T(8,128)(2,1)S(1)} %bitcast.80), kind=kOutput, calls=%fused_computation.1 | convolution fusion | flops 2149580800 | bytes 15204352 | tf_op jit(solution)/shard_map/dot_general | solution.py:17
  122.1 3.1 %collective-permute-start.12 = (bf16[176,256]{1,0:T(8,128)(2,1)S(1)}, bf16[176,256]{1,0:T(8,128)(2,1)S(1)}, u32[]{:S(2)}, u32[]{:S(2)}) collective-permute-start(bf16[176,256]{1,0:T(8,128)(2,1)S(1)} %add_convert_fusion.1), channel_id=1, source_target_pairs={{0,12},{1,13},{2,14},{3,15},{4,8},{5,9},{6,10},{7,11},{8,4},{9,5},... | collective-permute-start | bytes 270344 | tf_op jit(solution)/shard_map/ppermute | solution.py:89
  128.9 2.2 %collective-permute-start.3 = (bf16[1024,256]{1,0:T(8,128)(2,1)}, bf16[1024,256]{1,0:T(8,128)(2,1)}, u32[]{:S(2)}, u32[]{:S(2)}) collective-permute-start(bf16[1024,256]{1,0:T(8,128)(2,1)} %get-tuple-element.44), channel_id=1, source_target_pairs={{0,12},{1,13},{2,14},{3,15},{4,8},{5,9},{6,10},{7,11},{8,4},{9,5},... | collective-permute-start | bytes 1572872 | tf_op jit(solution)/shard_map/ppermute | solution.py:89
  133.0 4.9 %all-to-all-start.6 = ((bf16[16,96,256]{2,1,0:T(8,128)(2,1)}), bf16[16,96,256]{2,1,0:T(8,128)(2,1)S(1)}, u32[]{:S(2)}, u32[]{:S(2)}) async-start(bf16[16,96,256]{2,1,0:T(8,128)(2,1)} %broadcast_in_dim.8), calls=%async_computation.6 | async-start | bytes 1572864 | tf_op jit(solution)/shard_map/all_to_all | solution.py:79
  138.0 5.0 %collective-permute-done.1 = bf16[1024,256]{1,0:T(8,128)(2,1)} collective-permute-done((bf16[1024,256]{1,0:T(8,128)(2,1)}, bf16[1024,256]{1,0:T(8,128)(2,1)}, u32[]{:S(2)}, u32[]{:S(2)}) %collective-permute-start.1) | collective-permute-done | bytes 524320 | tf_op jit(solution)/shard_map/ppermute | solution.py:89
  143.0 9.9 %collective-permute-done.3 = bf16[1024,256]{1,0:T(8,128)(2,1)} collective-permute-done((bf16[1024,256]{1,0:T(8,128)(2,1)}, bf16[1024,256]{1,0:T(8,128)(2,1)}, u32[]{:S(2)}, u32[]{:S(2)}) %collective-permute-start.3) | collective-permute-done | bytes 524320 | tf_op jit(solution)/shard_map/ppermute | solution.py:89
  152.9 2.5 %collective-permute-done.2 = bf16[1024,256]{1,0:T(8,128)(2,1)} collective-permute-done((bf16[1024,256]{1,0:T(8,128)(2,1)S(1)}, bf16[1024,256]{1,0:T(8,128)(2,1)}, u32[]{:S(2)}, u32[]{:S(2)}) %collective-permute-start.2) | collective-permute-done | bytes 524320 | tf_op jit(solution)/shard_map/ppermute | solution.py:89
  157.8 2.7 %collective-permute-start.6 = (bf16[256,256]{1,0:T(8,128)(2,1)S(1)}, bf16[256,256]{1,0:T(8,128)(2,1)S(1)}, u32[]{:S(2)}, u32[]{:S(2)}) collective-permute-start(bf16[256,256]{1,0:T(8,128)(2,1)S(1)} %get-tuple-element.50), channel_id=1, source_target_pairs={{0,3},{1,2},{2,1},{3,0},{4,7},{5,6},{6,5},{7,4},{8,11},{9,10},{10,... | collective-permute-start | bytes 393224 | tf_op jit(solution)/shard_map/ppermute | solution.py:89
  160.5 3.1 %collective-permute-start.5 = (bf16[256,256]{1,0:T(8,128)(2,1)S(1)}, bf16[256,256]{1,0:T(8,128)(2,1)S(1)}, u32[]{:S(2)}, u32[]{:S(2)}) collective-permute-start(bf16[256,256]{1,0:T(8,128)(2,1)S(1)} %get-tuple-element.51), channel_id=1, source_target_pairs={{0,2},{1,3},{2,0},{3,1},{4,6},{5,7},{6,4},{7,5},{8,10},{9,11},{10,... | collective-permute-start | bytes 393224 | tf_op jit(solution)/shard_map/ppermute | solution.py:89
  165.4 5.6 %collective-permute-done.6 = bf16[256,256]{1,0:T(8,128)(2,1)S(1)} collective-permute-done((bf16[256,256]{1,0:T(8,128)(2,1)S(1)}, bf16[256,256]{1,0:T(8,128)(2,1)S(1)}, u32[]{:S(2)}, u32[]{:S(2)}) %collective-permute-start.6) | collective-permute-done | bytes 131104 | tf_op jit(solution)/shard_map/ppermute | solution.py:89
  (58 shorter events, 33.7 us)
Async XLA Ops:
  2.2 16.9 %all-to-all-start.1 = ((bf16[16,64,256]{2,1,0:T(8,128)(2,1)}), bf16[16,64,256]{2,1,0:T(8,128)(2,1)S(1)}, u32[]{:S(2)}, u32[]{:S(2)}) async-start(bf16[16,64,256]{2,1,0:T(8,128)(2,1)} %broadcast_in_dim.6), calls=%async_computation.1 | async-start | bytes 1048576 | tf_op jit(solution)/shard_map/all_to_all | solution.py:79
  19.1 14.6 %copy-start = (bf16[16,64,256]{2,1,0:T(8,128)(2,1)}, bf16[16,64,256]{2,1,0:T(8,128)(2,1)S(1)}, u32[]{:S(2)}) copy-start(bf16[16,64,256]{2,1,0:T(8,128)(2,1)S(1)} %all-to-all-done.1) | copy-start | bytes 1572868
  19.1 14.6 %all-to-all-start.2 = ((bf16[16,64,256]{2,1,0:T(8,128)(2,1)}), bf16[16,64,256]{2,1,0:T(8,128)(2,1)S(1)}, u32[]{:S(2)}, u32[]{:S(2)}) async-start(bf16[16,64,256]{2,1,0:T(8,128)(2,1)} %bitcast.89), calls=%async_computation.2 | async-start | bytes 1048576 | tf_op jit(solution)/shard_map/all_to_all | solution.py:79
  33.8 5.7 %copy-start.1 = (bf16[16,64,256]{2,1,0:T(8,128)(2,1)}, bf16[16,64,256]{2,1,0:T(8,128)(2,1)S(1)}, u32[]{:S(2)}) copy-start(bf16[16,64,256]{2,1,0:T(8,128)(2,1)S(1)} %all-to-all-done.2) | copy-start | bytes 1572868
  33.8 15.3 %all-to-all-start = ((bf16[16,64,256]{2,1,0:T(8,128)(2,1)}), bf16[16,64,256]{2,1,0:T(8,128)(2,1)S(1)}, u32[]{:S(2)}, u32[]{:S(2)}) async-start(bf16[16,64,256]{2,1,0:T(8,128)(2,1)} %bitcast.86), calls=%async_computation | async-start | bytes 1048576 | tf_op jit(solution)/shard_map/all_to_all | solution.py:79
  49.1 0.8 copy-start.2
  60.8 13.8 %all-to-all-start.4 = ((bf16[16,64,256]{2,1,0:T(8,128)(2,1)}), bf16[16,64,256]{2,1,0:T(8,128)(2,1)S(1)}, u32[]{:S(2)}, u32[]{:S(2)}) async-start(bf16[16,64,256]{2,1,0:T(8,128)(2,1)} %bitcast.84), calls=%async_computation.4 | async-start | bytes 1048576 | tf_op jit(solution)/shard_map/all_to_all | solution.py:79
  74.6 14.5 %all-to-all-start.3 = ((bf16[16,64,256]{2,1,0:T(8,128)(2,1)}), bf16[16,64,256]{2,1,0:T(8,128)(2,1)S(1)}, u32[]{:S(2)}, u32[]{:S(2)}) async-start(bf16[16,64,256]{2,1,0:T(8,128)(2,1)} %bitcast.9), calls=%async_computation.3 | async-start | bytes 1048576 | tf_op jit(solution)/shard_map/all_to_all | solution.py:79
  82.2 2.3 %collective-permute-start = (bf16[8,176,256]{2,1,0:T(8,128)(2,1)S(1)}, bf16[8,176,256]{2,1,0:T(8,128)(2,1)S(1)}, u32[]{:S(2)}, u32[]{:S(2)}) collective-permute-start(bf16[8,176,256]{2,1,0:T(8,128)(2,1)S(1)} %dynamic-slice_bitcast_fusion), channel_id=1, source_target_pairs={{0,16},{16,0},{32,48},{48,32},{64,80},{80,64},{96,112},{112,96},{1... | collective-permute-start | bytes 2162696 | tf_op jit(solution)/shard_map/ppermute | solution.py:256
  89.1 16.2 %all-to-all-start.5 = ((bf16[8,176,256]{2,1,0:T(8,128)(2,1)}), bf16[8,176,256]{2,1,0:T(8,128)(2,1)S(1)}, u32[]{:S(2)}, u32[]{:S(2)}) async-start(bf16[8,176,256]{2,1,0:T(8,128)(2,1)} %fusion.1), calls=%async_computation.5 | async-start | bytes 1441792 | tf_op jit(solution)/shard_map/all_to_all | solution.py:259
  105.3 15.2 %collective-permute-start.9 = (bf16[176,256]{1,0:T(8,128)(2,1)S(1)}, bf16[176,256]{1,0:T(8,128)(2,1)S(1)}, u32[]{:S(2)}, u32[]{:S(2)}) collective-permute-start(bf16[176,256]{1,0:T(8,128)(2,1)S(1)} %reduce_sum.12), channel_id=1, source_target_pairs={{0,3},{1,2},{2,1},{3,0},{4,7},{5,6},{6,5},{7,4},{8,11},{9,10},{10,... | collective-permute-start | bytes 270344 | tf_op jit(solution)/shard_map/ppermute | solution.py:89
  110.8 11.2 %collective-permute-start.8 = (bf16[176,256]{1,0:T(8,128)(2,1)S(1)}, bf16[176,256]{1,0:T(8,128)(2,1)S(1)}, u32[]{:S(2)}, u32[]{:S(2)}) collective-permute-start(bf16[176,256]{1,0:T(8,128)(2,1)S(1)} %reduce_sum.12), channel_id=1, source_target_pairs={{0,2},{1,3},{2,0},{3,1},{4,6},{5,7},{6,4},{7,5},{8,10},{9,11},{10,... | collective-permute-start | bytes 270344 | tf_op jit(solution)/shard_map/ppermute | solution.py:89
  112.3 9.8 %collective-permute-start.7 = (bf16[176,256]{1,0:T(8,128)(2,1)S(1)}, bf16[176,256]{1,0:T(8,128)(2,1)S(1)}, u32[]{:S(2)}, u32[]{:S(2)}) collective-permute-start(bf16[176,256]{1,0:T(8,128)(2,1)S(1)} %reduce_sum.12), channel_id=1, source_target_pairs={{0,1},{1,0},{2,3},{3,2},{4,5},{5,4},{6,7},{7,6},{8,9},{9,8},{10,11... | collective-permute-start | bytes 270344 | tf_op jit(solution)/shard_map/ppermute | solution.py:89
  122.1 9.0 %collective-permute-start.12 = (bf16[176,256]{1,0:T(8,128)(2,1)S(1)}, bf16[176,256]{1,0:T(8,128)(2,1)S(1)}, u32[]{:S(2)}, u32[]{:S(2)}) collective-permute-start(bf16[176,256]{1,0:T(8,128)(2,1)S(1)} %add_convert_fusion.1), channel_id=1, source_target_pairs={{0,12},{1,13},{2,14},{3,15},{4,8},{5,9},{6,10},{7,11},{8,4},{9,5},... | collective-permute-start | bytes 270344 | tf_op jit(solution)/shard_map/ppermute | solution.py:89
  125.2 6.8 %collective-permute-start.11 = (bf16[176,256]{1,0:T(8,128)(2,1)S(1)}, bf16[176,256]{1,0:T(8,128)(2,1)S(1)}, u32[]{:S(2)}, u32[]{:S(2)}) collective-permute-start(bf16[176,256]{1,0:T(8,128)(2,1)S(1)} %add_convert_fusion.1), channel_id=1, source_target_pairs={{0,8},{1,9},{2,10},{3,11},{4,12},{5,13},{6,14},{7,15},{8,0},{9,1},... | collective-permute-start | bytes 270344 | tf_op jit(solution)/shard_map/ppermute | solution.py:89
  125.8 6.2 %collective-permute-start.10 = (bf16[176,256]{1,0:T(8,128)(2,1)S(1)}, bf16[176,256]{1,0:T(8,128)(2,1)S(1)}, u32[]{:S(2)}, u32[]{:S(2)}) collective-permute-start(bf16[176,256]{1,0:T(8,128)(2,1)S(1)} %add_convert_fusion.1), channel_id=1, source_target_pairs={{0,4},{1,5},{2,6},{3,7},{4,0},{5,1},{6,2},{7,3},{8,12},{9,13},{10,... | collective-permute-start | bytes 270344 | tf_op jit(solution)/shard_map/ppermute | solution.py:89
  127.3 15.7 %collective-permute-start.1 = (bf16[1024,256]{1,0:T(8,128)(2,1)}, bf16[1024,256]{1,0:T(8,128)(2,1)}, u32[]{:S(2)}, u32[]{:S(2)}) collective-permute-start(bf16[1024,256]{1,0:T(8,128)(2,1)} %get-tuple-element.43), channel_id=1, source_target_pairs={{0,4},{1,5},{2,6},{3,7},{4,0},{5,1},{6,2},{7,3},{8,12},{9,13},{10,... | collective-permute-start | bytes 1572872 | tf_op jit(solution)/shard_map/ppermute | solution.py:89
  128.9 23.9 %collective-permute-start.3 = (bf16[1024,256]{1,0:T(8,128)(2,1)}, bf16[1024,256]{1,0:T(8,128)(2,1)}, u32[]{:S(2)}, u32[]{:S(2)}) collective-permute-start(bf16[1024,256]{1,0:T(8,128)(2,1)} %get-tuple-element.44), channel_id=1, source_target_pairs={{0,12},{1,13},{2,14},{3,15},{4,8},{5,9},{6,10},{7,11},{8,4},{9,5},... | collective-permute-start | bytes 1572872 | tf_op jit(solution)/shard_map/ppermute | solution.py:89
  131.1 24.3 %collective-permute-start.2 = (bf16[1024,256]{1,0:T(8,128)(2,1)S(1)}, bf16[1024,256]{1,0:T(8,128)(2,1)}, u32[]{:S(2)}, u32[]{:S(2)}) collective-permute-start(bf16[1024,256]{1,0:T(8,128)(2,1)S(1)} %get-tuple-element.45), channel_id=1, source_target_pairs={{0,8},{1,9},{2,10},{3,11},{4,12},{5,13},{6,14},{7,15},{8,0},{9,1},... | collective-permute-start | bytes 1572872 | tf_op jit(solution)/shard_map/ppermute | solution.py:89
  133.0 42.0 %all-to-all-start.6 = ((bf16[16,96,256]{2,1,0:T(8,128)(2,1)}), bf16[16,96,256]{2,1,0:T(8,128)(2,1)S(1)}, u32[]{:S(2)}, u32[]{:S(2)}) async-start(bf16[16,96,256]{2,1,0:T(8,128)(2,1)} %broadcast_in_dim.8), calls=%async_computation.6 | async-start | bytes 1572864 | tf_op jit(solution)/shard_map/all_to_all | solution.py:79
  157.1 8.3 %collective-permute-start.4 = (bf16[256,256]{1,0:T(8,128)(2,1)S(1)}, bf16[256,256]{1,0:T(8,128)(2,1)S(1)}, u32[]{:S(2)}, u32[]{:S(2)}) collective-permute-start(bf16[256,256]{1,0:T(8,128)(2,1)S(1)} %get-tuple-element.49), channel_id=1, source_target_pairs={{0,1},{1,0},{2,3},{3,2},{4,5},{5,4},{6,7},{7,6},{8,9},{9,8},{10,11... | collective-permute-start | bytes 393224 | tf_op jit(solution)/shard_map/ppermute | solution.py:89
  157.8 13.2 %collective-permute-start.6 = (bf16[256,256]{1,0:T(8,128)(2,1)S(1)}, bf16[256,256]{1,0:T(8,128)(2,1)S(1)}, u32[]{:S(2)}, u32[]{:S(2)}) collective-permute-start(bf16[256,256]{1,0:T(8,128)(2,1)S(1)} %get-tuple-element.50), channel_id=1, source_target_pairs={{0,3},{1,2},{2,1},{3,0},{4,7},{5,6},{6,5},{7,4},{8,11},{9,10},{10,... | collective-permute-start | bytes 393224 | tf_op jit(solution)/shard_map/ppermute | solution.py:89
  160.5 12.5 %collective-permute-start.5 = (bf16[256,256]{1,0:T(8,128)(2,1)S(1)}, bf16[256,256]{1,0:T(8,128)(2,1)S(1)}, u32[]{:S(2)}, u32[]{:S(2)}) collective-permute-start(bf16[256,256]{1,0:T(8,128)(2,1)S(1)} %get-tuple-element.51), channel_id=1, source_target_pairs={{0,2},{1,3},{2,0},{3,1},{4,6},{5,7},{6,4},{7,5},{8,10},{9,11},{10,... | collective-permute-start | bytes 393224 | tf_op jit(solution)/shard_map/ppermute | solution.py:89

commit v4 on v3

--- a/solution.py
+++ b/solution.py
@@ -11,6 +11,7 @@
 BF = jnp.bfloat16
 F32 = jnp.float32
 STEPS = {"y": 4, "z": 1}
+CHIPS = [list(range(c, 16, 2)) for c in (0, 1)]
 
 
 def contract(left, right, left_dim, right_dim):
@@ -19,8 +20,9 @@
     )
 
 
-def lookup_kernel(high_ref, low_ref, table_ref, counts_ref, embeds_ref):
-    groups = high_ref.shape[0]
+def lookup_kernel(high_ref, low_ref, table_ref, counts_ref, embeds_ref, held_ref, sems):
+    segments = sems.shape[0]
+    groups = high_ref.shape[0] // segments
     slot = lax.broadcasted_iota(jnp.int32, (256, 128), 0)
 
     def step(g, carry):
@@ -28,15 +30,23 @@
         right = jnp.where(slot == low_ref[pl.ds(g, 1), :], 1.0, 0.0).astype(BF)
         both = contract(left, right, 1, 1).astype(BF)
         for h in range(16):
-            counts_ref[pl.ds(pl.multiple_of(g * 16, 16), 16), h * 256 : (h + 1) * 256] = both[
+            held_ref[pl.ds(pl.multiple_of(g * 16, 16), 16), h * 256 : (h + 1) * 256] = both[
                 h * 16 : (h + 1) * 16
             ]
         return carry
 
-    lax.fori_loop(0, groups, step, 0, unroll=8)
+    def copy(i):
+        rows = pl.ds(i * groups * 16, groups * 16)
+        return pltpu.make_async_copy(held_ref.at[rows], counts_ref.at[rows], sems.at[i])
+
+    for i in range(segments):
+        lax.fori_loop(i * groups, (i + 1) * groups, step, 0, unroll=8)
+        copy(i).start()
     embeds_ref[...] = jnp.dot(
-        counts_ref[...], table_ref[...], preferred_element_type=F32
+        held_ref[...], table_ref[...], preferred_element_type=F32
     ).astype(BF)
+    for i in range(segments):
+        copy(i).wait()
 
 
 def lookup(emb_table, feature_ids):
@@ -49,22 +59,20 @@
     )
     high = (lanes // 256) * 16 + lax.broadcasted_iota(jnp.int32, lanes.shape, 1) % 16
     low = lanes % 256
-    steps = 1
     return pl.pallas_call(
         lookup_kernel,
-        grid=(steps,),
-        in_specs=[
-            pl.BlockSpec((rows // 16 // steps, 128), lambda i: (i, 0)),
-            pl.BlockSpec((rows // 16 // steps, 128), lambda i: (i, 0)),
-            pl.BlockSpec(emb_table.shape, lambda i: (0, 0)),
-        ],
+        in_specs=[pl.BlockSpec(memory_space=pltpu.VMEM)] * 3,
         out_specs=[
-            pl.BlockSpec((rows // steps, emb_table.shape[0]), lambda i: (i, 0)),
-            pl.BlockSpec((rows // steps, emb_table.shape[1]), lambda i: (i, 0)),
+            pl.BlockSpec(memory_space=pl.ANY),
+            pl.BlockSpec(memory_space=pltpu.VMEM),
         ],
         out_shape=[
             jax.ShapeDtypeStruct((rows, emb_table.shape[0]), BF),
             jax.ShapeDtypeStruct((rows, emb_table.shape[1]), BF),
+        ],
+        scratch_shapes=[
+            pltpu.VMEM((rows, emb_table.shape[0]), BF),
+            pltpu.SemaphoreType.DMA((SEGMENTS,)),
         ],
         cost_estimate=pl.CostEstimate(
             flops=4 * rows * emb_table.shape[0] * emb_table.shape[1],
@@ -106,6 +114,7 @@
 
 
 CHUNK = 256
+SEGMENTS = 4
 
 
 def sample_kernel(which, *refs):
@@ -218,6 +227,32 @@
     )(x, proj, out_grad, norm_gain[None], gate_weight, up_weight, down_weight, *before)
 
 
+def finish_kernel(core_ref, mine_ref, other_ref, gate_ref, up_ref, down_ref):
+    first = core_ref[0] == 0
+    for t in range(16):
+        own, swapped = mine_ref[t // 2], other_ref[t // 2]
+        piece = jnp.where(first == (t % 2 == 0), own, swapped).astype(F32)
+        rows = slice(t * 16, (t + 1) * 16)
+        gate_ref[rows, :256], gate_ref[rows, 256:] = piece[:16], piece[16:32]
+        up_ref[rows, :256], up_ref[rows, 256:] = piece[32:48], piece[48:64]
+        down_ref[t * 32 : (t + 1) * 32, :] = piece[64:96]
+
+
+def finish(core, mine, other, gate_shape, down_shape):
+    return pl.pallas_call(
+        finish_kernel,
+        in_specs=[pl.BlockSpec(memory_space=pltpu.SMEM)]
+        + [pl.BlockSpec(memory_space=pltpu.VMEM)] * 2,
+        out_specs=[pl.BlockSpec(memory_space=pltpu.VMEM)] * 3,
+        out_shape=[
+            jax.ShapeDtypeStruct(gate_shape, F32),
+            jax.ShapeDtypeStruct(gate_shape, F32),
+            jax.ShapeDtypeStruct(down_shape, F32),
+        ],
+        name="finish",
+    )(core[None], mine, other)
+
+
 def per_device(
     emb_table, feature_ids, projection, norm_gain, gate_weight, up_weight, down_weight, out_grad
 ):
@@ -256,28 +291,21 @@
     came = lax.ppermute(take(1 - core), "table", [(t, t ^ 1) for t in range(shards)])
     parts = (take(core).astype(F32) + came.astype(F32)).astype(BF)
     parts, backs[-1] = lax.optimization_barrier((parts, backs[-1]))
-    parts = lax.all_to_all(
-        parts, "table", 0, 0, axis_index_groups=[list(range(c, shards, 2)) for c in (0, 1)]
-    )
+    parts = lax.all_to_all(parts, "table", 0, 0, axis_index_groups=CHIPS)
     parts = jnp.sum(parts.astype(F32), axis=0).astype(BF)
     parts = sum_all(parts, "z")
     parts = sum_all(parts, "y")
     projection_grad = parts[96:160].astype(F32)
     gain_grad = parts[160].astype(F32)
-    weights = gathered(parts[:96], "table", shards)
-    weights = weights.astype(F32)
-
-    def joined(piece):
-        return (
-            piece.reshape(shards, 2, rank // shards, hidden_width // 2)
-            .transpose(0, 2, 1, 3)
-            .reshape(rank, hidden_width)
-        )
-
-    hidden_width = gate_weight.shape[1]
-    gate_grad = joined(weights[:, :32])
-    up_grad = joined(weights[:, 32:64])
-    down_grad = weights[:, 64:96].reshape(hidden_width, width)
+    mine = lax.all_to_all(
+        jnp.broadcast_to(parts[:96][None], (8, 96, width)),
+        "table",
+        0,
+        0,
+        axis_index_groups=CHIPS,
+    )
+    other = lax.ppermute(mine, "table", [(t, t ^ 1) for t in range(shards)])
+    gate_grad, up_grad, down_grad = finish(core, mine, other, gate_weight.shape, down_weight.shape)
 
     table_term = contract(counts[0], backs[0], 0, 0)
     for c in range(1, own):

time: 180 us -> 184 us (1.022)
  the two profiles are of different devices: /device:TPU:34 before, /device:TPU:1 now
where the time goes in v4:
time: 184 us; the launch traced here: 183 us
  starting transfers between devices  63.1 us (34%)
  waiting for transfers between devices  49.4 us (27%)
  Pallas kernels  39.7 us (22%)
  matrix products  12.1 us (7%)
  other arithmetic  9.49 us (5%)
  local copies, waits for them, and re-layouts  8.34 us (5%)
    ppermute x12, waiting for transfers between devices, swap(): return lax.ppermute(values, 'batch', pairs)  32.3 us
    all_to_all x5, starting transfers between devices, exchange(): return lax.all_to_all(values, axis, 0, 0)  27.8 us
    ppermute x12, starting transfers between devices, swap(): return lax.ppermute(values, 'batch', pairs)  20.5 us
    pallas_call x2, Pallas kernels, sample_pass(): pl.pallas_call(functools.partial(sample_kernel, which), out_shape=[shape(...  20.5 us
    pallas_call x2, Pallas kernels, lookup(): pl.pallas_call(lookup_kernel, in_specs=[pl.BlockSpec(memory_space=pltpu.V...  16.9 us
    all_to_all x5, waiting for transfers between devices, exchange(): return lax.all_to_all(values, axis, 0, 0)  15.2 us
    dot_general x2, matrix products, contract(): lax.dot_general(left, right, (((left_dim,), (right_dim,)), ((), ())), pre...  12.1 us
    ppermute x1, starting transfers between devices, per_device(): other = lax.ppermute(mine, 'table', [(t, t ^ 1) for t in range(shards)])  6.24 us
  transfers between devices with their start and end apart: 21, of which 12 were waited for; matrix products, arithmetic and copies ran while one was open for 14% of the time, Pallas kernels for 14%

profile of v4, /device:TPU:1, one launch (start us, length us, event | category | flops | bytes accessed | tf_op | source)
XLA Modules:
  0.0 183.0 jit_solution(1863826821678263371)
XLA Ops:
  2.2 7.2 %all-to-all-start.1 = ((bf16[16,64,256]{2,1,0:T(8,128)(2,1)}), bf16[16,64,256]{2,1,0:T(8,128)(2,1)S(1)}, u32[]{:S(2)}, u32[]{:S(2)}) async-start(bf16[16,64,256]{2,1,0:T(8,128)(2,1)} %broadcast_in_dim.8), calls=%async_computation.1 | async-start | bytes 1048576 | tf_op jit(solution)/shard_map/all_to_all | solution.py:87
  11.7 8.5 %lookup.3 = (bf16[1024,4096]{1,0:T(8,128)(2,1)}, bf16[1024,256]{1,0:T(8,128)(2,1)}) custom-call(s32[64,128]{1,0:T(8,128)} %get-tuple-element.58.high_ref, s32[64,128]{1,0:T(8,128)} %get-tuple-element.57.low_ref, bf16[4096,256]{1,0:T(8,128)(2,1)} %table_ref.3), custom_call_target="tpu_custom_call" | custom-call | flops 4294967296 | bytes 12582912 | tf_op jit(solution)/shard_map/lookup/pallas_call | solution.py:62
  20.2 5.7 %all-to-all-start.2 = ((bf16[16,64,256]{2,1,0:T(8,128)(2,1)}), bf16[16,64,256]{2,1,0:T(8,128)(2,1)S(1)}, u32[]{:S(2)}, u32[]{:S(2)}) async-start(bf16[16,64,256]{2,1,0:T(8,128)(2,1)} %bitcast.74), calls=%async_computation.2 | async-start | bytes 1048576 | tf_op jit(solution)/shard_map/all_to_all | solution.py:87
  25.9 8.5 %lookup.2 = (bf16[1024,4096]{1,0:T(8,128)(2,1)}, bf16[1024,256]{1,0:T(8,128)(2,1)}) custom-call(s32[64,128]{1,0:T(8,128)} %get-tuple-element.61.high_ref, s32[64,128]{1,0:T(8,128)} %get-tuple-element.62.low_ref, bf16[4096,256]{1,0:T(8,128)(2,1)} %table_ref.3), custom_call_target="tpu_custom_call" | custom-call | flops 4294967296 | bytes 12582912 | tf_op jit(solution)/shard_map/lookup/pallas_call | solution.py:62
  35.6 4.6 %all-to-all-start = ((bf16[16,64,256]{2,1,0:T(8,128)(2,1)}), bf16[16,64,256]{2,1,0:T(8,128)(2,1)S(1)}, u32[]{:S(2)}, u32[]{:S(2)}) async-start(bf16[16,64,256]{2,1,0:T(8,128)(2,1)} %bitcast.72), calls=%async_computation | async-start | bytes 1048576 | tf_op jit(solution)/shard_map/all_to_all | solution.py:87
  40.2 9.6 %sample_pass.2 = (bf16[1024,256]{1,0:T(8,128)(2,1)}, bf16[1024,256]{1,0:T(8,128)(2,1)}, f32[256,512]{1,0:T(8,128)}, f32[256,512]{1,0:T(8,128)}, f32[512,256]{1,0...) custom-call(bf16[1024,256]{1,0:T(8,128)(2,1)} %bitcast.71, bf16[1024,256]{1,0:T(8,128)(2,1)} %bitcast.68, ...), custom_call_target="tpu_custom_call" | custom-call | flops 10000000000 | bytes 4194304 | tf_op jit(solution)/shard_map/sample_pass/pallas_call | solution.py:210
  50.7 10.9 %sample_pass.3 = (bf16[1024,256]{1,0:T(8,128)(2,1)}, bf16[2,1024,256]{2,1,0:T(8,128)(2,1)}, bf16[2,8,176,256]{3,2,1,0:T(8,128)(2,1)}) custom-call(bf16[1024,256]{1,0:T(8,128)(2,1)} %bitcast.73, bf16[1024,256]{1,0:T(8,128)(2,1)} %bitcast.69, bf16[2,1024,256]{2,1,0:T(8,128)(2,1)} %refs_2_.3, f32[1,256]{1,0:T(1,128)} %bitcast.78, bf16[256,512]{1,0:T(8,128)(2,1)} %refs_4_.3, ...), custom_call_target="tpu_custom_call" | custom-call | flops 10000000000 | bytes 4194304 | tf_op jit(solution)/shard_map/sample_pass/pallas_call | solution.py:210
  61.6 5.6 %all-to-all-start.4 = ((bf16[16,64,256]{2,1,0:T(8,128)(2,1)}), bf16[16,64,256]{2,1,0:T(8,128)(2,1)S(1)}, u32[]{:S(2)}, u32[]{:S(2)}) async-start(bf16[16,64,256]{2,1,0:T(8,128)(2,1)} %bitcast.70), calls=%async_computation.4 | async-start | bytes 1048576 | tf_op jit(solution)/shard_map/all_to_all | solution.py:87
  67.3 9.7 %all-to-all-done.4 = bf16[16,64,256]{2,1,0:T(8,128)(2,1)S(1)} async-done(((bf16[16,64,256]{2,1,0:T(8,128)(2,1)}), bf16[16,64,256]{2,1,0:T(8,128)(2,1)S(1)}, u32[]{:S(2)}, u32[]{:S(2)}) %all-to-all-start.4) | async-done | bytes 524320 | tf_op jit(solution)/shard_map/all_to_all | solution.py:87
  76.9 4.6 %all-to-all-start.3 = ((bf16[16,64,256]{2,1,0:T(8,128)(2,1)}), bf16[16,64,256]{2,1,0:T(8,128)(2,1)S(1)}, u32[]{:S(2)}, u32[]{:S(2)}) async-start(bf16[16,64,256]{2,1,0:T(8,128)(2,1)} %bitcast.9), calls=%async_computation.3 | async-start | bytes 1048576 | tf_op jit(solution)/shard_map/all_to_all | solution.py:87
  87.2 4.1 %all-to-all-done.3 = bf16[16,64,256]{2,1,0:T(8,128)(2,1)S(1)} async-done(((bf16[16,64,256]{2,1,0:T(8,128)(2,1)}), bf16[16,64,256]{2,1,0:T(8,128)(2,1)S(1)}, u32[]{:S(2)}, u32[]{:S(2)}) %all-to-all-start.3) | async-done | bytes 524320 | tf_op jit(solution)/shard_map/all_to_all | solution.py:87
  91.3 3.8 %all-to-all-start.5 = ((bf16[8,176,256]{2,1,0:T(8,128)(2,1)}), bf16[8,176,256]{2,1,0:T(8,128)(2,1)S(1)}, u32[]{:S(2)}, u32[]{:S(2)}) async-start(bf16[8,176,256]{2,1,0:T(8,128)(2,1)} %fusion.1), calls=%async_computation.5 | async-start | bytes 1441792 | tf_op jit(solution)/shard_map/all_to_all | solution.py:294
  95.1 6.0 %fusion.13 = f32[4096,256]{1,0:T(8,128)S(1)} fusion(bf16[1024,4096]{1,0:T(8,128)(2,1)} %get-tuple-element.39, bf16[1024,256]{1,0:T(8,128)(2,1)S(1)} %bitcast.67), kind=kOutput, calls=%fused_computation.47 | convolution fusion | flops 2147483648 | bytes 13107200 | tf_op jit(solution)/shard_map/dot_general | solution.py:18
  101.0 6.2 %fusion = bf16[4096,256]{1,0:T(8,128)(2,1)S(1)} fusion(f32[4096,256]{1,0:T(8,128)S(1)} %fusion.13, bf16[1024,4096]{1,0:T(8,128)(2,1)} %get-tuple-element.41, bf16[1024,256]{1,0:T(8,128)(2,1)S(1)} %bitcast.66), kind=kOutput, calls=%fused_computation.1 | convolution fusion | flops 2149580800 | bytes 15204352 | tf_op jit(solution)/shard_map/dot_general | solution.py:18
  108.0 5.1 %collective-permute-start.9 = (bf16[176,256]{1,0:T(8,128)(2,1)}, bf16[176,256]{1,0:T(8,128)(2,1)S(1)}, u32[]{:S(2)}, u32[]{:S(2)}) collective-permute-start(bf16[176,256]{1,0:T(8,128)(2,1)} %reduce_sum.12), channel_id=1, source_target_pairs={{0,3},{1,2},{2,1},{3,0},{4,7},{5,6},{6,5},{7,4},{8,11},{9,10},{10,... | collective-permute-start | bytes 270344 | tf_op jit(solution)/shard_map/ppermute | solution.py:97
  121.6 2.4 %collective-permute-done.7 = bf16[176,256]{1,0:T(8,128)(2,1)S(1)} collective-permute-done((bf16[176,256]{1,0:T(8,128)(2,1)}, bf16[176,256]{1,0:T(8,128)(2,1)S(1)}, u32[]{:S(2)}, u32[]{:S(2)}) %collective-permute-start.7) | collective-permute-done | bytes 90144 | tf_op jit(solution)/shard_map/ppermute | solution.py:97
  124.9 2.9 %collective-permute-start.12 = (bf16[176,256]{1,0:T(8,128)(2,1)S(1)}, bf16[176,256]{1,0:T(8,128)(2,1)S(1)}, u32[]{:S(2)}, u32[]{:S(2)}) collective-permute-start(bf16[176,256]{1,0:T(8,128)(2,1)S(1)} %add_convert_fusion.1), channel_id=1, source_target_pairs={{0,12},{1,13},{2,14},{3,15},{4,8},{5,9},{6,10},{7,11},{8,4},{9,5},... | collective-permute-start | bytes 270344 | tf_op jit(solution)/shard_map/ppermute | solution.py:97
  128.1 15.7 %collective-permute-done.12 = bf16[176,256]{1,0:T(8,128)(2,1)S(1)} collective-permute-done((bf16[176,256]{1,0:T(8,128)(2,1)S(1)}, bf16[176,256]{1,0:T(8,128)(2,1)S(1)}, u32[]{:S(2)}, u32[]{:S(2)}) %collective-permute-start.12) | collective-permute-done | bytes 90144 | tf_op jit(solution)/shard_map/ppermute | solution.py:97
  144.2 3.3 %collective-permute-done.10 = bf16[176,256]{1,0:T(8,128)(2,1)S(1)} collective-permute-done((bf16[176,256]{1,0:T(8,128)(2,1)S(1)}, bf16[176,256]{1,0:T(8,128)(2,1)S(1)}, u32[]{:S(2)}, u32[]{:S(2)}) %collective-permute-start.10) | collective-permute-done | bytes 90144 | tf_op jit(solution)/shard_map/ppermute | solution.py:97
  149.0 4.6 %all-to-all-start.6 = ((bf16[8,96,256]{2,1,0:T(8,128)(2,1)}), bf16[8,96,256]{2,1,0:T(8,128)(2,1)S(1)}, u32[]{:S(2)}, u32[]{:S(2)}) async-start(bf16[8,96,256]{2,1,0:T(8,128)(2,1)} %broadcast_in_dim.22), calls=%async_computation.6 | async-start | bytes 786432 | tf_op jit(solution)/shard_map/all_to_all | solution.py:300
  156.4 3.3 %collective-permute-start.6 = (bf16[256,256]{1,0:T(8,128)(2,1)S(1)}, bf16[256,256]{1,0:T(8,128)(2,1)S(1)}, u32[]{:S(2)}, u32[]{:S(2)}) collective-permute-start(bf16[256,256]{1,0:T(8,128)(2,1)S(1)} %get-tuple-element.53), channel_id=1, source_target_pairs={{0,3},{1,2},{2,1},{3,0},{4,7},{5,6},{6,5},{7,4},{8,11},{9,10},{10,... | collective-permute-start | bytes 393224 | tf_op jit(solution)/shard_map/ppermute | solution.py:97
  162.4 7.9 %collective-permute-done.5 = bf16[256,256]{1,0:T(8,128)(2,1)S(1)} collective-permute-done((bf16[256,256]{1,0:T(8,128)(2,1)S(1)}, bf16[256,256]{1,0:T(8,128)(2,1)S(1)}, u32[]{:S(2)}, u32[]{:S(2)}) %collective-permute-start.5) | collective-permute-done | bytes 131104 | tf_op jit(solution)/shard_map/ppermute | solution.py:97
  171.1 6.2 %collective-permute-start.13 = (bf16[8,96,256]{2,1,0:T(8,128)(2,1)S(1)}, bf16[8,96,256]{2,1,0:T(8,128)(2,1)S(1)}, u32[]{:S(2)}, u32[]{:S(2)}) collective-permute-start(bf16[8,96,256]{2,1,0:T(8,128)(2,1)S(1)} %all-to-all-done.6.mine_ref), channel_id=1, source_target_pairs={{0,16},{16,0},{32,48},{48,32},{64,80},{80,64},{96,112},{112,96},{1... | collective-permute-start | bytes 1179656 | tf_op jit(solution)/shard_map/ppermute | solution.py:307
  180.7 2.3 %finish.1 = (f32[256,512]{1,0:T(8,128)}, f32[256,512]{1,0:T(8,128)}, f32[512,256]{1,0:T(8,128)}) custom-call(s32[1]{0:T(128)} %bitcast.26.core_ref, bf16[8,96,256]{2,1,0:T(8,128)(2,1)} %copy-done, bf16[8,96,256]{2,1,0:T(8,128)(2,1)} %copy-done.4), custom_call_target="tpu_custom_call" | custom-call | tf_op jit(solution)/shard_map/finish/pallas_call | solution.py:242
  (62 shorter events, 33.6 us)
Async XLA Ops:
  2.2 17.9 %all-to-all-start.1 = ((bf16[16,64,256]{2,1,0:T(8,128)(2,1)}), bf16[16,64,256]{2,1,0:T(8,128)(2,1)S(1)}, u32[]{:S(2)}, u32[]{:S(2)}) async-start(bf16[16,64,256]{2,1,0:T(8,128)(2,1)} %broadcast_in_dim.8), calls=%async_computation.1 | async-start | bytes 1048576 | tf_op jit(solution)/shard_map/all_to_all | solution.py:87
  20.2 14.2 %copy-start.1 = (bf16[16,64,256]{2,1,0:T(8,128)(2,1)}, bf16[16,64,256]{2,1,0:T(8,128)(2,1)S(1)}, u32[]{:S(2)}) copy-start(bf16[16,64,256]{2,1,0:T(8,128)(2,1)S(1)} %all-to-all-done.1) | copy-start | bytes 1572868
  20.2 15.4 %all-to-all-start.2 = ((bf16[16,64,256]{2,1,0:T(8,128)(2,1)}), bf16[16,64,256]{2,1,0:T(8,128)(2,1)S(1)}, u32[]{:S(2)}, u32[]{:S(2)}) async-start(bf16[16,64,256]{2,1,0:T(8,128)(2,1)} %bitcast.74), calls=%async_computation.2 | async-start | bytes 1048576 | tf_op jit(solution)/shard_map/all_to_all | solution.py:87
  35.6 4.6 %copy-start.2 = (bf16[16,64,256]{2,1,0:T(8,128)(2,1)}, bf16[16,64,256]{2,1,0:T(8,128)(2,1)S(1)}, u32[]{:S(2)}) copy-start(bf16[16,64,256]{2,1,0:T(8,128)(2,1)S(1)} %all-to-all-done.2) | copy-start | bytes 1572868
  35.6 14.4 %all-to-all-start = ((bf16[16,64,256]{2,1,0:T(8,128)(2,1)}), bf16[16,64,256]{2,1,0:T(8,128)(2,1)S(1)}, u32[]{:S(2)}, u32[]{:S(2)}) async-start(bf16[16,64,256]{2,1,0:T(8,128)(2,1)} %bitcast.72), calls=%async_computation | async-start | bytes 1048576 | tf_op jit(solution)/shard_map/all_to_all | solution.py:87
  61.6 15.3 %all-to-all-start.4 = ((bf16[16,64,256]{2,1,0:T(8,128)(2,1)}), bf16[16,64,256]{2,1,0:T(8,128)(2,1)S(1)}, u32[]{:S(2)}, u32[]{:S(2)}) async-start(bf16[16,64,256]{2,1,0:T(8,128)(2,1)} %bitcast.70), calls=%async_computation.4 | async-start | bytes 1048576 | tf_op jit(solution)/shard_map/all_to_all | solution.py:87
  76.9 14.4 %all-to-all-start.3 = ((bf16[16,64,256]{2,1,0:T(8,128)(2,1)}), bf16[16,64,256]{2,1,0:T(8,128)(2,1)S(1)}, u32[]{:S(2)}, u32[]{:S(2)}) async-start(bf16[16,64,256]{2,1,0:T(8,128)(2,1)} %bitcast.9), calls=%async_computation.3 | async-start | bytes 1048576 | tf_op jit(solution)/shard_map/all_to_all | solution.py:87
  82.7 2.3 %collective-permute-start = (bf16[8,176,256]{2,1,0:T(8,128)(2,1)S(1)}, bf16[8,176,256]{2,1,0:T(8,128)(2,1)S(1)}, u32[]{:S(2)}, u32[]{:S(2)}) collective-permute-start(bf16[8,176,256]{2,1,0:T(8,128)(2,1)S(1)} %dynamic-slice_bitcast_fusion), channel_id=1, source_target_pairs={{0,16},{16,0},{32,48},{48,32},{64,80},{80,64},{96,112},{112,96},{1... | collective-permute-start | bytes 2162696 | tf_op jit(solution)/shard_map/ppermute | solution.py:291
  91.3 15.9 %all-to-all-start.5 = ((bf16[8,176,256]{2,1,0:T(8,128)(2,1)}), bf16[8,176,256]{2,1,0:T(8,128)(2,1)S(1)}, u32[]{:S(2)}, u32[]{:S(2)}) async-start(bf16[8,176,256]{2,1,0:T(8,128)(2,1)} %fusion.1), calls=%async_computation.5 | async-start | bytes 1441792 | tf_op jit(solution)/shard_map/all_to_all | solution.py:294
  108.0 11.5 %collective-permute-start.9 = (bf16[176,256]{1,0:T(8,128)(2,1)}, bf16[176,256]{1,0:T(8,128)(2,1)S(1)}, u32[]{:S(2)}, u32[]{:S(2)}) collective-permute-start(bf16[176,256]{1,0:T(8,128)(2,1)} %reduce_sum.12), channel_id=1, source_target_pairs={{0,3},{1,2},{2,1},{3,0},{4,7},{5,6},{6,5},{7,4},{8,11},{9,10},{10,... | collective-permute-start | bytes 270344 | tf_op jit(solution)/shard_map/ppermute | solution.py:97
  113.1 8.5 %collective-permute-start.8 = (bf16[176,256]{1,0:T(8,128)(2,1)}, bf16[176,256]{1,0:T(8,128)(2,1)S(1)}, u32[]{:S(2)}, u32[]{:S(2)}) collective-permute-start(bf16[176,256]{1,0:T(8,128)(2,1)} %reduce_sum.12), channel_id=1, source_target_pairs={{0,2},{1,3},{2,0},{3,1},{4,6},{5,7},{6,4},{7,5},{8,10},{9,11},{10,... | collective-permute-start | bytes 270344 | tf_op jit(solution)/shard_map/ppermute | solution.py:97
  114.3 9.7 %collective-permute-start.7 = (bf16[176,256]{1,0:T(8,128)(2,1)}, bf16[176,256]{1,0:T(8,128)(2,1)S(1)}, u32[]{:S(2)}, u32[]{:S(2)}) collective-permute-start(bf16[176,256]{1,0:T(8,128)(2,1)} %reduce_sum.12), channel_id=1, source_target_pairs={{0,1},{1,0},{2,3},{3,2},{4,5},{5,4},{6,7},{7,6},{8,9},{9,8},{10,11... | collective-permute-start | bytes 270344 | tf_op jit(solution)/shard_map/ppermute | solution.py:97
  116.2 37.3 %collective-permute-start.1 = (bf16[1024,256]{1,0:T(8,128)(2,1)}, bf16[1024,256]{1,0:T(8,128)(2,1)S(1)}, u32[]{:S(2)}, u32[]{:S(2)}) collective-permute-start(bf16[1024,256]{1,0:T(8,128)(2,1)} %get-tuple-element.49), channel_id=1, source_target_pairs={{0,4},{1,5},{2,6},{3,7},{4,0},{5,1},{6,2},{7,3},{8,12},{9,13},{10,... | collective-permute-start | bytes 1572872 | tf_op jit(solution)/shard_map/ppermute | solution.py:97
  117.6 36.0 %collective-permute-start.3 = (bf16[1024,256]{1,0:T(8,128)(2,1)}, bf16[1024,256]{1,0:T(8,128)(2,1)}, u32[]{:S(2)}, u32[]{:S(2)}) collective-permute-start(bf16[1024,256]{1,0:T(8,128)(2,1)} %get-tuple-element.50), channel_id=1, source_target_pairs={{0,12},{1,13},{2,14},{3,15},{4,8},{5,9},{6,10},{7,11},{8,4},{9,5},... | collective-permute-start | bytes 1572872 | tf_op jit(solution)/shard_map/ppermute | solution.py:97
  119.5 34.1 %collective-permute-start.2 = (bf16[1024,256]{1,0:T(8,128)(2,1)S(1)}, bf16[1024,256]{1,0:T(8,128)(2,1)}, u32[]{:S(2)}, u32[]{:S(2)}) collective-permute-start(bf16[1024,256]{1,0:T(8,128)(2,1)S(1)} %get-tuple-element.51), channel_id=1, source_target_pairs={{0,8},{1,9},{2,10},{3,11},{4,12},{5,13},{6,14},{7,15},{8,0},{9,1},... | collective-permute-start | bytes 1572872 | tf_op jit(solution)/shard_map/ppermute | solution.py:97
  124.9 18.9 %collective-permute-start.12 = (bf16[176,256]{1,0:T(8,128)(2,1)S(1)}, bf16[176,256]{1,0:T(8,128)(2,1)S(1)}, u32[]{:S(2)}, u32[]{:S(2)}) collective-permute-start(bf16[176,256]{1,0:T(8,128)(2,1)S(1)} %add_convert_fusion.1), channel_id=1, source_target_pairs={{0,12},{1,13},{2,14},{3,15},{4,8},{5,9},{6,10},{7,11},{8,4},{9,5},... | collective-permute-start | bytes 270344 | tf_op jit(solution)/shard_map/ppermute | solution.py:97
  127.8 16.4 %collective-permute-start.11 = (bf16[176,256]{1,0:T(8,128)(2,1)S(1)}, bf16[176,256]{1,0:T(8,128)(2,1)S(1)}, u32[]{:S(2)}, u32[]{:S(2)}) collective-permute-start(bf16[176,256]{1,0:T(8,128)(2,1)S(1)} %add_convert_fusion.1), channel_id=1, source_target_pairs={{0,8},{1,9},{2,10},{3,11},{4,12},{5,13},{6,14},{7,15},{8,0},{9,1},... | collective-permute-start | bytes 270344 | tf_op jit(solution)/shard_map/ppermute | solution.py:97
  143.8 3.7 %collective-permute-start.10 = (bf16[176,256]{1,0:T(8,128)(2,1)S(1)}, bf16[176,256]{1,0:T(8,128)(2,1)S(1)}, u32[]{:S(2)}, u32[]{:S(2)}) collective-permute-start(bf16[176,256]{1,0:T(8,128)(2,1)S(1)} %add_convert_fusion.1), channel_id=1, source_target_pairs={{0,4},{1,5},{2,6},{3,7},{4,0},{5,1},{6,2},{7,3},{8,12},{9,13},{10,... | collective-permute-start | bytes 270344 | tf_op jit(solution)/shard_map/ppermute | solution.py:97
  149.0 22.1 %all-to-all-start.6 = ((bf16[8,96,256]{2,1,0:T(8,128)(2,1)}), bf16[8,96,256]{2,1,0:T(8,128)(2,1)S(1)}, u32[]{:S(2)}, u32[]{:S(2)}) async-start(bf16[8,96,256]{2,1,0:T(8,128)(2,1)} %broadcast_in_dim.22), calls=%async_computation.6 | async-start | bytes 786432 | tf_op jit(solution)/shard_map/all_to_all | solution.py:300
  155.1 6.2 %collective-permute-start.4 = (bf16[256,256]{1,0:T(8,128)(2,1)S(1)}, bf16[256,256]{1,0:T(8,128)(2,1)S(1)}, u32[]{:S(2)}, u32[]{:S(2)}) collective-permute-start(bf16[256,256]{1,0:T(8,128)(2,1)S(1)} %get-tuple-element.52), channel_id=1, source_target_pairs={{0,1},{1,0},{2,3},{3,2},{4,5},{5,4},{6,7},{7,6},{8,9},{9,8},{10,11... | collective-permute-start | bytes 393224 | tf_op jit(solution)/shard_map/ppermute | solution.py:97
  156.4 6.0 %collective-permute-start.6 = (bf16[256,256]{1,0:T(8,128)(2,1)S(1)}, bf16[256,256]{1,0:T(8,128)(2,1)S(1)}, u32[]{:S(2)}, u32[]{:S(2)}) collective-permute-start(bf16[256,256]{1,0:T(8,128)(2,1)S(1)} %get-tuple-element.53), channel_id=1, source_target_pairs={{0,3},{1,2},{2,1},{3,0},{4,7},{5,6},{6,5},{7,4},{8,11},{9,10},{10,... | collective-permute-start | bytes 393224 | tf_op jit(solution)/shard_map/ppermute | solution.py:97
  159.7 10.6 %collective-permute-start.5 = (bf16[256,256]{1,0:T(8,128)(2,1)S(1)}, bf16[256,256]{1,0:T(8,128)(2,1)S(1)}, u32[]{:S(2)}, u32[]{:S(2)}) collective-permute-start(bf16[256,256]{1,0:T(8,128)(2,1)S(1)} %get-tuple-element.54), channel_id=1, source_target_pairs={{0,2},{1,3},{2,0},{3,1},{4,6},{5,7},{6,4},{7,5},{8,10},{9,11},{10,... | collective-permute-start | bytes 393224 | tf_op jit(solution)/shard_map/ppermute | solution.py:97
  171.1 8.9 %copy-start = (bf16[8,96,256]{2,1,0:T(8,128)(2,1)}, bf16[8,96,256]{2,1,0:T(8,128)(2,1)S(1)}, u32[]{:S(2)}) copy-start(bf16[8,96,256]{2,1,0:T(8,128)(2,1)S(1)} %all-to-all-done.6.mine_ref) | copy-start | bytes 1179652
  171.1 8.9 %collective-permute-start.13 = (bf16[8,96,256]{2,1,0:T(8,128)(2,1)S(1)}, bf16[8,96,256]{2,1,0:T(8,128)(2,1)S(1)}, u32[]{:S(2)}, u32[]{:S(2)}) collective-permute-start(bf16[8,96,256]{2,1,0:T(8,128)(2,1)S(1)} %all-to-all-done.6.mine_ref), channel_id=1, source_target_pairs={{0,16},{16,0},{32,48},{48,32},{64,80},{80,64},{96,112},{112,96},{1... | collective-permute-start | bytes 1179656 | tf_op jit(solution)/shard_map/ppermute | solution.py:307
  (3 other events, 2.2 us)

commit v5 on v4

--- a/solution.py
+++ b/solution.py
@@ -20,14 +20,16 @@
     )
 
 
-def lookup_kernel(high_ref, low_ref, table_ref, counts_ref, embeds_ref, held_ref, sems):
+def lookup_kernel(ids_ref, table_ref, counts_ref, embeds_ref, held_ref, sems):
     segments = sems.shape[0]
-    groups = high_ref.shape[0] // segments
+    groups = ids_ref.shape[0] // segments
     slot = lax.broadcasted_iota(jnp.int32, (256, 128), 0)
+    lane = lax.broadcasted_iota(jnp.int32, (1, 128), 1) & 15
 
     def step(g, carry):
-        left = jnp.where(slot == high_ref[pl.ds(g, 1), :], 1.0, 0.0).astype(BF)
-        right = jnp.where(slot == low_ref[pl.ds(g, 1), :], 1.0, 0.0).astype(BF)
+        ids = ids_ref[pl.ds(g, 1), :]
+        left = jnp.where(slot == (ids >> 8) * 16 + lane, 1.0, 0.0).astype(BF)
+        right = jnp.where(slot == (ids & 255), 1.0, 0.0).astype(BF)
         both = contract(left, right, 1, 1).astype(BF)
         for h in range(16):
             held_ref[pl.ds(pl.multiple_of(g * 16, 16), 16), h * 256 : (h + 1) * 256] = both[
@@ -57,11 +59,9 @@
         .transpose(0, 1, 3, 2)
         .reshape(rows // 16, 128)
     )
-    high = (lanes // 256) * 16 + lax.broadcasted_iota(jnp.int32, lanes.shape, 1) % 16
-    low = lanes % 256
     return pl.pallas_call(
         lookup_kernel,
-        in_specs=[pl.BlockSpec(memory_space=pltpu.VMEM)] * 3,
+        in_specs=[pl.BlockSpec(memory_space=pltpu.VMEM)] * 2,
         out_specs=[
             pl.BlockSpec(memory_space=pl.ANY),
             pl.BlockSpec(memory_space=pltpu.VMEM),
@@ -80,7 +80,7 @@
             transcendentals=0,
         ),
         name="lookup",
-    )(high, low, emb_table)
+    )(lanes, emb_table)
 
 
 def exchange(values, axis):
@@ -113,7 +113,7 @@
     return exchange(jnp.broadcast_to(values[None], (size,) + values.shape), axis)
 
 
-CHUNK = 256
+CHUNK = 512
 SEGMENTS = 4
 
 
@@ -227,6 +227,46 @@
     )(x, proj, out_grad, norm_gain[None], gate_weight, up_weight, down_weight, *before)
 
 
+def quarter_kernel(_, counts0_ref, counts1_ref, back0_ref, back1_ref, out_ref, total_ref):
+    term = jnp.dot(back0_ref[...].T, counts0_ref[...], preferred_element_type=F32)
+    term += jnp.dot(back1_ref[...].T, counts1_ref[...], preferred_element_type=F32)
+    step = pl.program_id(0)
+
+    @pl.when(step == 0)
+    def _():
+        total_ref[...] = term
+
+    @pl.when(step > 0)
+    def _():
+        total_ref[...] += term
+
+    @pl.when(step == pl.num_programs(0) - 1)
+    def _():
+        out_ref[...] = total_ref[...].T.astype(BF)
+
+
+def quarter(which, counts, backs):
+    rows, width = backs[0].shape
+    size = counts[0].shape[1] // 4
+    steps = 2
+    return pl.pallas_call(
+        quarter_kernel,
+        grid_spec=pltpu.PrefetchScalarGridSpec(
+            num_scalar_prefetch=1,
+            grid=(steps,),
+            in_specs=[pl.BlockSpec((rows // steps, size), lambda i, w: (i, w[0]))] * 2
+            + [pl.BlockSpec((rows // steps, width), lambda i, w: (i, 0))] * 2,
+            out_specs=pl.BlockSpec((size, width), lambda i, w: (0, 0)),
+            scratch_shapes=[pltpu.VMEM((width, size), F32)],
+        ),
+        out_shape=jax.ShapeDtypeStruct((size, width), BF),
+        cost_estimate=pl.CostEstimate(
+            flops=4 * rows * size * width, bytes_accessed=4 * rows * size, transcendentals=0
+        ),
+        name="quarter",
+    )(which[None], *counts, *backs)
+
+
 def finish_kernel(core_ref, mine_ref, other_ref, gate_ref, up_ref, down_ref):
     first = core_ref[0] == 0
     for t in range(16):
@@ -307,12 +347,14 @@
     other = lax.ppermute(mine, "table", [(t, t ^ 1) for t in range(shards)])
     gate_grad, up_grad, down_grad = finish(core, mine, other, gate_weight.shape, down_weight.shape)
 
-    table_term = contract(counts[0], backs[0], 0, 0)
-    for c in range(1, own):
-        table_term = table_term + contract(counts[c], backs[c], 0, 0)
-    table_term = table_term.astype(BF)
-    here = table_term.shape[0] // 16
-    table_term = sum_scattered(table_term.reshape(4, 4 * here, width), "y").astype(BF)
+    mine = place("y")
+    came = []
+    for k in (2, 1, 3):
+        piece = quarter(mine ^ k, counts, backs)
+        came.append(swap(piece, "y", k))
+    piece = quarter(mine, counts, backs)
+    table_term = sum((c.astype(F32) for c in came), piece.astype(F32)).astype(BF)
+    here = table_term.shape[0] // 4
     table_grad = sum_scattered(table_term.reshape(4, here, width), "z")
     return (block_out, table_grad, projection_grad, gain_grad, gate_grad, up_grad, down_grad)
 

time: 184 us -> 173 us (0.940)
  the two profiles are of different devices: /device:TPU:1 before, /device:TPU:33 now
where the time goes in v5:
time: 173 us; the launch traced here: 172 us
  starting transfers between devices  61 us (35%)
  Pallas kernels  54.7 us (32%)
  waiting for transfers between devices  45.5 us (26%)
  local copies, waits for them, and re-layouts  6.81 us (4%)
  other arithmetic  3.48 us (2%)
    ppermute x12, waiting for transfers between devices, swap(): return lax.ppermute(values, 'batch', pairs)  27.8 us
    all_to_all x5, starting transfers between devices, exchange(): return lax.all_to_all(values, axis, 0, 0)  27.5 us
    ppermute x12, starting transfers between devices, swap(): return lax.ppermute(values, 'batch', pairs)  23 us
    pallas_call x2, Pallas kernels, sample_pass(): pl.pallas_call(functools.partial(sample_kernel, which), out_shape=[shape(...  18.3 us
    pallas_call x4, Pallas kernels, quarter(): pl.pallas_call(quarter_kernel, grid_spec=pltpu.PrefetchScalarGridSpec(num...  17.2 us
    pallas_call x2, Pallas kernels, lookup(): pl.pallas_call(lookup_kernel, in_specs=[pl.BlockSpec(memory_space=pltpu.V...  16.9 us
    all_to_all x5, waiting for transfers between devices, exchange(): return lax.all_to_all(values, axis, 0, 0)  15.5 us
    all_to_all x1, starting transfers between devices, per_device(): lax.all_to_all(jnp.broadcast_to(parts[:96][None], (8, 96, width)), 'table...  4.23 us
  transfers between devices with their start and end apart: 21, of which 8 were waited for; matrix products, arithmetic and copies ran while one was open for 4% of the time, Pallas kernels for 25%

profile of v5, /device:TPU:33, one launch (start us, length us, event | category | flops | bytes accessed | tf_op | source)
XLA Modules:
  0.0 172.4 jit_solution(10531270911646287501)
XLA Ops:
  2.3 6.1 %all-to-all-start.1 = ((bf16[16,64,256]{2,1,0:T(8,128)(2,1)}), bf16[16,64,256]{2,1,0:T(8,128)(2,1)S(1)}, u32[]{:S(2)}, u32[]{:S(2)}) async-start(bf16[16,64,256]{2,1,0:T(8,128)(2,1)} %broadcast_in_dim.31), calls=%async_computation.1 | async-start | bytes 1048576 | tf_op jit(solution)/shard_map/all_to_all | solution.py:87
  9.3 8.5 %lookup.3 = (bf16[1024,4096]{1,0:T(8,128)(2,1)}, bf16[1024,256]{1,0:T(8,128)(2,1)}) custom-call(s32[64,128]{1,0:T(8,128)} %reshape.65.ids_ref, bf16[4096,256]{1,0:T(8,128)(2,1)} %table_ref.3), custom_call_target="tpu_custom_call" | custom-call | flops 4294967296 | bytes 12582912 | tf_op jit(solution)/shard_map/lookup/pallas_call | solution.py:62
  17.8 5.7 %all-to-all-start.2 = ((bf16[16,64,256]{2,1,0:T(8,128)(2,1)}), bf16[16,64,256]{2,1,0:T(8,128)(2,1)S(1)}, u32[]{:S(2)}, u32[]{:S(2)}) async-start(bf16[16,64,256]{2,1,0:T(8,128)(2,1)} %bitcast.66), calls=%async_computation.2 | async-start | bytes 1048576 | tf_op jit(solution)/shard_map/all_to_all | solution.py:87
  24.5 8.5 %lookup.2 = (bf16[1024,4096]{1,0:T(8,128)(2,1)}, bf16[1024,256]{1,0:T(8,128)(2,1)}) custom-call(s32[64,128]{1,0:T(8,128)} %reshape.62.ids_ref, bf16[4096,256]{1,0:T(8,128)(2,1)} %table_ref.3), custom_call_target="tpu_custom_call" | custom-call | flops 4294967296 | bytes 12582912 | tf_op jit(solution)/shard_map/lookup/pallas_call | solution.py:62
  33.0 5.7 %all-to-all-start = ((bf16[16,64,256]{2,1,0:T(8,128)(2,1)}), bf16[16,64,256]{2,1,0:T(8,128)(2,1)S(1)}, u32[]{:S(2)}, u32[]{:S(2)}) async-start(bf16[16,64,256]{2,1,0:T(8,128)(2,1)} %bitcast.68), calls=%async_computation | async-start | bytes 1048576 | tf_op jit(solution)/shard_map/all_to_all | solution.py:87
  38.7 8.5 %sample_pass.2 = (bf16[1024,256]{1,0:T(8,128)(2,1)}, bf16[1024,256]{1,0:T(8,128)(2,1)}, f32[256,512]{1,0:T(8,128)}, f32[256,512]{1,0:T(8,128)}, f32[512,256]{1,0...) custom-call(bf16[1024,256]{1,0:T(8,128)(2,1)} %bitcast.65, bf16[1024,256]{1,0:T(8,128)(2,1)} %bitcast.62, ...), custom_call_target="tpu_custom_call" | custom-call | flops 10000000000 | bytes 4194304 | tf_op jit(solution)/shard_map/sample_pass/pallas_call | solution.py:210
  49.0 9.8 %sample_pass.3 = (bf16[1024,256]{1,0:T(8,128)(2,1)}, bf16[2,1024,256]{2,1,0:T(8,128)(2,1)}, bf16[2,8,176,256]{3,2,1,0:T(8,128)(2,1)}) custom-call(bf16[1024,256]{1,0:T(8,128)(2,1)} %bitcast.67, bf16[1024,256]{1,0:T(8,128)(2,1)} %bitcast.63, bf16[2,1024,256]{2,1,0:T(8,128)(2,1)} %refs_2_.3, f32[1,256]{1,0:T(1,128)} %bitcast.72, bf16[256,512]{1,0:T(8,128)(2,1)} %refs_4_.3, ...), custom_call_target="tpu_custom_call" | custom-call | flops 10000000000 | bytes 4194304 | tf_op jit(solution)/shard_map/sample_pass/pallas_call | solution.py:210
  58.8 5.0 %all-to-all-start.4 = ((bf16[16,64,256]{2,1,0:T(8,128)(2,1)}), bf16[16,64,256]{2,1,0:T(8,128)(2,1)S(1)}, u32[]{:S(2)}, u32[]{:S(2)}) async-start(bf16[16,64,256]{2,1,0:T(8,128)(2,1)} %bitcast.64), calls=%async_computation.4 | async-start | bytes 1048576 | tf_op jit(solution)/shard_map/all_to_all | solution.py:87
  63.8 9.4 %all-to-all-done.4 = bf16[16,64,256]{2,1,0:T(8,128)(2,1)S(1)} async-done(((bf16[16,64,256]{2,1,0:T(8,128)(2,1)}), bf16[16,64,256]{2,1,0:T(8,128)(2,1)S(1)}, u32[]{:S(2)}, u32[]{:S(2)}) %all-to-all-start.4) | async-done | bytes 524320 | tf_op jit(solution)/shard_map/all_to_all | solution.py:87
  73.2 4.9 %all-to-all-start.3 = ((bf16[16,64,256]{2,1,0:T(8,128)(2,1)}), bf16[16,64,256]{2,1,0:T(8,128)(2,1)S(1)}, u32[]{:S(2)}, u32[]{:S(2)}) async-start(bf16[16,64,256]{2,1,0:T(8,128)(2,1)} %bitcast.10), calls=%async_computation.3 | async-start | bytes 1048576 | tf_op jit(solution)/shard_map/all_to_all | solution.py:87
  82.6 5.1 %all-to-all-done.3 = bf16[16,64,256]{2,1,0:T(8,128)(2,1)S(1)} async-done(((bf16[16,64,256]{2,1,0:T(8,128)(2,1)}), bf16[16,64,256]{2,1,0:T(8,128)(2,1)S(1)}, u32[]{:S(2)}, u32[]{:S(2)}) %all-to-all-start.3) | async-done | bytes 524320 | tf_op jit(solution)/shard_map/all_to_all | solution.py:87
  87.6 3.8 %all-to-all-start.5 = ((bf16[8,176,256]{2,1,0:T(8,128)(2,1)}), bf16[8,176,256]{2,1,0:T(8,128)(2,1)S(1)}, u32[]{:S(2)}, u32[]{:S(2)}) async-start(bf16[8,176,256]{2,1,0:T(8,128)(2,1)} %fusion), calls=%async_computation.5 | async-start | bytes 1441792 | tf_op jit(solution)/shard_map/all_to_all | solution.py:334
  91.5 4.3 %quarter.7 = bf16[1024,256]{1,0:T(8,128)(2,1)} custom-call(s32[1]{0:T(128)} %bitcast.18._, bf16[1024,4096]{1,0:T(8,128)(2,1)} %get-tuple-element.39.counts0_ref, bf16[1024,4096]{1,0:T(8,128)(2,1)} %get-tuple-element.40.counts1_ref, bf16[1024,256]{1,0:T(8,128)(2,1)} %bitcast.54, bf16[1024,256]{1,0:T(8,128)(2,1)} %bitcast.50), custom_call_target="tpu_custom_call" | custom-call | flops 1073741824 | bytes 4194304 | tf_op jit(solution)/shard_map/quarter/pallas_call | solution.py:252
  95.8 2.7 %collective-permute-start.3 = (bf16[1024,256]{1,0:T(8,128)(2,1)}, bf16[1024,256]{1,0:T(8,128)(2,1)S(1)}, u32[]{:S(2)}, u32[]{:S(2)}) collective-permute-start(bf16[1024,256]{1,0:T(8,128)(2,1)} %quarter.7), channel_id=1, source_target_pairs={{0,12},{1,13},{2,14},{3,15},{4,8},{5,9},{6,10},{7,11},{8,4},{9,5},... | collective-permute-start | bytes 1572872 | tf_op jit(solution)/shard_map/ppermute | solution.py:97
  98.5 4.3 %quarter.6 = bf16[1024,256]{1,0:T(8,128)(2,1)} custom-call(s32[1]{0:T(128)} %bitcast.17._, bf16[1024,4096]{1,0:T(8,128)(2,1)} %get-tuple-element.39.counts0_ref, bf16[1024,4096]{1,0:T(8,128)(2,1)} %get-tuple-element.40.counts1_ref, bf16[1024,256]{1,0:T(8,128)(2,1)} %bitcast.55, bf16[1024,256]{1,0:T(8,128)(2,1)} %bitcast.51), custom_call_target="tpu_custom_call" | custom-call | flops 1073741824 | bytes 4194304 | tf_op jit(solution)/shard_map/quarter/pallas_call | solution.py:252
  102.9 5.2 %collective-permute-start.9 = (bf16[176,256]{1,0:T(8,128)(2,1)S(1)}, bf16[176,256]{1,0:T(8,128)(2,1)S(1)}, u32[]{:S(2)}, u32[]{:S(2)}) collective-permute-start(bf16[176,256]{1,0:T(8,128)(2,1)S(1)} %reduce_sum.12), channel_id=1, source_target_pairs={{0,3},{1,2},{2,1},{3,0},{4,7},{5,6},{6,5},{7,4},{8,11},{9,10},{10,... | collective-permute-start | bytes 270344 | tf_op jit(solution)/shard_map/ppermute | solution.py:97
  110.5 4.3 %quarter.5 = bf16[1024,256]{1,0:T(8,128)(2,1)} custom-call(s32[1]{0:T(128)} %bitcast.16._, bf16[1024,4096]{1,0:T(8,128)(2,1)} %get-tuple-element.39.counts0_ref, bf16[1024,4096]{1,0:T(8,128)(2,1)} %get-tuple-element.40.counts1_ref, bf16[1024,256]{1,0:T(8,128)(2,1)} %bitcast.56, bf16[1024,256]{1,0:T(8,128)(2,1)} %bitcast.52), custom_call_target="tpu_custom_call" | custom-call | flops 1073741824 | bytes 4194304 | tf_op jit(solution)/shard_map/quarter/pallas_call | solution.py:252
  114.8 2.7 %collective-permute-start.1 = (bf16[1024,256]{1,0:T(8,128)(2,1)}, bf16[1024,256]{1,0:T(8,128)(2,1)S(1)}, u32[]{:S(2)}, u32[]{:S(2)}) collective-permute-start(bf16[1024,256]{1,0:T(8,128)(2,1)} %quarter.5), channel_id=1, source_target_pairs={{0,8},{1,9},{2,10},{3,11},{4,12},{5,13},{6,14},{7,15},{8,0},{9,1},... | collective-permute-start | bytes 1572872 | tf_op jit(solution)/shard_map/ppermute | solution.py:97
  120.3 14.0 %collective-permute-done.12 = bf16[176,256]{1,0:T(8,128)(2,1)S(1)} collective-permute-done((bf16[176,256]{1,0:T(8,128)(2,1)S(1)}, bf16[176,256]{1,0:T(8,128)(2,1)S(1)}, u32[]{:S(2)}, u32[]{:S(2)}) %collective-permute-start.12) | collective-permute-done | bytes 90144 | tf_op jit(solution)/shard_map/ppermute | solution.py:97
  135.7 4.3 %quarter.4 = bf16[1024,256]{1,0:T(8,128)(2,1)} custom-call(s32[1]{0:T(128)} %bitcast.9._, bf16[1024,4096]{1,0:T(8,128)(2,1)} %get-tuple-element.39.counts0_ref, bf16[1024,4096]{1,0:T(8,128)(2,1)} %get-tuple-element.40.counts1_ref, bf16[1024,256]{1,0:T(8,128)(2,1)} %bitcast.57, bf16[1024,256]{1,0:T(8,128)(2,1)} %bitcast.53), custom_call_target="tpu_custom_call" | custom-call | flops 1073741824 | bytes 4194304 | tf_op jit(solution)/shard_map/quarter/pallas_call | solution.py:252
  140.9 4.2 %all-to-all-start.6 = ((bf16[8,96,256]{2,1,0:T(8,128)(2,1)}), bf16[8,96,256]{2,1,0:T(8,128)(2,1)S(1)}, u32[]{:S(2)}, u32[]{:S(2)}) async-start(bf16[8,96,256]{2,1,0:T(8,128)(2,1)} %broadcast_in_dim.38), calls=%async_computation.6 | async-start | bytes 786432 | tf_op jit(solution)/shard_map/all_to_all | solution.py:340
  145.5 3.3 %collective-permute-start.6 = (bf16[256,256]{1,0:T(8,128)(2,1)S(1)}, bf16[256,256]{1,0:T(8,128)(2,1)S(1)}, u32[]{:S(2)}, u32[]{:S(2)}) collective-permute-start(bf16[256,256]{1,0:T(8,128)(2,1)S(1)} %get-tuple-element.50), channel_id=1, source_target_pairs={{0,3},{1,2},{2,1},{3,0},{4,7},{5,6},{6,5},{7,4},{8,11},{9,10},{10,... | collective-permute-start | bytes 393224 | tf_op jit(solution)/shard_map/ppermute | solution.py:97
  151.8 13.3 %collective-permute-done.5 = bf16[256,256]{1,0:T(8,128)(2,1)S(1)} collective-permute-done((bf16[256,256]{1,0:T(8,128)(2,1)S(1)}, bf16[256,256]{1,0:T(8,128)(2,1)S(1)}, u32[]{:S(2)}, u32[]{:S(2)}) %collective-permute-start.5) | collective-permute-done | bytes 131104 | tf_op jit(solution)/shard_map/ppermute | solution.py:97
  170.1 2.3 %finish.1 = (f32[256,512]{1,0:T(8,128)}, f32[256,512]{1,0:T(8,128)}, f32[512,256]{1,0:T(8,128)}) custom-call(s32[1]{0:T(128)} %bitcast.25.core_ref, bf16[8,96,256]{2,1,0:T(8,128)(2,1)} %copy-done.3, bf16[8,96,256]{2,1,0:T(8,128)(2,1)} %copy-done.8), custom_call_target="tpu_custom_call" | custom-call | tf_op jit(solution)/shard_map/finish/pallas_call | solution.py:282
  (67 shorter events, 25.5 us)
Async XLA Ops:
  2.3 15.5 %all-to-all-start.1 = ((bf16[16,64,256]{2,1,0:T(8,128)(2,1)}), bf16[16,64,256]{2,1,0:T(8,128)(2,1)S(1)}, u32[]{:S(2)}, u32[]{:S(2)}) async-start(bf16[16,64,256]{2,1,0:T(8,128)(2,1)} %broadcast_in_dim.31), calls=%async_computation.1 | async-start | bytes 1048576 | tf_op jit(solution)/shard_map/all_to_all | solution.py:87
  17.8 15.1 %copy-start.5 = (bf16[16,64,256]{2,1,0:T(8,128)(2,1)}, bf16[16,64,256]{2,1,0:T(8,128)(2,1)S(1)}, u32[]{:S(2)}) copy-start(bf16[16,64,256]{2,1,0:T(8,128)(2,1)S(1)} %all-to-all-done.1) | copy-start | bytes 1572868
  17.8 15.2 %all-to-all-start.2 = ((bf16[16,64,256]{2,1,0:T(8,128)(2,1)}), bf16[16,64,256]{2,1,0:T(8,128)(2,1)S(1)}, u32[]{:S(2)}, u32[]{:S(2)}) async-start(bf16[16,64,256]{2,1,0:T(8,128)(2,1)} %bitcast.66), calls=%async_computation.2 | async-start | bytes 1048576 | tf_op jit(solution)/shard_map/all_to_all | solution.py:87
  33.0 15.2 %all-to-all-start = ((bf16[16,64,256]{2,1,0:T(8,128)(2,1)}), bf16[16,64,256]{2,1,0:T(8,128)(2,1)S(1)}, u32[]{:S(2)}, u32[]{:S(2)}) async-start(bf16[16,64,256]{2,1,0:T(8,128)(2,1)} %bitcast.68), calls=%async_computation | async-start | bytes 1048576 | tf_op jit(solution)/shard_map/all_to_all | solution.py:87
  58.8 19.4 %copy-start.4 = (bf16[2,8,176,256]{3,2,1,0:T(8,128)(2,1)S(1)}, bf16[2,8,176,256]{3,2,1,0:T(8,128)(2,1)}, u32[]{:S(2)}) copy-start(bf16[2,8,176,256]{3,2,1,0:T(8,128)(2,1)} %get-tuple-element.42) | copy-start | bytes 4325380
  58.8 14.5 %all-to-all-start.4 = ((bf16[16,64,256]{2,1,0:T(8,128)(2,1)}), bf16[16,64,256]{2,1,0:T(8,128)(2,1)S(1)}, u32[]{:S(2)}, u32[]{:S(2)}) async-start(bf16[16,64,256]{2,1,0:T(8,128)(2,1)} %bitcast.64), calls=%async_computation.4 | async-start | bytes 1048576 | tf_op jit(solution)/shard_map/all_to_all | solution.py:87
  73.2 9.3 %copy-start = (bf16[16,64,256]{2,1,0:T(8,128)(2,1)}, bf16[16,64,256]{2,1,0:T(8,128)(2,1)S(1)}, u32[]{:S(2)}) copy-start(bf16[16,64,256]{2,1,0:T(8,128)(2,1)S(1)} %all-to-all-done.4) | copy-start | bytes 1572868
  73.2 14.4 %all-to-all-start.3 = ((bf16[16,64,256]{2,1,0:T(8,128)(2,1)}), bf16[16,64,256]{2,1,0:T(8,128)(2,1)S(1)}, u32[]{:S(2)}, u32[]{:S(2)}) async-start(bf16[16,64,256]{2,1,0:T(8,128)(2,1)} %bitcast.10), calls=%async_computation.3 | async-start | bytes 1048576 | tf_op jit(solution)/shard_map/all_to_all | solution.py:87
  79.1 2.4 %collective-permute-start = (bf16[8,176,256]{2,1,0:T(8,128)(2,1)}, bf16[8,176,256]{2,1,0:T(8,128)(2,1)S(1)}, u32[]{:S(2)}, u32[]{:S(2)}) collective-permute-start(bf16[8,176,256]{2,1,0:T(8,128)(2,1)} %dynamic-slice_bitcast_fusion), channel_id=1, source_target_pairs={{0,16},{16,0},{32,48},{48,32},{64,80},{80,64},{96,112},{112,96},{1... | collective-permute-start | bytes 2162696 | tf_op jit(solution)/shard_map/ppermute | solution.py:331
  87.6 15.2 %all-to-all-start.5 = ((bf16[8,176,256]{2,1,0:T(8,128)(2,1)}), bf16[8,176,256]{2,1,0:T(8,128)(2,1)S(1)}, u32[]{:S(2)}, u32[]{:S(2)}) async-start(bf16[8,176,256]{2,1,0:T(8,128)(2,1)} %fusion), calls=%async_computation.5 | async-start | bytes 1441792 | tf_op jit(solution)/shard_map/all_to_all | solution.py:334
  95.8 49.4 %collective-permute-start.3 = (bf16[1024,256]{1,0:T(8,128)(2,1)}, bf16[1024,256]{1,0:T(8,128)(2,1)S(1)}, u32[]{:S(2)}, u32[]{:S(2)}) collective-permute-start(bf16[1024,256]{1,0:T(8,128)(2,1)} %quarter.7), channel_id=1, source_target_pairs={{0,12},{1,13},{2,14},{3,15},{4,8},{5,9},{6,10},{7,11},{8,4},{9,5},... | collective-permute-start | bytes 1572872 | tf_op jit(solution)/shard_map/ppermute | solution.py:97
  102.8 42.3 %collective-permute-start.2 = (bf16[1024,256]{1,0:T(8,128)(2,1)}, bf16[1024,256]{1,0:T(8,128)(2,1)S(1)}, u32[]{:S(2)}, u32[]{:S(2)}) collective-permute-start(bf16[1024,256]{1,0:T(8,128)(2,1)} %quarter.6), channel_id=1, source_target_pairs={{0,4},{1,5},{2,6},{3,7},{4,0},{5,1},{6,2},{7,3},{8,12},{9,13},{10,... | collective-permute-start | bytes 1572872 | tf_op jit(solution)/shard_map/ppermute | solution.py:97
  102.9 11.9 %collective-permute-start.9 = (bf16[176,256]{1,0:T(8,128)(2,1)S(1)}, bf16[176,256]{1,0:T(8,128)(2,1)S(1)}, u32[]{:S(2)}, u32[]{:S(2)}) collective-permute-start(bf16[176,256]{1,0:T(8,128)(2,1)S(1)} %reduce_sum.12), channel_id=1, source_target_pairs={{0,3},{1,2},{2,1},{3,0},{4,7},{5,6},{6,5},{7,4},{8,11},{9,10},{10,... | collective-permute-start | bytes 270344 | tf_op jit(solution)/shard_map/ppermute | solution.py:97
  108.1 9.4 %collective-permute-start.8 = (bf16[176,256]{1,0:T(8,128)(2,1)S(1)}, bf16[176,256]{1,0:T(8,128)(2,1)S(1)}, u32[]{:S(2)}, u32[]{:S(2)}) collective-permute-start(bf16[176,256]{1,0:T(8,128)(2,1)S(1)} %reduce_sum.12), channel_id=1, source_target_pairs={{0,2},{1,3},{2,0},{3,1},{4,6},{5,7},{6,4},{7,5},{8,10},{9,11},{10,... | collective-permute-start | bytes 270344 | tf_op jit(solution)/shard_map/ppermute | solution.py:97
  109.3 8.2 %collective-permute-start.7 = (bf16[176,256]{1,0:T(8,128)(2,1)S(1)}, bf16[176,256]{1,0:T(8,128)(2,1)S(1)}, u32[]{:S(2)}, u32[]{:S(2)}) collective-permute-start(bf16[176,256]{1,0:T(8,128)(2,1)S(1)} %reduce_sum.12), channel_id=1, source_target_pairs={{0,1},{1,0},{2,3},{3,2},{4,5},{5,4},{6,7},{7,6},{8,9},{9,8},{10,11... | collective-permute-start | bytes 270344 | tf_op jit(solution)/shard_map/ppermute | solution.py:97
  114.8 30.3 %collective-permute-start.1 = (bf16[1024,256]{1,0:T(8,128)(2,1)}, bf16[1024,256]{1,0:T(8,128)(2,1)S(1)}, u32[]{:S(2)}, u32[]{:S(2)}) collective-permute-start(bf16[1024,256]{1,0:T(8,128)(2,1)} %quarter.5), channel_id=1, source_target_pairs={{0,8},{1,9},{2,10},{3,11},{4,12},{5,13},{6,14},{7,15},{8,0},{9,1},... | collective-permute-start | bytes 1572872 | tf_op jit(solution)/shard_map/ppermute | solution.py:97
  117.6 16.6 %collective-permute-start.12 = (bf16[176,256]{1,0:T(8,128)(2,1)S(1)}, bf16[176,256]{1,0:T(8,128)(2,1)S(1)}, u32[]{:S(2)}, u32[]{:S(2)}) collective-permute-start(bf16[176,256]{1,0:T(8,128)(2,1)S(1)} %add_convert_fusion.2), channel_id=1, source_target_pairs={{0,12},{1,13},{2,14},{3,15},{4,8},{5,9},{6,10},{7,11},{8,4},{9,5},... | collective-permute-start | bytes 270344 | tf_op jit(solution)/shard_map/ppermute | solution.py:97
  118.8 21.2 %collective-permute-start.11 = (bf16[176,256]{1,0:T(8,128)(2,1)S(1)}, bf16[176,256]{1,0:T(8,128)(2,1)S(1)}, u32[]{:S(2)}, u32[]{:S(2)}) collective-permute-start(bf16[176,256]{1,0:T(8,128)(2,1)S(1)} %add_convert_fusion.2), channel_id=1, source_target_pairs={{0,8},{1,9},{2,10},{3,11},{4,12},{5,13},{6,14},{7,15},{8,0},{9,1},... | collective-permute-start | bytes 270344 | tf_op jit(solution)/shard_map/ppermute | solution.py:97
  134.3 5.8 %collective-permute-start.10 = (bf16[176,256]{1,0:T(8,128)(2,1)S(1)}, bf16[176,256]{1,0:T(8,128)(2,1)S(1)}, u32[]{:S(2)}, u32[]{:S(2)}) collective-permute-start(bf16[176,256]{1,0:T(8,128)(2,1)S(1)} %add_convert_fusion.2), channel_id=1, source_target_pairs={{0,4},{1,5},{2,6},{3,7},{4,0},{5,1},{6,2},{7,3},{8,12},{9,13},{10,... | collective-permute-start | bytes 270344 | tf_op jit(solution)/shard_map/ppermute | solution.py:97
  140.9 24.9 %all-to-all-start.6 = ((bf16[8,96,256]{2,1,0:T(8,128)(2,1)}), bf16[8,96,256]{2,1,0:T(8,128)(2,1)S(1)}, u32[]{:S(2)}, u32[]{:S(2)}) async-start(bf16[8,96,256]{2,1,0:T(8,128)(2,1)} %broadcast_in_dim.38), calls=%async_computation.6 | async-start | bytes 786432 | tf_op jit(solution)/shard_map/all_to_all | solution.py:340
  145.5 6.3 %collective-permute-start.6 = (bf16[256,256]{1,0:T(8,128)(2,1)S(1)}, bf16[256,256]{1,0:T(8,128)(2,1)S(1)}, u32[]{:S(2)}, u32[]{:S(2)}) collective-permute-start(bf16[256,256]{1,0:T(8,128)(2,1)S(1)} %get-tuple-element.50), channel_id=1, source_target_pairs={{0,3},{1,2},{2,1},{3,0},{4,7},{5,6},{6,5},{7,4},{8,11},{9,10},{10,... | collective-permute-start | bytes 393224 | tf_op jit(solution)/shard_map/ppermute | solution.py:97
  148.8 16.3 %collective-permute-start.5 = (bf16[256,256]{1,0:T(8,128)(2,1)S(1)}, bf16[256,256]{1,0:T(8,128)(2,1)S(1)}, u32[]{:S(2)}, u32[]{:S(2)}) collective-permute-start(bf16[256,256]{1,0:T(8,128)(2,1)S(1)} %get-tuple-element.51), channel_id=1, source_target_pairs={{0,2},{1,3},{2,0},{3,1},{4,6},{5,7},{6,4},{7,5},{8,10},{9,11},{10,... | collective-permute-start | bytes 393224 | tf_op jit(solution)/shard_map/ppermute | solution.py:97
  150.9 14.1 %collective-permute-start.4 = (bf16[256,256]{1,0:T(8,128)(2,1)S(1)}, bf16[256,256]{1,0:T(8,128)(2,1)S(1)}, u32[]{:S(2)}, u32[]{:S(2)}) collective-permute-start(bf16[256,256]{1,0:T(8,128)(2,1)S(1)} %get-tuple-element.49), channel_id=1, source_target_pairs={{0,1},{1,0},{2,3},{3,2},{4,5},{5,4},{6,7},{7,6},{8,9},{9,8},{10,11... | collective-permute-start | bytes 393224 | tf_op jit(solution)/shard_map/ppermute | solution.py:97
  165.8 3.5 %collective-permute-start.13 = (bf16[8,96,256]{2,1,0:T(8,128)(2,1)S(1)}, bf16[8,96,256]{2,1,0:T(8,128)(2,1)S(1)}, u32[]{:S(2)}, u32[]{:S(2)}) collective-permute-start(bf16[8,96,256]{2,1,0:T(8,128)(2,1)S(1)} %all-to-all-done.6.mine_ref), channel_id=1, source_target_pairs={{0,16},{16,0},{32,48},{48,32},{64,80},{80,64},{96,112},{112,96},{1... | collective-permute-start | bytes 1179656 | tf_op jit(solution)/shard_map/ppermute | solution.py:347
  (7 other events, 27.4 us)
